TPU v7x, 32 devices: a whole 2x2x4 slice. The times are simulated.
32 devices in a mesh: ctx: 8 (over z, x), fsdp: 4 (over y, core).
Axes of the slice: x: 2, y: 2, z: 4, core: 2. Of those that a mesh axis runs over, the one named last changes fastest.
Arguments:
- tokens: bfloat16 [4, 2048, 768], P('fsdp', 'ctx'), may hold values from -6 to 6
- starts: int32 [4, 4], P('fsdp'), may hold values from 0 to 2047, as said below
- labels: int32 [4, 4], P('fsdp'), may hold values from 0 to 13
- cotangent: bfloat16 [4, 2048, 768], P('fsdp', 'ctx'), may hold values from -6 to 6
- w_query: bfloat16 [768, 768], P('fsdp'), may hold values from -0.21875 to 0.21875
- b_query: bfloat16 [768], P('fsdp'), may hold values from -1.75 to 1.75
- w_key: bfloat16 [768, 768], P('fsdp'), may hold values from -0.21875 to 0.21875
- w_value: bfloat16 [768, 768], P('fsdp'), may hold values from -0.21875 to 0.21875
- b_value: bfloat16 [768], P('fsdp'), may hold values from -0.125 to 0.125
- w_out: bfloat16 [768, 768], P('fsdp'), may hold values from -4 to 4
- b_out: bfloat16 [768], P('fsdp'), may hold values from -1.75 to 1.75
- norm1_gain: bfloat16 [768], P('fsdp'), may hold values from 0.5 to 1.5
- norm1_bias: bfloat16 [768], P('fsdp'), may hold values from -1.75 to 1.75
- w_up: bfloat16 [768, 3072], P('fsdp'), may hold values from -0.21875 to 0.21875
- b_up: bfloat16 [3072], P('fsdp'), may hold values from -1.75 to 1.75
- w_down: bfloat16 [3072, 768], P('fsdp'), may hold values from -0.109375 to 0.109375
- b_down: bfloat16 [768], P('fsdp'), may hold values from -1.75 to 1.75
- norm2_gain: bfloat16 [768], P('fsdp'), may hold values from 0.5 to 1.5
- norm2_bias: bfloat16 [768], P('fsdp'), may hold values from -1.75 to 1.75
- w_student: bfloat16 [768, 128], P('fsdp'), may hold values from -0.21875 to 0.21875
- b_student: bfloat16 [128], P('fsdp'), may hold values from -0.3125 to 0.3125
- pool_query: bfloat16 [128], P('fsdp'), may hold values from -6 to 6
- w_pool: bfloat16 [128, 128], P('fsdp'), may hold values from -1 to 1
- b_pool: bfloat16 [128], P('fsdp'), may hold values from -1.75 to 1.75
- w_class: bfloat16 [128, 14], P('fsdp'), may hold values from -1.5 to 1.5
- b_class: bfloat16 [14], replicated, may hold values from -3 to 3
Outputs:
- hidden: bfloat16 [4, 2048, 768], P('fsdp', 'ctx')
- logits: float32 [4, 4, 14], P('fsdp')
- grad_tokens: float32 [4, 2048, 768], P('fsdp', 'ctx')
- grad_w_query: float32 [768, 768], P('fsdp')
- grad_b_query: float32 [768], P('fsdp')
- grad_w_key: float32 [768, 768], P('fsdp')
- grad_w_value: float32 [768, 768], P('fsdp')
- grad_b_value: float32 [768], P('fsdp')
- grad_w_out: float32 [768, 768], P('fsdp')
- grad_b_out: float32 [768], P('fsdp')
- grad_norm1_gain: float32 [768], P('fsdp')
- grad_norm1_bias: float32 [768], P('fsdp')
- grad_w_up: float32 [768, 3072], P('fsdp')
- grad_b_up: float32 [3072], P('fsdp')
- grad_w_down: float32 [3072, 768], P('fsdp')
- grad_b_down: float32 [768], P('fsdp')
- grad_norm2_gain: float32 [768], P('fsdp')
- grad_norm2_bias: float32 [768], P('fsdp')
- grad_w_student: float32 [768, 128], P('fsdp')
- grad_b_student: float32 [128], P('fsdp')
- grad_pool_query: float32 [128], P('fsdp')
- grad_w_pool: float32 [128, 128], P('fsdp')
- grad_b_pool: float32 [128], P('fsdp')
- grad_w_class: float32 [128, 14], P('fsdp')
- grad_b_class: float32 [14], replicated
Inputs may be any that keep to these rules, and one draw needn't show every extreme that they name: `starts`: each row lists the first positions of its stream's 4 documents in increasing order; the first is 0 and every document has at least one token. In one stream the last document is a single token.
All inputs are finite; a program needn't handle non-finite values.
Results may differ from a plain program's by a relative error of at most 0.022.
Values may be sent and summed in bfloat16 or wider, within the bound.
No kernel may reach another device: no remote copies, remote signals or barrier semaphores. Data moves between devices by JAX's collectives and lax.ppermute only.
A program may use at most 256 MiB of HBM per device.

v0:
```python
import math

import jax
import jax.numpy as jnp
from jax import lax
from jax.sharding import PartitionSpec as P

HEADS = 12
HEAD_DIM = 64
POOL_HEADS = 2
CLASSES = 14
NDOC = 4


big_negative = -1e30
norm_eps = 1e-05


def joined(shard, axis, combine):
    everything = jax.tree.map(lambda part: lax.all_gather(part, axis), shard)
    first = jax.tree.map(lambda part: part[0], everything)

    def lap(k, so_far):
        return combine(so_far, jax.tree.map(lambda part: part[k], everything))

    return lax.fori_loop(1, lax.axis_size(axis), lap, first)


def doc_of(positions, starts_row):
    return jnp.sum((starts_row[None, :] <= positions[:, None]).astype(jnp.int32), axis=1) - 1


def layer_forward(field_in, gain_row, bias_row):
    centre = field_in - jnp.mean(field_in, axis=-1, keepdims=True)
    inv_std = lax.rsqrt(jnp.mean(centre * centre, axis=-1, keepdims=True) + norm_eps)
    normed = centre * inv_std
    return (normed * gain_row + bias_row, normed, inv_std)


def layer_backward(grad_in, normed, inv_std, gain_row):
    scaled = grad_in * gain_row
    back_out = inv_std * (
        scaled
        - jnp.mean(scaled, axis=-1, keepdims=True)
        - normed * jnp.mean(scaled * normed, axis=-1, keepdims=True)
    )
    return (back_out, jnp.sum(grad_in * normed, axis=0), jnp.sum(grad_in, axis=0))


def gelu_slope(field_in):
    normal_cdf = 0.5 * (1.0 + lax.erf(field_in * (1.0 / math.sqrt(2.0))))
    normal_pdf = jnp.exp(-0.5 * field_in * field_in) * (1.0 / math.sqrt(2.0 * math.pi))
    return normal_cdf + field_in * normal_pdf


def cross_rows(left_mat, right_mat):
    return lax.dot_general(
        left_mat, right_mat, (((0,), (0,)), ((), ())), preferred_element_type=jnp.float32
    )


def back_mul(left_mat, right_mat):
    return lax.dot_general(
        left_mat, right_mat, (((1,), (1,)), ((), ())), preferred_element_type=jnp.float32
    )


def small_dot(left_mat, right_mat):
    return jnp.dot(left_mat, right_mat, precision=lax.Precision.HIGHEST)


def shards(
    tokens,
    starts,
    labels,
    cotangent,
    w_query,
    b_query,
    w_key,
    w_value,
    b_value,
    w_out,
    b_out,
    norm1_gain,
    norm1_bias,
    w_up,
    b_up,
    w_down,
    b_down,
    norm2_gain,
    norm2_bias,
    w_student,
    b_student,
    pool_query,
    w_pool,
    b_pool,
    w_class,
    b_class,
):
    gathered = (
        lax.all_gather(w_query, "fsdp", axis=0, tiled=True),
        lax.all_gather(b_query, "fsdp", axis=0, tiled=True),
        lax.all_gather(w_key, "fsdp", axis=0, tiled=True),
        lax.all_gather(w_value, "fsdp", axis=0, tiled=True),
        lax.all_gather(b_value, "fsdp", axis=0, tiled=True),
        lax.all_gather(w_out, "fsdp", axis=0, tiled=True),
        lax.all_gather(b_out, "fsdp", axis=0, tiled=True),
        lax.all_gather(norm1_gain, "fsdp", axis=0, tiled=True),
        lax.all_gather(norm1_bias, "fsdp", axis=0, tiled=True),
        lax.all_gather(w_up, "fsdp", axis=0, tiled=True),
        lax.all_gather(b_up, "fsdp", axis=0, tiled=True),
        lax.all_gather(w_down, "fsdp", axis=0, tiled=True),
        lax.all_gather(b_down, "fsdp", axis=0, tiled=True),
        lax.all_gather(norm2_gain, "fsdp", axis=0, tiled=True),
        lax.all_gather(norm2_bias, "fsdp", axis=0, tiled=True),
        lax.all_gather(w_student, "fsdp", axis=0, tiled=True),
        lax.all_gather(b_student, "fsdp", axis=0, tiled=True),
        lax.all_gather(pool_query, "fsdp", axis=0, tiled=True),
        lax.all_gather(w_pool, "fsdp", axis=0, tiled=True),
        lax.all_gather(b_pool, "fsdp", axis=0, tiled=True),
        lax.all_gather(w_class, "fsdp", axis=0, tiled=True),
    )
    (
        full_wq,
        full_bq,
        full_wk,
        full_wv,
        full_bv,
        full_wo,
        full_bo,
        full_g1,
        full_e1,
        full_w1,
        full_c1,
        full_w2,
        full_c2,
        full_g2,
        full_e2,
        full_ws,
        full_bs,
        full_qp,
        full_wp,
        full_bp,
        full_wc,
    ) = gathered
    f32 = jnp.float32
    bf16 = jnp.bfloat16
    cycle_size = lax.axis_size("ctx")
    cycle_index = lax.axis_index("ctx")
    tok_rows = tokens.shape[1]
    width = tokens.shape[2]
    seq_total = tok_rows * cycle_size
    score_scale = 1.0 / math.sqrt(HEAD_DIM)
    starts_row = starts[0]
    local_pos = cycle_index * tok_rows + jnp.arange(tok_rows, dtype=jnp.int32)
    local_doc = doc_of(local_pos, starts_row)
    x_in = tokens[0]
    query_b = (jnp.dot(x_in, full_wq, preferred_element_type=f32) + full_bq.astype(f32)).astype(
        bf16
    )
    key_b = jnp.dot(x_in, full_wk, preferred_element_type=f32).astype(bf16)
    value_b = (jnp.dot(x_in, full_wv, preferred_element_type=f32) + full_bv.astype(f32)).astype(
        bf16
    )
    query_heads = query_b.reshape(tok_rows, HEADS, HEAD_DIM)

    def same_doc_mask(key_first, row_count):
        key_doc = doc_of(key_first + jnp.arange(row_count, dtype=jnp.int32), starts_row)
        return (local_doc[:, None] == key_doc[None, :])[None]

    def attend_block(state_now, key_blk, value_blk, key_first):
        run_max, run_sum, run_acc = state_now
        row_count = key_blk.shape[0]
        same_doc = same_doc_mask(key_first, row_count)
        scores = (
            jnp.einsum(
                "qhd,khd->hqk",
                query_heads,
                key_blk.reshape(row_count, HEADS, HEAD_DIM),
                preferred_element_type=f32,
            )
            * score_scale
        )
        masked = jnp.where(same_doc, scores, big_negative)
        new_max = jnp.maximum(run_max, jnp.max(masked, axis=2))
        weights = jnp.where(same_doc, jnp.exp(masked - new_max[:, :, None]), 0.0)
        factor = jnp.exp(run_max - new_max)
        new_sum = run_sum * factor + jnp.sum(weights, axis=2)
        new_acc = run_acc * factor[:, :, None] + jnp.einsum(
            "hqk,khd->hqd",
            weights.astype(bf16),
            value_blk.reshape(row_count, HEADS, HEAD_DIM),
            preferred_element_type=f32,
        )
        return (new_max, new_sum, new_acc)

    start_state = (
        jnp.full((HEADS, tok_rows), big_negative, f32),
        jnp.zeros((HEADS, tok_rows), f32),
        jnp.zeros((HEADS, tok_rows, HEAD_DIM), f32),
    )
    key_part = lax.all_gather(key_b, "ctx", axis=0, tiled=True)
    value_part = lax.all_gather(value_b, "ctx", axis=0, tiled=True)
    block_count = key_part.shape[0] // tok_rows

    def step_block(state_in, block_pack):
        key_blk, value_blk, block_index = block_pack
        return (attend_block(state_in, key_blk, value_blk, block_index * tok_rows), None)

    state_out, unused_out = lax.scan(
        step_block,
        start_state,
        (
            key_part.reshape(block_count, tok_rows, width),
            value_part.reshape(block_count, tok_rows, width),
            jnp.arange(block_count, dtype=jnp.int32),
        ),
    )
    row_max, row_sum, row_acc = state_out
    row_lse = row_max + jnp.log(row_sum)
    attn_f = jnp.transpose(row_acc / row_sum[:, :, None], (1, 0, 2))
    attn_b = attn_f.reshape(tok_rows, width).astype(bf16)
    branch = jnp.dot(attn_b, full_wo, preferred_element_type=f32) + full_bo.astype(f32)
    gain_one = full_g1.astype(f32)
    gain_two = full_g2.astype(f32)
    hidden_one, normed_one, inv_one = layer_forward(
        x_in.astype(f32) + branch, gain_one, full_e1.astype(f32)
    )
    hidden_one_b = hidden_one.astype(bf16)
    up_pre = jnp.dot(hidden_one_b, full_w1, preferred_element_type=f32) + full_c1.astype(f32)
    up_b = jax.nn.gelu(up_pre, approximate=False).astype(bf16)
    down_out = jnp.dot(up_b, full_w2, preferred_element_type=f32) + full_c2.astype(f32)
    layer_out, normed_two, inv_two = layer_forward(
        hidden_one + down_out, gain_two, full_e2.astype(f32)
    )
    out_b = layer_out.astype(bf16)
    pool_width = full_ws.shape[1]
    pool_dim = pool_width // POOL_HEADS
    pool_scale = 1.0 / math.sqrt(pool_dim)
    student = jnp.dot(out_b, full_ws, preferred_element_type=f32) + full_bs.astype(f32)
    query_pool = full_qp.astype(f32)
    onehot_bool = local_doc[:, None] == jnp.arange(NDOC, dtype=jnp.int32)[None, :]
    onehot = onehot_bool.astype(f32)

    def pick_rows(table):
        return jnp.sum(jnp.where(onehot_bool[:, :, None], table[None, :, :], 0.0), axis=1)

    pool_scores = (
        jnp.sum((student * query_pool[None, :]).reshape(tok_rows, POOL_HEADS, pool_dim), axis=2)
        * pool_scale
    )
    local_max = jnp.max(
        jnp.where(onehot_bool[:, :, None], pool_scores[:, None, :], big_negative), axis=0
    )
    tok_weight = jnp.exp(pool_scores - pick_rows(local_max))
    local_total = small_dot(onehot.T, tok_weight)
    local_acc = small_dot(onehot.T, jnp.repeat(tok_weight, pool_dim, axis=1) * student)

    def merge_pool(first_part, second_part):
        max_a, total_a, acc_a = first_part
        max_b, total_b, acc_b = second_part
        both_max = jnp.maximum(max_a, max_b)
        fac_a = jnp.exp(max_a - both_max)
        fac_b = jnp.exp(max_b - both_max)
        both_acc = acc_a * jnp.repeat(fac_a, pool_dim, axis=1) + acc_b * jnp.repeat(
            fac_b, pool_dim, axis=1
        )
        return (both_max, total_a * fac_a + total_b * fac_b, both_acc)

    doc_max, doc_total, doc_acc = joined((local_max, local_total, local_acc), "ctx", merge_pool)
    pooled = doc_acc / jnp.repeat(doc_total, pool_dim, axis=1)
    pool_w = full_wp.astype(f32)
    class_w = full_wc.astype(f32)
    head_act = jnp.tanh(small_dot(pooled, pool_w) + full_bp.astype(f32))
    logits = small_dot(head_act, class_w) + b_class.astype(f32)
    label_hot = (labels[0][:, None] == jnp.arange(CLASSES, dtype=jnp.int32)[None, :]).astype(f32)
    grad_logits = jax.nn.softmax(logits, axis=-1) - label_hot
    grad_wc = small_dot(head_act.T, grad_logits)
    grad_bc = jnp.sum(grad_logits, axis=0)
    grad_pre = small_dot(grad_logits, class_w.T) * (1.0 - head_act * head_act)
    grad_wp = small_dot(pooled.T, grad_pre)
    grad_bp = jnp.sum(grad_pre, axis=0)
    grad_pooled = small_dot(grad_pre, pool_w.T)
    tok_norm_w = jnp.exp(pool_scores - pick_rows(doc_max)) / pick_rows(doc_total)
    tok_gpool = pick_rows(grad_pooled)
    tok_pooled = pick_rows(pooled)
    inner_dot = jnp.sum(
        (tok_gpool * (student - tok_pooled)).reshape(tok_rows, POOL_HEADS, pool_dim), axis=2
    )
    grad_score = tok_norm_w * inner_dot
    spread_score = jnp.repeat(grad_score, pool_dim, axis=1)
    grad_student_f = (
        jnp.repeat(tok_norm_w, pool_dim, axis=1) * tok_gpool
        + spread_score * query_pool[None, :] * pool_scale
    )
    grad_qp = jnp.sum(spread_score * student, axis=0) * pool_scale
    grad_student_b = grad_student_f.astype(bf16)
    grad_ws = cross_rows(out_b, grad_student_b)
    grad_bs = jnp.sum(grad_student_b.astype(f32), axis=0)
    grad_layer = cotangent[0].astype(f32) + back_mul(grad_student_b, full_ws)
    grad_res2, grad_g2, grad_e2 = layer_backward(grad_layer, normed_two, inv_two, gain_two)
    grad_down_b = grad_res2.astype(bf16)
    grad_w2 = cross_rows(up_b, grad_down_b)
    grad_c2 = jnp.sum(grad_down_b.astype(f32), axis=0)
    grad_up_b = (back_mul(grad_down_b, full_w2) * gelu_slope(up_pre)).astype(bf16)
    grad_w1 = cross_rows(hidden_one_b, grad_up_b)
    grad_c1 = jnp.sum(grad_up_b.astype(f32), axis=0)
    grad_hidden = grad_res2 + back_mul(grad_up_b, full_w1)
    grad_res1, grad_g1, grad_e1 = layer_backward(grad_hidden, normed_one, inv_one, gain_one)
    grad_branch_b = grad_res1.astype(bf16)
    grad_wo = cross_rows(attn_b, grad_branch_b)
    grad_bo = jnp.sum(grad_branch_b.astype(f32), axis=0)
    grad_attn_b = back_mul(grad_branch_b, full_wo).astype(bf16)
    grad_heads = grad_attn_b.reshape(tok_rows, HEADS, HEAD_DIM)
    row_delta = jnp.einsum("qhd,qhd->hq", attn_f, grad_heads.astype(f32))

    def block_grads(key_blk, value_blk, key_first):
        row_count = key_blk.shape[0]
        same_doc = same_doc_mask(key_first, row_count)
        key_h = key_blk.reshape(row_count, HEADS, HEAD_DIM)
        value_h = value_blk.reshape(row_count, HEADS, HEAD_DIM)
        scores = (
            jnp.einsum("qhd,khd->hqk", query_heads, key_h, preferred_element_type=f32) * score_scale
        )
        prob_blk = jnp.exp(jnp.where(same_doc, scores - row_lse[:, :, None], big_negative))
        grad_prob = jnp.einsum("qhd,khd->hqk", grad_heads, value_h, preferred_element_type=f32)
        grad_scores_b = (prob_blk * (grad_prob - row_delta[:, :, None])).astype(bf16)
        query_part = (
            jnp.einsum("hqk,khd->qhd", grad_scores_b, key_h, preferred_element_type=f32)
            * score_scale
        )
        key_part = (
            jnp.einsum("hqk,qhd->khd", grad_scores_b, query_heads, preferred_element_type=f32)
            * score_scale
        )
        value_part = jnp.einsum(
            "hqk,qhd->khd", prob_blk.astype(bf16), grad_heads, preferred_element_type=f32
        )
        return (
            query_part,
            key_part.reshape(row_count, width),
            value_part.reshape(row_count, width),
        )

    all_keys, all_values = (
        lax.all_gather(key_b, "ctx", axis=0, tiled=True),
        lax.all_gather(value_b, "ctx", axis=0, tiled=True),
    )
    group_size = 1
    while group_size * 2 * tok_rows <= 1024 and cycle_size % (group_size * 2) == 0:
        group_size = group_size * 2
    block_rows = group_size * tok_rows
    block_count = seq_total // block_rows

    def scan_block(query_sum, block_pack):
        key_blk, value_blk, block_index = block_pack
        query_part, key_part, value_part = block_grads(key_blk, value_blk, block_index * block_rows)
        return (query_sum + query_part, (key_part, value_part))

    grad_query_f, (key_terms, value_terms) = lax.scan(
        scan_block,
        jnp.zeros((tok_rows, HEADS, HEAD_DIM), f32),
        (
            all_keys.reshape(block_count, block_rows, width),
            all_values.reshape(block_count, block_rows, width),
            jnp.arange(block_count, dtype=jnp.int32),
        ),
    )
    grad_key_f, grad_value_f = (
        lax.psum_scatter(
            key_terms.reshape(seq_total, width).astype(jnp.bfloat16),
            "ctx",
            scatter_dimension=0,
            tiled=True,
        ).astype(jnp.float32),
        lax.psum_scatter(
            value_terms.reshape(seq_total, width).astype(jnp.bfloat16),
            "ctx",
            scatter_dimension=0,
            tiled=True,
        ).astype(jnp.float32),
    )
    grad_query_b = grad_query_f.reshape(tok_rows, width).astype(bf16)
    grad_key_b = grad_key_f.astype(bf16)
    grad_value_b = grad_value_f.astype(bf16)
    grad_wq = cross_rows(x_in, grad_query_b)
    grad_bq = jnp.sum(grad_query_b.astype(f32), axis=0)
    grad_wk = cross_rows(x_in, grad_key_b)
    grad_wv = cross_rows(x_in, grad_value_b)
    grad_bv = jnp.sum(grad_value_b.astype(f32), axis=0)
    grad_tokens = (
        grad_res1
        + back_mul(grad_query_b, full_wq)
        + back_mul(grad_key_b, full_wk)
        + back_mul(grad_value_b, full_wv)
    )
    head_owner = (cycle_index == 0).astype(f32)
    grad_wp_own = grad_wp * head_owner
    grad_bp_own = grad_bp * head_owner
    grad_wc_own = grad_wc * head_owner
    grad_bc_own = grad_bc * head_owner
    fsdp_size = lax.axis_size("fsdp")
    class_rows = jnp.broadcast_to(grad_bc_own[None, :], (fsdp_size, grad_bc_own.shape[0]))
    scattered = (
        lax.psum_scatter(
            grad_wq.astype(jnp.bfloat16), "fsdp", scatter_dimension=0, tiled=True
        ).astype(jnp.float32),
        lax.psum_scatter(
            grad_bq.astype(jnp.bfloat16), "fsdp", scatter_dimension=0, tiled=True
        ).astype(jnp.float32),
        lax.psum_scatter(
            grad_wk.astype(jnp.bfloat16), "fsdp", scatter_dimension=0, tiled=True
        ).astype(jnp.float32),
        lax.psum_scatter(
            grad_wv.astype(jnp.bfloat16), "fsdp", scatter_dimension=0, tiled=True
        ).astype(jnp.float32),
        lax.psum_scatter(
            grad_bv.astype(jnp.bfloat16), "fsdp", scatter_dimension=0, tiled=True
        ).astype(jnp.float32),
        lax.psum_scatter(
            grad_wo.astype(jnp.bfloat16), "fsdp", scatter_dimension=0, tiled=True
        ).astype(jnp.float32),
        lax.psum_scatter(
            grad_bo.astype(jnp.bfloat16), "fsdp", scatter_dimension=0, tiled=True
        ).astype(jnp.float32),
        lax.psum_scatter(
            grad_g1.astype(jnp.bfloat16), "fsdp", scatter_dimension=0, tiled=True
        ).astype(jnp.float32),
        lax.psum_scatter(
            grad_e1.astype(jnp.bfloat16), "fsdp", scatter_dimension=0, tiled=True
        ).astype(jnp.float32),
        lax.psum_scatter(
            grad_w1.astype(jnp.bfloat16), "fsdp", scatter_dimension=0, tiled=True
        ).astype(jnp.float32),
        lax.psum_scatter(
            grad_c1.astype(jnp.bfloat16), "fsdp", scatter_dimension=0, tiled=True
        ).astype(jnp.float32),
        lax.psum_scatter(
            grad_w2.astype(jnp.bfloat16), "fsdp", scatter_dimension=0, tiled=True
        ).astype(jnp.float32),
        lax.psum_scatter(
            grad_c2.astype(jnp.bfloat16), "fsdp", scatter_dimension=0, tiled=True
        ).astype(jnp.float32),
        lax.psum_scatter(
            grad_g2.astype(jnp.bfloat16), "fsdp", scatter_dimension=0, tiled=True
        ).astype(jnp.float32),
        lax.psum_scatter(
            grad_e2.astype(jnp.bfloat16), "fsdp", scatter_dimension=0, tiled=True
        ).astype(jnp.float32),
        lax.psum_scatter(
            grad_ws.astype(jnp.bfloat16), "fsdp", scatter_dimension=0, tiled=True
        ).astype(jnp.float32),
        lax.psum_scatter(
            grad_bs.astype(jnp.bfloat16), "fsdp", scatter_dimension=0, tiled=True
        ).astype(jnp.float32),
        lax.psum_scatter(
            grad_qp.astype(jnp.bfloat16), "fsdp", scatter_dimension=0, tiled=True
        ).astype(jnp.float32),
        lax.psum_scatter(
            grad_wp_own.astype(jnp.bfloat16), "fsdp", scatter_dimension=0, tiled=True
        ).astype(jnp.float32),
        lax.psum_scatter(
            grad_bp_own.astype(jnp.bfloat16), "fsdp", scatter_dimension=0, tiled=True
        ).astype(jnp.float32),
        lax.psum_scatter(
            grad_wc_own.astype(jnp.bfloat16), "fsdp", scatter_dimension=0, tiled=True
        ).astype(jnp.float32),
        lax.psum_scatter(
            class_rows.astype(jnp.bfloat16), "fsdp", scatter_dimension=0, tiled=True
        ).astype(jnp.float32),
    )
    reduced = (
        lax.psum(scattered[0].astype(jnp.bfloat16), "ctx").astype(jnp.float32),
        lax.psum(scattered[1].astype(jnp.bfloat16), "ctx").astype(jnp.float32),
        lax.psum(scattered[2].astype(jnp.bfloat16), "ctx").astype(jnp.float32),
        lax.psum(scattered[3].astype(jnp.bfloat16), "ctx").astype(jnp.float32),
        lax.psum(scattered[4].astype(jnp.bfloat16), "ctx").astype(jnp.float32),
        lax.psum(scattered[5].astype(jnp.bfloat16), "ctx").astype(jnp.float32),
        lax.psum(scattered[6].astype(jnp.bfloat16), "ctx").astype(jnp.float32),
        lax.psum(scattered[7].astype(jnp.bfloat16), "ctx").astype(jnp.float32),
        lax.psum(scattered[8].astype(jnp.bfloat16), "ctx").astype(jnp.float32),
        lax.psum(scattered[9].astype(jnp.bfloat16), "ctx").astype(jnp.float32),
        lax.psum(scattered[10].astype(jnp.bfloat16), "ctx").astype(jnp.float32),
        lax.psum(scattered[11].astype(jnp.bfloat16), "ctx").astype(jnp.float32),
        lax.psum(scattered[12].astype(jnp.bfloat16), "ctx").astype(jnp.float32),
        lax.psum(scattered[13].astype(jnp.bfloat16), "ctx").astype(jnp.float32),
        lax.psum(scattered[14].astype(jnp.bfloat16), "ctx").astype(jnp.float32),
        lax.psum(scattered[15].astype(jnp.bfloat16), "ctx").astype(jnp.float32),
        lax.psum(scattered[16].astype(jnp.bfloat16), "ctx").astype(jnp.float32),
        lax.psum(scattered[17].astype(jnp.bfloat16), "ctx").astype(jnp.float32),
        lax.psum(scattered[18].astype(jnp.bfloat16), "ctx").astype(jnp.float32),
        lax.psum(scattered[19].astype(jnp.bfloat16), "ctx").astype(jnp.float32),
        lax.psum(scattered[20].astype(jnp.bfloat16), "ctx").astype(jnp.float32),
        lax.psum(scattered[21].astype(jnp.bfloat16), "ctx").astype(jnp.float32),
    )
    shard_list = tuple(reduced[:21])
    class_grad = reduced[21][0]
    return (out_b[None], logits[None], grad_tokens[None]) + shard_list + (class_grad,)


def solution(mesh):
    in_specs = (
        P("fsdp", "ctx", None),
        P("fsdp", None),
        P("fsdp", None),
        P("fsdp", "ctx", None),
        P("fsdp", None),
        P("fsdp"),
        P("fsdp", None),
        P("fsdp", None),
        P("fsdp"),
        P("fsdp", None),
        P("fsdp"),
        P("fsdp"),
        P("fsdp"),
        P("fsdp", None),
        P("fsdp"),
        P("fsdp", None),
        P("fsdp"),
        P("fsdp"),
        P("fsdp"),
        P("fsdp", None),
        P("fsdp"),
        P("fsdp"),
        P("fsdp", None),
        P("fsdp"),
        P("fsdp", None),
        P(),
    )
    out_specs = (
        P("fsdp", "ctx", None),
        P("fsdp", None, None),
        P("fsdp", "ctx", None),
        P("fsdp", None),
        P("fsdp"),
        P("fsdp", None),
        P("fsdp", None),
        P("fsdp"),
        P("fsdp", None),
        P("fsdp"),
        P("fsdp"),
        P("fsdp"),
        P("fsdp", None),
        P("fsdp"),
        P("fsdp", None),
        P("fsdp"),
        P("fsdp"),
        P("fsdp"),
        P("fsdp", None),
        P("fsdp"),
        P("fsdp"),
        P("fsdp", None),
        P("fsdp"),
        P("fsdp", None),
        P(),
    )
    return jax.shard_map(shards, mesh=mesh, in_specs=in_specs, out_specs=out_specs, check_vma=False)
```

profile of v0, /device:TPU:0, one launch (start us, length us, event | category | flops | bytes accessed | tf_op | source)
XLA Modules:
  0.0 1148.3 jit_solution(8617533415597164119)
XLA Ops:
  9.6 20.3 %all-gather.17.cloned.1.call-done = bf16[768,768]{1,0:T(8,128)(2,1)} async-done(((bf16[192,768]{1,0:T(8,128)(2,1)}), bf16[768,768]{1,0:T(8,128)(2,1)}) %all-gather.17.cloned.1.call-update) | async-done | bytes 1179664 | tf_op jit(solution)/shard_map/all_gather | solution.py:103
  37.2 11.5 all-reduce.27
  66.4 6.0 all_gather.106
  87.8 43.8 %all-gather.19.cloned.1.call-done = bf16[2048,768]{1,0:T(8,128)(2,1)} async-done(((bf16[256,768]{1,0:T(8,128)(2,1)}), bf16[2048,768]{1,0:T(8,128)(2,1)}) %all-gather.19.cloned.1.call-update) | async-done | bytes 3145744 | tf_op jit(solution)/shard_map/all_gather | solution.py:202
  131.6 61.7 %all-gather.25.cloned.1.call-done = bf16[2048,768]{1,0:T(8,128)(2,1)} async-done(((bf16[256,768]{1,0:T(8,128)(2,1)}), bf16[2048,768]{1,0:T(8,128)(2,1)}) %all-gather.25.cloned.1.call-update) | async-done | bytes 3145744 | tf_op jit(solution)/shard_map/all_gather | solution.py:203
  193.9 146.8 %while.54 = (s32[]{:T(128)}, f32[12,256]{1,0:T(8,128)}, f32[12,256]{1,0:T(8,128)}, f32[12,256,64]{1,2,0:T(8,128)}, s32[256]{0:T(256)}, /*index=5*/s32[1,4]{1,0:T...) while((s32[]{:T(128)}, f32[12,256]{1,0:T(8,128)}, ...), condition=%wide.region_5.6_spmd.clone, body=%wide.region_1.5_spmd.clone.sunk | while | flops 212224256 | bytes 15801537 | solution.py:210
  344.3 10.9 fusion.29
  361.7 18.2 %all-gather.4 = f32[8,4,2]{1,2,0:T(2,128)S(1)} all-gather(f32[1,4,2]{1,2,0:T(2,128)S(1)} %bitcast.291), channel_id=2, replica_groups=mesh['ctx'=8,'fsdp'=4] {'ctx'}, dimensions={0}, use_global_device_ids=true | all-gather | bytes 288 | tf_op jit(solution)/shard_map/all_gather | solution.py:20
  380.8 16.3 %all-gather.5 = f32[8,4,2]{1,2,0:T(2,128)S(1)} all-gather(f32[1,4,2]{1,2,0:T(2,128)S(1)} %convolution_bitcast_fusion.1), channel_id=3, replica_groups=mesh['ctx'=8,'fsdp'=4] {'ctx'}, dimensions={0}, use_global_device_ids=true | all-gather | bytes 288 | tf_op jit(solution)/shard_map/all_gather | solution.py:20
  397.9 26.4 %all-gather.6 = f32[8,4,128]{2,1,0:T(4,128)S(1)} all-gather(f32[1,4,128]{2,1,0:T(4,128)S(1)} %convolution_bitcast_fusion), channel_id=4, replica_groups=mesh['ctx'=8,'fsdp'=4] {'ctx'}, dimensions={0}, use_global_device_ids=true | all-gather | bytes 18432 | tf_op jit(solution)/shard_map/all_gather | solution.py:20
  445.8 100.6 %while.55 = (s32[]{:T(128)}, f32[256,12,64]{0,2,1:T(8,128)}, bf16[2,1024,768]{2,1,0:T(8,128)(2,1)}, bf16[2,1024,768]{2,1,0:T(8,128)(2,1)}, bf16[2,1024,768]{2,1,...) while((s32[]{:T(128)}, f32[256,12,64]{0,2,1:T(8,128)}, ...), condition=%wide.region_28.29_spmd.clone, body=%wide.region_26.28_spmd.clone.sunk | while | flops 2047161344 | bytes 113620408 | solution.py:360
  448.1 6.4 fusion.185
  459.8 11.7 %fusion.186 = bf16[12,256,1024]{1,2,0:T(8,128)(2,1)} fusion(f32[12,1024,256]{2,1,0:T(8,128)} %fusion.185, f32[12,256]{1,0:T(8,128)S(1)} %get-tuple-element.1251, f32[12,256]{1,0:T(8,128)} %get-tuple-element.1248, pred[256,1024]{0,1:T(8,128)(4,1)} %broadcast_compare_fusion.5, bf16[1024,12,64]{0,2,1:T(8,128)(2,1)} %bitcast.276, ...), kind=kOutput, calls=%fused_computation.32.clone.1 | convolution fusion | flops 421527552 | bytes 21127168 | tf_op jit(solution)/shard_map/while/body/eval_jaxpr/qhd,khd->hqk/dot_general | solution.py:326
  475.7 9.1 fusion.188
  486.5 6.0 convolution_multiply_fusion.7
  498.3 6.4 fusion.185
  510.0 11.7 %fusion.186 = bf16[12,256,1024]{1,2,0:T(8,128)(2,1)} fusion(f32[12,1024,256]{2,1,0:T(8,128)} %fusion.185, f32[12,256]{1,0:T(8,128)S(1)} %get-tuple-element.1251, f32[12,256]{1,0:T(8,128)} %get-tuple-element.1248, pred[256,1024]{0,1:T(8,128)(4,1)} %broadcast_compare_fusion.5, bf16[1024,12,64]{0,2,1:T(8,128)(2,1)} %bitcast.276, ...), kind=kOutput, calls=%fused_computation.32.clone.1 | convolution fusion | flops 421527552 | bytes 21127168 | tf_op jit(solution)/shard_map/while/body/eval_jaxpr/qhd,khd->hqk/dot_general | solution.py:326
  525.9 9.1 fusion.188
  550.3 68.1 %reduce-scatter.20.cloned.1.call-done = bf16[256,768]{1,0:T(8,128)(2,1)} async-done(((bf16[2048,768]{1,0:T(8,128)(2,1)}), bf16[256,768]{1,0:T(8,128)(2,1)}) %reduce-scatter.20.cloned.1.call-update) | async-done | bytes 393232 | tf_op jit(solution)/shard_map/reduce_scatter | solution.py:370
  621.6 73.9 %reduce-scatter.22.cloned.1.call-done = bf16[256,768]{1,0:T(8,128)(2,1)} async-done(((bf16[2048,768]{1,0:T(8,128)(2,1)}), bf16[256,768]{1,0:T(8,128)(2,1)}) %reduce-scatter.22.cloned.1.call-update) | async-done | bytes 393232 | tf_op jit(solution)/shard_map/reduce_scatter | solution.py:376
  713.1 9.8 reduce-scatter.34.cloned.1.call-done
  724.8 26.5 %reduce-scatter.36.cloned.1.call-done = bf16[192,768]{1,0:T(8,128)(2,1)} async-done(((bf16[768,768]{1,0:T(8,128)(2,1)}), bf16[192,768]{1,0:T(8,128)(2,1)}) %reduce-scatter.36.cloned.1.call-update) | async-done | bytes 294928
  753.1 26.4 %reduce-scatter.38.cloned.1.call-done = bf16[192,768]{1,0:T(8,128)(2,1)} async-done(((bf16[768,768]{1,0:T(8,128)(2,1)}), bf16[192,768]{1,0:T(8,128)(2,1)}) %reduce-scatter.38.cloned.1.call-update) | async-done | bytes 294928
  781.4 26.5 %reduce-scatter.24.cloned.1.call-done = bf16[192,768]{1,0:T(8,128)(2,1)} async-done(((bf16[768,768]{1,0:T(8,128)(2,1)}), bf16[192,768]{1,0:T(8,128)(2,1)}) %reduce-scatter.24.cloned.1.call-update) | async-done | bytes 294928 | tf_op jit(solution)/shard_map/reduce_scatter | solution.py:420
  807.9 50.2 %reduce-scatter.26.cloned.1.call-done = bf16[192,3072]{1,0:T(8,128)(2,1)} async-done(((bf16[768,3072]{1,0:T(8,128)(2,1)}), bf16[192,3072]{1,0:T(8,128)(2,1)}) %reduce-scatter.26.cloned.1.call-update) | async-done | bytes 1179664 | tf_op jit(solution)/shard_map/reduce_scatter | solution.py:432
  858.1 50.4 %reduce-scatter.28.cloned.1.call-done = bf16[768,768]{1,0:T(8,128)(2,1)} async-done(((bf16[3072,768]{1,0:T(8,128)(2,1)}), bf16[768,768]{1,0:T(8,128)(2,1)}) %reduce-scatter.28.cloned.1.call-update) | async-done | bytes 1179664 | tf_op jit(solution)/shard_map/reduce_scatter | solution.py:438
  919.9 10.9 reduce-scatter.40.cloned.1.call-done
  931.7 10.9 all-reduce.26
  944.1 8.9 reduce-scatter.32.cloned.1.call-done
  953.1 22.8 %reduce-scatter.30.cloned.1.call-done = bf16[192,128]{1,0:T(8,128)(2,1)} async-done(((bf16[768,128]{1,0:T(8,128)(2,1)}), bf16[192,128]{1,0:T(8,128)(2,1)}) %reduce-scatter.30.cloned.1.call-update) | async-done | bytes 49168 | tf_op jit(solution)/shard_map/reduce_scatter | solution.py:450
  975.9 40.9 %all-reduce.24 = (bf16[192]{0:T(256)(128)(2,1)S(1)}, bf16[192]{0:T(256)(128)(2,1)S(1)}, bf16[192]{0:T(256)(128)(2,1)S(1)}, bf16[192]{0:T(256)(128)(2,1)S(1)}, bf...) all-reduce(bf16[192]{0:T(256)(128)(2,1)S(1)} %dynamic-slice.12, ...), channel_id=1, replica_groups=mesh['ctx'=8,'fsdp'=4] {'ctx'}, use_global_device_ids=true, to_apply=%region_35.36 | all-reduce | flops 31534 | bytes 126136 | tf_op jit(solution)/shard_map/psum | solution.py:474
  1030.0 101.1 %all-reduce.30.cloned.1.call-done = (bf16[192,768]{0,1:T(8,128)(2,1)}, bf16[192,768]{0,1:T(8,128)(2,1)}, bf16[192,768]{0,1:T(8,128)(2,1)}, bf16[192,768]{1,0:T(8...) async-done(((bf16[192,768]{0,1:T(8,128)(2,1)}, bf16[192,768]{0,1:T(8,128)(2,1)}, bf16[192,768]{0,1:T(8,128)(2,1)}, bf16[192,768]{1,0:T(8,128)(2,1)}, ...) | async-done | bytes 3538960 | tf_op jit(solution)/shard_map/psum | solution.py:473
  (634 shorter events, 323.0 us)
Async XLA Ops:
  7.3 22.6 %all-gather.17.cloned.1.call-start = ((), (), s32[]{:S(2)}) async-start(), calls=%async_computation.11 | async-start | bytes 1474560 | tf_op jit(solution)/shard_map/all_gather | solution.py:103
  8.1 41.4 %all-gather.23.cloned.1.call-start = ((), (), s32[]{:S(2)}) async-start(), calls=%async_computation.14 | async-start | bytes 1474560 | tf_op jit(solution)/shard_map/all_gather | solution.py:104
  8.8 77.1 %all-gather.21.cloned.1.call-start = ((), (), s32[]{:S(2)}) async-start(), calls=%async_computation.13 | async-start | bytes 1474560 | tf_op jit(solution)/shard_map/all_gather | solution.py:101
  9.6 122.1 %all-gather.19.cloned.1.call-start = ((), (), s32[]{:S(2)}) async-start(), calls=%async_computation.12 | async-start | bytes 3538944 | tf_op jit(solution)/shard_map/all_gather | solution.py:202
  32.6 160.8 %all-gather.25.cloned.1.call-start = ((), (), s32[]{:S(2)}) async-start(), calls=%async_computation.15 | async-start | bytes 3538944 | tf_op jit(solution)/shard_map/all_gather | solution.py:203
  52.0 289.9 %all-gather.27.cloned.1.call-start = ((), (), s32[]{:S(2)}) async-start(), calls=%async_computation.16 | async-start | bytes 1474560 | tf_op jit(solution)/shard_map/all_gather | solution.py:106
  52.6 291.7 %all-gather.29.cloned.1.call-start = ((), (), s32[]{:S(2)}) async-start(), calls=%async_computation.17 | async-start | bytes 5898240 | tf_op jit(solution)/shard_map/all_gather | solution.py:110
  53.3 301.9 %all-gather.31.cloned.1.call-start = ((), (), s32[]{:S(2)}) async-start(), calls=%async_computation.18 | async-start | bytes 5898240 | tf_op jit(solution)/shard_map/all_gather | solution.py:112
  54.1 564.4 %reduce-scatter.20.cloned.1.call-start = ((), (), s32[]{:S(2)}) async-start(), calls=%async_computation.19 | async-start | bytes 3538944 | tf_op jit(solution)/shard_map/reduce_scatter | solution.py:370
  344.0 97.8 %copy-start.6 = (f32[256,768]{1,0:T(8,128)}, f32[256,768]{1,0:T(8,128)S(1)}, u32[]{:S(2)}) copy-start(f32[256,768]{1,0:T(8,128)S(1)} %get-tuple-element.914) | copy-start | bytes 2359300
  359.8 73.2 %copy-start.4 = (f32[256,768]{1,0:T(8,128)}, f32[256,768]{1,0:T(8,128)S(1)}, u32[]{:S(2)}) copy-start(f32[256,768]{1,0:T(8,128)S(1)} %get-tuple-element.918) | copy-start | bytes 2359300
  359.9 73.1 %copy-start.48 = (f32[256]{0:T(256)}, f32[256]{0:T(256)S(1)}, u32[]{:S(2)}) copy-start(f32[256]{0:T(256)S(1)} %broadcast_multiply_fusion.6) | copy-start | bytes 3076
  546.4 149.0 %reduce-scatter.22.cloned.1.call-start = ((), (), s32[]{:S(2)}) async-start(), calls=%async_computation.20 | async-start | bytes 3538944 | tf_op jit(solution)/shard_map/reduce_scatter | solution.py:376
  547.0 175.9 %reduce-scatter.34.cloned.1.call-start = ((), (), s32[]{:S(2)}) async-start(), calls=%async_computation.26 | async-start | bytes 1474560
  550.3 200.9 %reduce-scatter.36.cloned.1.call-start = ((), (), s32[]{:S(2)}) async-start(), calls=%async_computation.27 | async-start | bytes 1474560
  621.5 77.1 %copy-start.9 = (f32[256,768]{1,0:T(8,128)S(1)}, f32[256,768]{1,0:T(8,128)}, u32[]{:S(2)}) copy-start(f32[256,768]{1,0:T(8,128)} %copy-done.8) | copy-start | bytes 2359300
  621.5 77.1 %copy-start.18 = (bf16[256,12,64]{0,2,1:T(8,128)(2,1)S(1)}, bf16[256,12,64]{0,2,1:T(8,128)(2,1)}, u32[]{:S(2)}) copy-start(bf16[256,12,64]{0,2,1:T(8,128)(2,1)} %copy-done.17) | copy-start | bytes 1179652
  621.5 158.1 %reduce-scatter.38.cloned.1.call-start = ((), (), s32[]{:S(2)}) async-start(), calls=%async_computation.28 | async-start | bytes 1474560
  698.5 109.4 %reduce-scatter.24.cloned.1.call-start = ((), (), s32[]{:S(2)}) async-start(), calls=%async_computation.21 | async-start | bytes 1474560 | tf_op jit(solution)/shard_map/reduce_scatter | solution.py:420
  700.1 158.0 %reduce-scatter.26.cloned.1.call-start = ((), (), s32[]{:S(2)}) async-start(), calls=%async_computation.22 | async-start | bytes 5898240 | tf_op jit(solution)/shard_map/reduce_scatter | solution.py:432
  703.9 204.6 %reduce-scatter.28.cloned.1.call-start = ((), (), s32[]{:S(2)}) async-start(), calls=%async_computation.23 | async-start | bytes 5898240 | tf_op jit(solution)/shard_map/reduce_scatter | solution.py:438
  709.3 221.4 %reduce-scatter.40.cloned.1.call-start = ((), (), s32[]{:S(2)}) async-start(), calls=%async_computation.29 | async-start | bytes 40960
  710.9 242.2 %reduce-scatter.32.cloned.1.call-start = ((), (), s32[]{:S(2)}) async-start(), calls=%async_computation.25 | async-start | bytes 40960 | tf_op jit(solution)/shard_map/reduce_scatter | solution.py:459
  711.9 264.0 %reduce-scatter.30.cloned.1.call-start = ((), (), s32[]{:S(2)}) async-start(), calls=%async_computation.24 | async-start | bytes 245760 | tf_op jit(solution)/shard_map/reduce_scatter | solution.py:450
  713.0 204.0 %copy-start.5 = (f32[256,768]{1,0:T(8,128)S(1)}, f32[256,768]{1,0:T(8,128)}, u32[]{:S(2)}) copy-start(f32[256,768]{1,0:T(8,128)} %copy-done.4) | copy-start | bytes 2359300
  713.0 204.0 %copy-start.44 = (f32[768]{0:T(1024)S(1)}, f32[768]{0:T(1024)}, u32[]{:S(2)}) copy-start(f32[768]{0:T(1024)} %convert_element_type.352) | copy-start | bytes 9220
  713.0 204.0 %copy-start.49 = (f32[256]{0:T(256)S(1)}, f32[256]{0:T(256)}, u32[]{:S(2)}) copy-start(f32[256]{0:T(256)} %copy-done.48) | copy-start | bytes 3076
  713.0 204.0 %copy-start.51 = (f32[768]{0:T(1024)S(1)}, f32[768]{0:T(1024)}, u32[]{:S(2)}) copy-start(f32[768]{0:T(1024)} %convert_element_type.353) | copy-start | bytes 9220
  713.0 204.0 %copy-start.56 = (f32[256]{0:T(256)S(1)}, f32[256]{0:T(256)}, u32[]{:S(2)}) copy-start(f32[256]{0:T(256)} %copy-done.55) | copy-start | bytes 3076
  713.0 418.0 %all-reduce.30.cloned.1.call-start = ((), (), s32[]{:S(2)}) async-start(), calls=%async_computation.30 | async-start | bytes 7667712 | tf_op jit(solution)/shard_map/psum | solution.py:473
  724.8 193.2 %copy-start.23 = (bf16[256,12,64]{0,2,1:T(8,128)(2,1)S(1)}, bf16[256,12,64]{0,2,1:T(8,128)(2,1)}, u32[]{:S(2)}) copy-start(bf16[256,12,64]{0,2,1:T(8,128)(2,1)} %copy-done.22) | copy-start | bytes 1179652
  908.6 117.2 %copy-start.13 = (bf16[768,768]{1,0:T(8,128)(2,1)S(1)}, bf16[768,768]{1,0:T(8,128)(2,1)}, u32[]{:S(2)}) copy-start(bf16[768,768]{1,0:T(8,128)(2,1)} %all-gather.17.cloned.1.call-done) | copy-start | bytes 3538948
  (98 other events, 1703.0 us)
Sparse Core Ops, SparseCore 0:
  9.7 20.1 all-gather.16
  31.5 17.9 all-gather.22
  51.0 17.4 all-gather.20
  71.2 60.4 all-gather.18
  134.2 59.0 all-gather.24
  194.8 16.0 all-gather.26
  212.5 37.4 all-gather.28
  251.5 37.4 all-gather.30
  546.6 71.8 reduce-scatter.19
  621.9 73.5 reduce-scatter.21
  698.0 24.8 reduce-scatter.33
  725.5 25.7 reduce-scatter.35
  753.8 25.7 reduce-scatter.37
  782.1 25.7 reduce-scatter.23
  810.3 47.8 reduce-scatter.25
  860.7 47.7 reduce-scatter.27
  911.4 19.3 reduce-scatter.39
  933.7 19.3 reduce-scatter.31
  956.1 19.7 reduce-scatter.29
  980.7 150.2 all-reduce.29
where the time goes:
time: 1160 us; the launch traced here: 1150 us
  waiting for transfers between devices  607 us (52%)
  matrix products  173 us (15%)
  blocking collectives  146 us (13%)
  local copies, waits for them, and re-layouts  107 us (9%)
  other arithmetic  87.5 us (8%)
  between operations  19.2 us (2%)
    psum x1, waiting for transfers between devices, shards(): lax.psum(scattered[0].astype(jnp.bfloat16), 'ctx').astype(jnp.float32)  101 us
    unnamed x24, waiting for transfers between devices  78.3 us
    reduce_scatter x1, waiting for transfers between devices, shards(): lax.psum_scatter(value_terms.reshape(seq_total, width).astype(jnp.bfloat1...  73.9 us
    reduce_scatter x1, waiting for transfers between devices, shards(): lax.psum_scatter(key_terms.reshape(seq_total, width).astype(jnp.bfloat16)...  68.1 us
    all_gather x1, waiting for transfers between devices, shards(): value_part = lax.all_gather(value_b, 'ctx', axis=0, tiled=True)  61.7 us
    all_gather x3, blocking collectives, joined(): everything = jax.tree.map(lambda part: lax.all_gather(part, axis), shard)  61 us
    reduce_scatter x1, waiting for transfers between devices, shards(): lax.psum_scatter(grad_w2.astype(jnp.bfloat16), 'fsdp', scatter_dimension=...  50.4 us
    reduce_scatter x1, waiting for transfers between devices, shards(): lax.psum_scatter(grad_w1.astype(jnp.bfloat16), 'fsdp', scatter_dimension=...  50.2 us
  transfers between devices with their start and end apart: 20, of which 16 were waited for; matrix products, arithmetic and copies ran while one was open for 20% of the time, Pallas kernels for 0%

commit v1 on v0

v1 whole, which is shorter than its diff:
```python
import functools
import math

import jax
import jax.numpy as jnp
from jax import lax
from jax.experimental import pallas as pl
from jax.experimental.pallas import tpu as pltpu
from jax.sharding import PartitionSpec as P

HEADS = 12
HEAD_DIM = 64
POOL_HEADS = 2
CLASSES = 14
NDOC = 4

big_negative = -1e30
norm_eps = 1e-05
f32 = jnp.float32
bf16 = jnp.bfloat16
VMEM_LIMIT = 56 * 1024 * 1024


def doc_of(positions, starts_row):
    return jnp.sum((starts_row[None, :] <= positions[:, None]).astype(jnp.int32), axis=1) - 1


def layer_forward(field_in, gain_row, bias_row):
    centre = field_in - jnp.mean(field_in, axis=-1, keepdims=True)
    inv_std = lax.rsqrt(jnp.mean(centre * centre, axis=-1, keepdims=True) + norm_eps)
    normed = centre * inv_std
    return (normed * gain_row + bias_row, normed, inv_std)


def layer_backward(grad_in, normed, inv_std, gain_row):
    scaled = grad_in * gain_row
    back_out = inv_std * (
        scaled
        - jnp.mean(scaled, axis=-1, keepdims=True)
        - normed * jnp.mean(scaled * normed, axis=-1, keepdims=True)
    )
    return (back_out, jnp.sum(grad_in * normed, axis=0), jnp.sum(grad_in, axis=0))


def gelu_slope(field_in):
    normal_cdf = 0.5 * (1.0 + lax.erf(field_in * (1.0 / math.sqrt(2.0))))
    normal_pdf = jnp.exp(-0.5 * field_in * field_in) * (1.0 / math.sqrt(2.0 * math.pi))
    return normal_cdf + field_in * normal_pdf


def cross_rows(left_mat, right_mat):
    return lax.dot_general(
        left_mat, right_mat, (((0,), (0,)), ((), ())), preferred_element_type=f32
    )


def back_mul(left_mat, right_mat):
    return lax.dot_general(
        left_mat, right_mat, (((1,), (1,)), ((), ())), preferred_element_type=f32
    )


def small_dot(left_mat, right_mat):
    return jnp.dot(left_mat, right_mat, precision=lax.Precision.HIGHEST)


def _half_mask(shape, axis, half):
    return (lax.broadcasted_iota(jnp.int32, shape, axis) // HEAD_DIM) == half


def _split3(row):
    hi = row.astype(bf16)
    rest = row - hi.astype(f32)
    mid = rest.astype(bf16)
    low = (rest - mid.astype(f32)).astype(bf16)
    return hi.astype(f32), mid.astype(f32), low.astype(f32)


def _extra_rows(docrow, row=None):
    at = lax.broadcasted_iota(jnp.int32, (128, docrow.shape[1]), 0)
    out = jnp.where((at < NDOC) & (at != docrow), big_negative, 0.0)
    if row is not None:
        for k, part in enumerate(_split3(row)):
            out = out + jnp.where(at == NDOC + k, part, 0.0)
    return out.astype(bf16)


def attend_kernel(chunks, q_ref, k_ref, v_ref, extra_ref, doc_ref, attn_ref, low_ref, lse_ref, s_ref):
    rows = k_ref.shape[0] // chunks
    q_t = q_ref[...].astype(f32).T
    bias = _extra_rows(doc_ref[...])
    outs = []
    for half in range(2):
        q_aug = jnp.concatenate(
            [jnp.where(_half_mask(q_t.shape, 0, half), q_t, 0.0).astype(bf16), bias], axis=0
        )
        top = None
        for c in range(chunks):
            at = pl.ds(c * rows, rows)
            k_aug = jnp.concatenate([k_ref[at, :], extra_ref[at, :]], axis=1)
            s_now = jnp.dot(k_aug, q_aug, preferred_element_type=f32)
            s_ref[half, at, :] = s_now
            top_now = jnp.max(s_now, axis=0, keepdims=True)
            top = top_now if top is None else jnp.maximum(top, top_now)
        total = jnp.zeros_like(top)
        mixed = jnp.zeros((2 * HEAD_DIM, q_t.shape[1]), f32)
        for c in range(chunks):
            at = pl.ds(c * rows, rows)
            p_now = jnp.exp(s_ref[half, at, :] - top)
            total = total + jnp.sum(p_now, axis=0, keepdims=True)
            mixed = mixed + cross_rows(v_ref[at, :], p_now.astype(bf16))
        lse_ref[0, pl.ds(half, 1), :] = top + jnp.log(total)
        outs.append(mixed[half * HEAD_DIM : (half + 1) * HEAD_DIM] / total)
    out_t = jnp.concatenate(outs, axis=0)
    attn_ref[...] = out_t
    low_ref[...] = out_t.T.astype(bf16)


def attend(query, keys, values, extra, docs):
    tok, width = query.shape
    seq = keys.shape[0]
    pairs = width // (2 * HEAD_DIM)
    lanes = 2 * HEAD_DIM
    return pl.pallas_call(
        functools.partial(attend_kernel, 4),
        grid=(pairs,),
        in_specs=[
            pl.BlockSpec((tok, lanes), lambda p: (0, p)),
            pl.BlockSpec((seq, lanes), lambda p: (0, p)),
            pl.BlockSpec((seq, lanes), lambda p: (0, p)),
            pl.BlockSpec((seq, lanes), lambda p: (0, 0)),
            pl.BlockSpec((1, tok), lambda p: (0, 0)),
        ],
        out_specs=[
            pl.BlockSpec((lanes, tok), lambda p: (p, 0)),
            pl.BlockSpec((tok, lanes), lambda p: (0, p)),
            pl.BlockSpec((1, 2, tok), lambda p: (p, 0, 0)),
        ],
        out_shape=[
            jax.ShapeDtypeStruct((width, tok), f32),
            jax.ShapeDtypeStruct((tok, width), bf16),
            jax.ShapeDtypeStruct((pairs, 2, tok), f32),
        ],
        scratch_shapes=[pltpu.VMEM((2, seq, tok), f32)],
        compiler_params=pltpu.CompilerParams(vmem_limit_bytes=VMEM_LIMIT),
        cost_estimate=pl.CostEstimate(
            flops=4 * tok * seq * width, transcendentals=tok * seq * HEADS, bytes_accessed=4 * seq * width
        ),
        name="attend",
    )(query, keys, values, extra, docs)


def attend_back_kernel(
    chunks, q_ref, k_ref, v_ref, extra_ref, doc_ref, attn_ref, lse_ref, g_ref, dq_ref, dk_ref, dv_ref
):
    rows = k_ref.shape[0] // chunks
    q_low = q_ref[...]
    g_low = g_ref[...]
    q_t = q_low.astype(f32).T
    g_t = g_low.astype(f32).T
    prod = attn_ref[...] * g_t
    lanes = 2 * HEAD_DIM
    q_side, g_side, q_rows, g_rows = [], [], [], []
    for half in range(2):
        pick = _half_mask(q_t.shape, 0, half)
        delta = jnp.sum(prod[half * HEAD_DIM : (half + 1) * HEAD_DIM], axis=0, keepdims=True)
        q_side.append(
            jnp.concatenate(
                [
                    jnp.where(pick, q_t, 0.0).astype(bf16),
                    _extra_rows(doc_ref[...], -lse_ref[0, pl.ds(half, 1), :]),
                ],
                axis=0,
            )
        )
        g_side.append(
            jnp.concatenate(
                [
                    jnp.where(pick, g_t, 0.0).astype(bf16),
                    _extra_rows(jnp.full_like(doc_ref[...], -1), -delta)
                    * (lax.broadcasted_iota(jnp.int32, (128, q_t.shape[1]), 0) >= NDOC).astype(bf16),
                ],
                axis=0,
            )
        )
        pick_lane = _half_mask(q_low.shape, 1, half)
        q_rows.append(jnp.where(pick_lane, q_low.astype(f32), 0.0).astype(bf16))
        g_rows.append(jnp.where(pick_lane, g_low.astype(f32), 0.0).astype(bf16))
    q_rows = jnp.concatenate(q_rows, axis=0)
    g_rows = jnp.concatenate(g_rows, axis=0)
    dq_t = [jnp.zeros((lanes, q_t.shape[1]), f32) for half in range(2)]
    for c in range(chunks):
        at = pl.ds(c * rows, rows)
        k_now = k_ref[at, :]
        extra = extra_ref[at, :]
        k_aug = jnp.concatenate([k_now, extra], axis=1)
        v_aug = jnp.concatenate([v_ref[at, :], extra], axis=1)
        p_low, s_low = [], []
        for half in range(2):
            prob = jnp.exp(jnp.dot(k_aug, q_side[half], preferred_element_type=f32))
            slope = jnp.dot(v_aug, g_side[half], preferred_element_type=f32)
            p_low.append(prob.astype(bf16))
            s_low.append((prob * slope).astype(bf16))
            dq_t[half] = dq_t[half] + cross_rows(k_now, s_low[half])
        dk_ref[at, :] = jnp.dot(
            jnp.concatenate(s_low, axis=1), q_rows, preferred_element_type=f32
        ).astype(bf16)
        dv_ref[at, :] = jnp.dot(
            jnp.concatenate(p_low, axis=1), g_rows, preferred_element_type=f32
        ).astype(bf16)
    pick = _half_mask(q_t.shape, 0, 0)
    dq_ref[...] = (jnp.where(pick, dq_t[0], dq_t[1]).T * (1.0 / math.sqrt(HEAD_DIM))).astype(bf16)


def attend_back(query, keys, values, extra, docs, attn_t, lse, grad_attn):
    tok, width = query.shape
    seq = keys.shape[0]
    pairs = width // (2 * HEAD_DIM)
    lanes = 2 * HEAD_DIM
    return pl.pallas_call(
        functools.partial(attend_back_kernel, 4),
        grid=(pairs,),
        in_specs=[
            pl.BlockSpec((tok, lanes), lambda p: (0, p)),
            pl.BlockSpec((seq, lanes), lambda p: (0, p)),
            pl.BlockSpec((seq, lanes), lambda p: (0, p)),
            pl.BlockSpec((seq, lanes), lambda p: (0, 0)),
            pl.BlockSpec((1, tok), lambda p: (0, 0)),
            pl.BlockSpec((lanes, tok), lambda p: (p, 0)),
            pl.BlockSpec((1, 2, tok), lambda p: (p, 0, 0)),
            pl.BlockSpec((tok, lanes), lambda p: (0, p)),
        ],
        out_specs=[
            pl.BlockSpec((tok, lanes), lambda p: (0, p)),
            pl.BlockSpec((seq, lanes), lambda p: (0, p)),
            pl.BlockSpec((seq, lanes), lambda p: (0, p)),
        ],
        out_shape=[
            jax.ShapeDtypeStruct((tok, width), bf16),
            jax.ShapeDtypeStruct((seq, width), bf16),
            jax.ShapeDtypeStruct((seq, width), bf16),
        ],
        compiler_params=pltpu.CompilerParams(vmem_limit_bytes=VMEM_LIMIT),
        cost_estimate=pl.CostEstimate(
            flops=10 * tok * seq * width, transcendentals=tok * seq * HEADS, bytes_accessed=8 * seq * width
        ),
        name="attend_back",
    )(query, keys, values, extra, docs, attn_t, lse, grad_attn)


def swap(value, axis, bit):
    count = lax.axis_size(axis)
    return lax.ppermute(value, axis, [(i, i ^ bit) for i in range(count)])


def gather_shards(shard):
    index = lax.axis_index("fsdp")
    core, far = index % 2, index // 2
    other = swap(shard, "fsdp", 2)
    column = jnp.where(far == 0, jnp.stack([shard, other]), jnp.stack([other, shard]))
    across = swap(column, "fsdp", 1)
    full = jnp.where(
        core == 0, jnp.stack([column, across], axis=1), jnp.stack([across, column], axis=1)
    )
    return full.reshape(4 * shard.shape[0], shard.shape[1])


def bits_of(axis):
    return [1 << k for k in range(lax.axis_size(axis).bit_length() - 1)]


def halve(value, axis, bit, at):
    mine = (lax.axis_index(axis) // bit) % 2
    send = lax.dynamic_index_in_dim(value, 1 - mine, at, keepdims=False)
    keep = lax.dynamic_index_in_dim(value, mine, at, keepdims=False)
    got = swap(send, axis, bit)
    return (keep.astype(f32) + got.astype(f32)).astype(bf16)


def scatter_sum(full, axis):
    rows, n = full.shape[1:]
    for bit in bits_of(axis):
        full = halve(full.reshape(-1, 2, rows, n), axis, bit, 1)
    return full.reshape(rows, n)


def double(value, axis, bit):
    mine = (lax.axis_index(axis) // bit) % 2
    got = swap(value, axis, bit)
    return jnp.where(mine == 0, jnp.stack([value, got]), jnp.stack([got, value]))


def ring_sum(rows):
    total, n = rows.shape
    bits = bits_of("ctx")
    for bit in bits:
        rows = halve(rows.reshape(2, -1, n), "ctx", bit, 0)
    for bit in reversed(bits):
        rows = double(rows, "ctx", bit).reshape(-1, n)
    return rows


def reduce_grad(blocks):
    return ring_sum(scatter_sum(blocks, "fsdp"))


def shards(
    tokens,
    starts,
    labels,
    cotangent,
    w_query,
    b_query,
    w_key,
    w_value,
    b_value,
    w_out,
    b_out,
    norm1_gain,
    norm1_bias,
    w_up,
    b_up,
    w_down,
    b_down,
    norm2_gain,
    norm2_bias,
    w_student,
    b_student,
    pool_query,
    w_pool,
    b_pool,
    w_class,
    b_class,
):
    cycle_size = lax.axis_size("ctx")
    cycle_index = lax.axis_index("ctx")
    fsdp_size = lax.axis_size("fsdp")
    fsdp_index = lax.axis_index("fsdp")
    tok_rows = tokens.shape[1]
    width = tokens.shape[2]
    part = width // fsdp_size
    seq_total = tok_rows * cycle_size
    score_scale = 1.0 / math.sqrt(HEAD_DIM)
    starts_row = starts[0]
    x_in = tokens[0]
    x_all = lax.all_gather(x_in, "ctx", axis=0, tiled=True)

    hidden_part = b_up.shape[0]
    ups = hidden_part // part
    pool_part, pool_width = w_pool.shape

    def pack(tall, pools, classes, vectors, ups_vector, pool_vectors, extra_row):
        first = jnp.concatenate(jnp.split(tall, width // pool_width, axis=0), axis=1)
        kind = tall.dtype
        room = width - 2 * pool_width
        half_room = room // 2
        cells = [jnp.pad(v, (0, half_room - part)) for v in vectors]
        cells += [jnp.pad(v, (0, half_room - part)) for v in jnp.split(ups_vector, ups)]
        lines = jnp.concatenate(cells).reshape(-1, room)
        last = jnp.concatenate(pool_vectors + [extra_row])
        lines = jnp.concatenate([lines, jnp.pad(last, (0, room - last.shape[0]))[None]], axis=0)
        lines = jnp.pad(lines, ((0, pool_part - lines.shape[0]), (0, 0)))
        second = jnp.concatenate(
            [pools, jnp.pad(classes, ((0, 0), (0, pool_width - CLASSES))), lines], axis=1
        )
        return jnp.concatenate([first, second], axis=0).astype(kind)

    def unpack(rows):
        blocks = rows.shape[0]
        high = part * pool_width // width
        first = rows[:, :high].reshape(blocks, high, width // pool_width, pool_width)
        tall = jnp.concatenate([first[:, :, k] for k in range(width // pool_width)], axis=1)
        second = rows[:, high:]
        room = width - 2 * pool_width
        half_room = room // 2
        lines = second[:, :, 2 * pool_width :]
        cells = [
            lines[:, k // 2, (k % 2) * half_room : (k % 2) * half_room + part] for k in range(8 + ups)
        ]
        last = lines[:, (8 + ups) // 2]
        return (
            tall.reshape(-1, pool_width),
            second[:, :, :pool_width].reshape(-1, pool_width),
            second[:, :, pool_width : pool_width + CLASSES].reshape(-1, CLASSES),
            [c.reshape(-1) for c in cells[:8]],
            jnp.stack(cells[8:], axis=1).reshape(-1),
            [last[:, k * pool_part : (k + 1) * pool_part].reshape(-1) for k in range(3)],
            last[0, 3 * pool_part : 3 * pool_part + CLASSES],
        )

    vectors = [b_query, b_value, b_out, norm1_gain, norm1_bias, b_down, norm2_gain, norm2_bias]
    small = pack(
        w_student, w_pool, w_class, vectors, b_up, [b_student, pool_query, b_pool], jnp.zeros((CLASSES,), bf16)
    )
    first = gather_shards(jnp.concatenate([w_query, w_key, w_value, small], axis=0)).reshape(
        fsdp_size, -1, width
    )
    full_wq = first[:, :part].reshape(width, width)
    full_wk = first[:, part : 2 * part].reshape(width, width)
    full_wv = first[:, 2 * part : 3 * part].reshape(width, width)
    full_wo = gather_shards(w_out)
    full_w1 = gather_shards(w_up)
    full_w2 = gather_shards(w_down)
    full_ws, pool_w, class_w, vectors, full_c1, pool_vectors, _ = unpack(first[:, 3 * part :])
    full_bq, full_bv, full_bo, gain_one, full_e1, full_c2, gain_two, full_e2 = (
        v.astype(f32) for v in vectors
    )
    full_bs, query_pool, full_bp = (v.astype(f32) for v in pool_vectors)
    full_c1, pool_w, class_w = full_c1.astype(f32), pool_w.astype(f32), class_w.astype(f32)

    local_pos = cycle_index * tok_rows + jnp.arange(tok_rows, dtype=jnp.int32)
    local_doc = doc_of(local_pos, starts_row)
    all_doc = doc_of(jnp.arange(seq_total, dtype=jnp.int32), starts_row)
    at = jnp.arange(128, dtype=jnp.int32)[None, :]
    extra = ((at == all_doc[:, None]) | ((at >= NDOC) & (at < NDOC + 3))).astype(bf16)
    docs = local_doc[None, :]

    query_b = (jnp.dot(x_in, full_wq, preferred_element_type=f32) + full_bq).astype(bf16)
    query_s = (query_b.astype(f32) * score_scale).astype(bf16)
    key_b = jnp.dot(x_all, full_wk, preferred_element_type=f32).astype(bf16)
    value_b = (jnp.dot(x_all, full_wv, preferred_element_type=f32) + full_bv).astype(bf16)
    attn_t, attn_b, lse = attend(query_s, key_b, value_b, extra, docs)

    branch = jnp.dot(attn_b, full_wo, preferred_element_type=f32) + full_bo
    hidden_one, normed_one, inv_one = layer_forward(x_in.astype(f32) + branch, gain_one, full_e1)
    hidden_one_b = hidden_one.astype(bf16)
    up_pre = jnp.dot(hidden_one_b, full_w1, preferred_element_type=f32) + full_c1
    up_b = jax.nn.gelu(up_pre, approximate=False).astype(bf16)
    down_out = jnp.dot(up_b, full_w2, preferred_element_type=f32) + full_c2
    layer_out, normed_two, inv_two = layer_forward(hidden_one + down_out, gain_two, full_e2)
    out_b = layer_out.astype(bf16)
    pool_dim = pool_width // POOL_HEADS
    pool_scale = 1.0 / math.sqrt(pool_dim)
    student = jnp.dot(out_b, full_ws, preferred_element_type=f32) + full_bs
    onehot_bool = local_doc[:, None] == jnp.arange(NDOC, dtype=jnp.int32)[None, :]
    onehot = onehot_bool.astype(f32)

    def pick_rows(table):
        return jnp.sum(jnp.where(onehot_bool[:, :, None], table[None, :, :], 0.0), axis=1)

    pool_scores = (
        jnp.sum((student * query_pool[None, :]).reshape(tok_rows, POOL_HEADS, pool_dim), axis=2)
        * pool_scale
    )
    local_max = jnp.max(
        jnp.where(onehot_bool[:, :, None], pool_scores[:, None, :], big_negative), axis=0
    )
    tok_weight = jnp.exp(pool_scores - pick_rows(local_max))
    local_total = small_dot(onehot.T, tok_weight)
    local_acc = small_dot(onehot.T, jnp.repeat(tok_weight, pool_dim, axis=1) * student)
    packed = jnp.concatenate([local_acc, jnp.pad(local_max, ((0, 0), (0, 62))), jnp.pad(local_total, ((0, 0), (0, 62)))], axis=1)
    parts = lax.all_to_all(jnp.broadcast_to(packed[None], (cycle_size,) + packed.shape), "ctx", 0, 0, tiled=True)
    part_acc = parts[:, :, :pool_width]
    part_max = parts[:, :, pool_width : pool_width + POOL_HEADS]
    part_total = parts[:, :, pool_width + 64 : pool_width + 64 + POOL_HEADS]
    doc_max = jnp.max(part_max, axis=0)
    factor = jnp.exp(part_max - doc_max[None])
    doc_total = jnp.sum(part_total * factor, axis=0)
    doc_acc = jnp.sum(part_acc * jnp.repeat(factor, pool_dim, axis=2), axis=0)
    pooled = doc_acc / jnp.repeat(doc_total, pool_dim, axis=1)
    head_act = jnp.tanh(small_dot(pooled, pool_w) + full_bp)
    logits = small_dot(head_act, class_w) + b_class.astype(f32)
    label_hot = (labels[0][:, None] == jnp.arange(CLASSES, dtype=jnp.int32)[None, :]).astype(f32)
    grad_logits = jax.nn.softmax(logits, axis=-1) - label_hot
    grad_wc = small_dot(head_act.T, grad_logits)
    grad_bc = jnp.sum(grad_logits, axis=0)
    grad_pre = small_dot(grad_logits, class_w.T) * (1.0 - head_act * head_act)
    grad_wp = small_dot(pooled.T, grad_pre)
    grad_bp = jnp.sum(grad_pre, axis=0)
    grad_pooled = small_dot(grad_pre, pool_w.T)
    tok_norm_w = jnp.exp(pool_scores - pick_rows(doc_max)) / pick_rows(doc_total)
    tok_gpool = pick_rows(grad_pooled)
    tok_pooled = pick_rows(pooled)
    inner_dot = jnp.sum(
        (tok_gpool * (student - tok_pooled)).reshape(tok_rows, POOL_HEADS, pool_dim), axis=2
    )
    grad_score = tok_norm_w * inner_dot
    spread_score = jnp.repeat(grad_score, pool_dim, axis=1)
    grad_student_f = (
        jnp.repeat(tok_norm_w, pool_dim, axis=1) * tok_gpool
        + spread_score * query_pool[None, :] * pool_scale
    )
    grad_qp = jnp.sum(spread_score * student, axis=0) * pool_scale
    grad_student_b = grad_student_f.astype(bf16)
    grad_ws = cross_rows(out_b, grad_student_b)
    grad_bs = jnp.sum(grad_student_b.astype(f32), axis=0)
    grad_layer = cotangent[0].astype(f32) + back_mul(grad_student_b, full_ws)
    grad_res2, grad_g2, grad_e2 = layer_backward(grad_layer, normed_two, inv_two, gain_two)
    grad_down_b = grad_res2.astype(bf16)
    grad_w2 = cross_rows(up_b, grad_down_b).astype(bf16)
    done_w2 = reduce_grad(grad_w2.reshape(fsdp_size, -1, width))
    grad_c2 = jnp.sum(grad_down_b.astype(f32), axis=0)
    grad_up_b = (back_mul(grad_down_b, full_w2) * gelu_slope(up_pre)).astype(bf16)
    grad_w1 = cross_rows(hidden_one_b, grad_up_b).astype(bf16)
    grad_w1 = grad_w1.reshape(fsdp_size, part, -1)
    done_w1 = reduce_grad(
        jnp.concatenate([grad_w1[:, :, k * width : (k + 1) * width] for k in range(ups)], axis=1)
    )
    grad_c1 = jnp.sum(grad_up_b.astype(f32), axis=0)
    grad_hidden = grad_res2 + back_mul(grad_up_b, full_w1)
    grad_res1, grad_g1, grad_e1 = layer_backward(grad_hidden, normed_one, inv_one, gain_one)
    grad_branch_b = grad_res1.astype(bf16)
    grad_wo = cross_rows(attn_b, grad_branch_b).astype(bf16)
    grad_bo = jnp.sum(grad_branch_b.astype(f32), axis=0)
    grad_attn_b = back_mul(grad_branch_b, full_wo).astype(bf16)

    grad_query_b, grad_key_b, grad_value_b = attend_back(
        query_s, key_b, value_b, extra, docs, attn_t, lse, grad_attn_b
    )
    others = (back_mul(grad_key_b, full_wk) + back_mul(grad_value_b, full_wv)).astype(bf16)
    others = scatter_sum(others.reshape(cycle_size, tok_rows, width), "ctx")
    grad_wq = cross_rows(x_in, grad_query_b).astype(bf16)
    grad_bq = jnp.sum(grad_query_b.astype(f32), axis=0)
    grad_wk = cross_rows(x_all, grad_key_b).astype(bf16)
    grad_wv = cross_rows(x_all, grad_value_b).astype(bf16)
    grad_bv = jnp.sum(grad_value_b.astype(f32), axis=0)
    grad_tokens = grad_res1 + back_mul(grad_query_b, full_wq) + others.astype(f32)

    head_owner = (cycle_index == 0).astype(f32)
    zero_row = jnp.zeros((width,), f32)

    def block(value, k):
        size = value.shape[0] // fsdp_size
        return value[k * size : (k + 1) * size]

    vectors = [zero_row, zero_row, grad_bo, grad_g1, grad_e1, grad_c2, grad_g2, grad_e2]
    small = jnp.stack(
        [
            pack(
                block(grad_ws, k),
                block(grad_wp, k) * head_owner,
                block(grad_wc, k) * head_owner,
                [block(v, k) for v in vectors],
                block(grad_c1, k),
                [block(grad_bs, k), block(grad_qp, k), block(grad_bp, k) * head_owner],
                grad_bc * head_owner,
            )
            for k in range(fsdp_size)
        ]
    ).astype(bf16)
    middle = reduce_grad(jnp.concatenate([grad_wo.reshape(fsdp_size, part, width), small], axis=1))
    middle = middle.astype(f32)
    done_ws, done_wp, done_wc, done_v, done_c1, done_p, done_bc = unpack(middle[None, part:])
    done_wo = middle[:part]
    late = jnp.concatenate([grad_bq.reshape(fsdp_size, 1, part), grad_bv.reshape(fsdp_size, 1, part)], axis=1)
    late = jnp.pad(late, ((0, 0), (0, 62), (0, width - part))).astype(bf16)
    last = jnp.concatenate(
        [g.reshape(fsdp_size, part, width) for g in (grad_wq, grad_wk, grad_wv)] + [late], axis=1
    )
    last = reduce_grad(last).astype(f32)
    done_wq, done_wk, done_wv = (last[k * part : (k + 1) * part] for k in range(3))
    done_v[0] = last[3 * part, :part]
    done_v[1] = last[3 * part + 1, :part]
    done_w1 = jnp.concatenate(jnp.split(done_w1.astype(f32), ups, axis=0), axis=1)
    return (
        out_b[None],
        logits[None],
        grad_tokens[None],
        done_wq,
        done_v[0],
        done_wk,
        done_wv,
        done_v[1],
        done_wo,
        done_v[2],
        done_v[3],
        done_v[4],
        done_w1,
        done_c1,
        done_w2.astype(f32),
        done_v[5],
        done_v[6],
        done_v[7],
        done_ws,
        done_p[0],
        done_p[1],
        done_wp,
        done_p[2],
        done_wc,
        done_bc,
    )


def solution(mesh):
    in_specs = (
        P("fsdp", "ctx", None),
        P("fsdp", None),
        P("fsdp", None),
        P("fsdp", "ctx", None),
        P("fsdp", None),
        P("fsdp"),
        P("fsdp", None),
        P("fsdp", None),
        P("fsdp"),
        P("fsdp", None),
        P("fsdp"),
        P("fsdp"),
        P("fsdp"),
        P("fsdp", None),
        P("fsdp"),
        P("fsdp", None),
        P("fsdp"),
        P("fsdp"),
        P("fsdp"),
        P("fsdp", None),
        P("fsdp"),
        P("fsdp"),
        P("fsdp", None),
        P("fsdp"),
        P("fsdp", None),
        P(),
    )
    out_specs = (
        P("fsdp", "ctx", None),
        P("fsdp", None, None),
        P("fsdp", "ctx", None),
        P("fsdp", None),
        P("fsdp"),
        P("fsdp", None),
        P("fsdp", None),
        P("fsdp"),
        P("fsdp", None),
        P("fsdp"),
        P("fsdp"),
        P("fsdp"),
        P("fsdp", None),
        P("fsdp"),
        P("fsdp", None),
        P("fsdp"),
        P("fsdp"),
        P("fsdp"),
        P("fsdp", None),
        P("fsdp"),
        P("fsdp"),
        P("fsdp", None),
        P("fsdp"),
        P("fsdp", None),
        P(),
    )
    return jax.shard_map(shards, mesh=mesh, in_specs=in_specs, out_specs=out_specs, check_vma=False)
```

time: 1160 us -> 634 us (0.55)
  waiting for transfers between devices: 607 us -> 214 us
  blocking collectives: 146 us -> 0 us
  matrix products: 173 us -> 65.3 us
  local copies, waits for them, and re-layouts: 107 us -> 168 us
  Pallas kernels: 0 us -> 39.1 us
  starting transfers between devices: 0.81 us -> 29.6 us
    reduce_scatter x7 -> x0, waiting for transfers between devices: 301 us -> none  [the longest x1 73.9 us: shards(): lax.psum_scatter(value_terms.reshape(seq_total, width).astype(jnp.bfloat1...]
    ppermute x0 -> x43, waiting for transfers between devices: none -> 208 us  [swap(): return lax.ppermute(value, axis, [(i, i ^ bit) for i in range(count)])]
    all_gather x8 -> x1, waiting for transfers between devices: 127 us -> 0.02 us  [shards(): x_all = lax.all_gather(x_in, 'ctx', axis=0, tiled=True)]
    dot_general x33 -> x7, matrix products: 142 us -> 26.7 us  [the longest x1 9.48 us: shards(): jnp.dot(hidden_one_b, full_w1, preferred_element_type=f32) + full_c1]
    psum x1 -> x0, waiting for transfers between devices: 101 us -> none  [shards(): lax.psum(scattered[0].astype(jnp.bfloat16), 'ctx').astype(jnp.float32)]
    all_gather x7 -> x0, blocking collectives: 83.1 us -> none  [the longest x3 61 us: joined(): everything = jax.tree.map(lambda part: lax.all_gather(part, axis), shard)]
    unnamed x24 -> x1, waiting for transfers between devices: 78.3 us -> 0.68 us
    unnamed x244 -> x231, local copies, waits for them, and re-layouts: 26.5 us -> 85.9 us
  transfers between devices with their start and end apart: 20 -> 45, of which waited for: 16 -> 28; matrix products, arithmetic and copies ran while one was open for 20% -> 21% of each run, Pallas kernels for 0% -> 0%
where the time goes in v1:
time: 634 us; the launch traced here: 622 us
  waiting for transfers between devices  214 us (34%)
  local copies, waits for them, and re-layouts  168 us (26%)
  other arithmetic  89.4 us (14%)
  matrix products  65.3 us (10%)
  Pallas kernels  39.1 us (6%)
  starting transfers between devices  29.6 us (5%)
  between operations  16.5 us (3%)
    ppermute x43, waiting for transfers between devices, swap(): return lax.ppermute(value, axis, [(i, i ^ bit) for i in range(count)])  208 us
    unnamed x231, local copies, waits for them, and re-layouts  85.9 us
    pallas_call x1, Pallas kernels, attend_back(): pl.pallas_call(functools.partial(attend_back_kernel, 4), grid=(pairs,), i...  23.8 us
    ppermute x43, starting transfers between devices, swap(): return lax.ppermute(value, axis, [(i, i ^ bit) for i in range(count)])  23.2 us
    select_n x8, other arithmetic, gather_shards(): jnp.where(far == 0, jnp.stack([shard, other]), jnp.stack([other, shard]))  18.7 us
    pad x26, local copies, waits for them, and re-layouts, pack(): cells = [jnp.pad(v, (0, half_room - part)) for v in vectors]  17 us
    dot_general x7, matrix products, back_mul(): lax.dot_general(left_mat, right_mat, (((1,), (1,)), ((), ())), preferred_...  16.7 us
    pallas_call x1, Pallas kernels, attend(): pl.pallas_call(functools.partial(attend_kernel, 4), grid=(pairs,), in_spe...  15.3 us
  transfers between devices with their start and end apart: 45, of which 28 were waited for; matrix products, arithmetic and copies ran while one was open for 21% of the time, Pallas kernels for 0%

profile of v1, /device:TPU:0, one launch (start us, length us, event | category | flops | bytes accessed | tf_op | source)
XLA Modules:
  0.0 621.7 jit_solution(11741492935008555461)
XLA Ops:
  45.5 8.4 %collective-permute-done = bf16[640,768]{1,0:T(8,128)(2,1)S(1)} collective-permute-done((bf16[640,768]{1,0:T(8,128)(2,1)S(1)}, bf16[640,768]{1,0:T(8,128)(2,1)S(1)}, u32[]{:S(2)}, u32[]{:S(2)}) %collective-permute-start) | collective-permute-done | bytes 983072 | tf_op jit(solution)/shard_map/ppermute | solution.py:253
  56.5 22.8 %collective-permute-done.4 = bf16[192,3072]{1,0:T(8,128)(2,1)} collective-permute-done((bf16[192,3072]{1,0:T(8,128)(2,1)}, bf16[192,3072]{1,0:T(8,128)(2,1)}, u32[]{:S(2)}, u32[]{:S(2)}) %collective-permute-start.4) | collective-permute-done | bytes 1179680 | tf_op jit(solution)/shard_map/ppermute | solution.py:253
  79.3 4.3 maximum_select_fusion.4
  83.6 19.6 %collective-permute-done.6 = bf16[768,768]{1,0:T(8,128)(2,1)} collective-permute-done((bf16[768,768]{1,0:T(8,128)(2,1)}, bf16[768,768]{1,0:T(8,128)(2,1)}, u32[]{:S(2)}, u32[]{:S(2)}) %collective-permute-start.6) | collective-permute-done | bytes 1179680 | tf_op jit(solution)/shard_map/ppermute | solution.py:253
  103.1 4.3 maximum_select_fusion.6
  107.5 4.2 maximum_select_fusion.5
  111.7 4.3 maximum_select_fusion.3
  136.3 5.8 maximum_select_fusion
  142.1 5.9 maximum_select_fusion.1
  148.1 6.6 %fusion.25.k_ref = bf16[2048,768]{1,0:T(8,128)(2,1)} fusion(bf16[768,768]{1,0:T(8,128)(2,1)} %bitcast.447, bf16[1,2048,768]{2,1,0:T(8,128)(2,1)} %all-gather.3.cloned.1.call-done), kind=kOutput, calls=%fused_computation.52 | convolution fusion | flops 2417491968 | bytes 7471104 | tf_op jit(solution)/shard_map/dot_general | solution.py:420
  158.7 15.3 %attend.1 = (f32[768,256]{1,0:T(8,128)}, bf16[256,768]{1,0:T(8,128)(2,1)}, f32[6,2,256]{2,1,0:T(2,128)}) custom-call(bf16[256,768]{1,0:T(8,128)(2,1)} %fusion.45.q_ref, bf16[2048,768]{1,0:T(8,128)(2,1)} %fusion.25.k_ref, bf16[2048,768]{1,0:T(8,128)(2,1)} %fusion.28.v_ref, bf16[2048,128]{1,0:T(8,128)(2,1)} %fusion.50.extra_ref, s32[1,256]{1,0:T(1,128)} %bitcast.505), custom_call_target="tpu_custom_call" | custom-call | flops 1610612736 | bytes 6291456 | tf_op jit(solution)/shard_map/attend/pallas_call | solution.py:124
  176.0 9.5 %fusion.6 = (bf16[256,3072]{1,0:T(8,128)(2,1)S(1)}, f32[256,3072]{1,0:T(8,128)}) fusion(f32[3072]{0:T(1024)S(1)} %reshape.1065, bf16[768,3072]{1,0:T(8,128)(2,1)S(1)} %bitcast.407, f32[256,768]{1,0:T(8,128)S(1)} %get-tuple-element.458, f32[768]{0:T(1024)S(1)} %reshape.1064, f32[768]{0:T(1024)S(1)} %reshape.1063, f32[256]{0:T(256)S(1)} %add_rsqrt_fusion.1, ...), kind=kOutput, calls=%fused_computation.23 | convolution fusion | flops 1260847104 | bytes 10244096 | tf_op jit(solution)/shard_map/dot_general | solution.py:427
  197.5 6.3 %all-to-all-start = ((f32[8,4,256]{2,1,0:T(4,128)}), f32[8,4,256]{2,1,0:T(4,128)}, u32[]{:S(2)}, u32[]{:S(2)}) async-start(f32[8,4,256]{2,1,0:T(4,128)} %broadcast_in_dim.192), calls=%async_computation | async-start | bytes 65536 | tf_op jit(solution)/shard_map/all_to_all | solution.py:452
  205.5 5.1 all-to-all-done
  252.0 4.6 convert_reduce_fusion
  265.0 23.8 %attend_back.1 = (bf16[256,768]{1,0:T(8,128)(2,1)}, bf16[2048,768]{1,0:T(8,128)(2,1)}, bf16[2048,768]{1,0:T(8,128)(2,1)}) custom-call(bf16[256,768]{1,0:T(8,128)(2,1)} %fusion.45.q_ref, bf16[2048,768]{1,0:T(8,128)(2,1)} %fusion.25.k_ref, bf16[2048,768]{1,0:T(8,128)(2,1)} %fusion.28.v_ref, bf16[2048,128]{1,0:T(8,128)(2,1)} %fusion.50.extra_ref, ...), custom_call_target="tpu_custom_call" | custom-call | flops 4026531840 | bytes 12582912 | tf_op jit(solution)/shard_map/attend_back/pallas_call | solution.py:220
  402.4 7.4 %collective-permute-done.20 = bf16[1,256,768]{2,1,0:T(8,128)(2,1)S(1)} collective-permute-done((bf16[1,256,768]{2,1,0:T(8,128)(2,1)S(1)}, bf16[1,256,768]{2,1,0:T(8,128)(2,1)S(1)}, u32[]{:S(2)}, u32[]{:S(2)}) %collective-permute-start.20) | collective-permute-done | bytes 393248 | tf_op jit(solution)/shard_map/ppermute | solution.py:253
  412.0 16.1 %collective-permute-done.21 = bf16[128,768]{1,0:T(8,128)(2,1)S(1)} collective-permute-done((bf16[128,768]{1,0:T(8,128)(2,1)S(1)}, bf16[128,768]{1,0:T(8,128)(2,1)S(1)}, u32[]{:S(2)}, u32[]{:S(2)}) %collective-permute-start.21) | collective-permute-done | bytes 196640 | tf_op jit(solution)/shard_map/ppermute | solution.py:253
  439.4 4.1 collective-permute-done.24
  468.1 17.0 %collective-permute-done.12 = bf16[1,640,768]{2,1,0:T(8,128)(2,1)S(1)} collective-permute-done((bf16[1,640,768]{2,1,0:T(8,128)(2,1)S(1)}, bf16[1,640,768]{2,1,0:T(8,128)(2,1)S(1)}, u32[]{:S(2)}, u32[]{:S(2)}) %collective-permute-start.12) | collective-permute-done | bytes 983072 | tf_op jit(solution)/shard_map/ppermute | solution.py:253
  491.1 4.2 collective-permute-done.13
  497.2 13.3 %collective-permute-done.36 = bf16[1,768,768]{2,1,0:T(8,128)(2,1)} collective-permute-done((bf16[1,768,768]{2,1,0:T(8,128)(2,1)}, bf16[1,768,768]{2,1,0:T(8,128)(2,1)}, u32[]{:S(2)}, u32[]{:S(2)}) %collective-permute-start.36) | collective-permute-done | bytes 1179680 | tf_op jit(solution)/shard_map/ppermute | solution.py:253
  513.1 18.0 %collective-permute-done.28 = bf16[1,768,768]{2,1,0:T(8,128)(2,1)} collective-permute-done((bf16[1,768,768]{2,1,0:T(8,128)(2,1)}, bf16[1,768,768]{2,1,0:T(8,128)(2,1)}, u32[]{:S(2)}, u32[]{:S(2)}) %collective-permute-start.28) | collective-permute-done | bytes 1179680 | tf_op jit(solution)/shard_map/ppermute | solution.py:253
  534.4 8.4 %collective-permute-done.15 = bf16[80,768]{1,0:T(8,128)(2,1)S(1)} collective-permute-done((bf16[80,768]{1,0:T(8,128)(2,1)S(1)}, bf16[80,768]{1,0:T(8,128)(2,1)S(1)}, u32[]{:S(2)}, u32[]{:S(2)}) %collective-permute-start.15) | collective-permute-done | bytes 122912 | tf_op jit(solution)/shard_map/ppermute | solution.py:253
  544.0 5.2 collective-permute-done.16
  551.9 7.9 %collective-permute-done.17 = bf16[160,768]{1,0:T(8,128)(2,1)S(1)} collective-permute-done((bf16[160,768]{1,0:T(8,128)(2,1)S(1)}, bf16[160,768]{1,0:T(8,128)(2,1)S(1)}, u32[]{:S(2)}, u32[]{:S(2)}) %collective-permute-start.17) | collective-permute-done | bytes 245792 | tf_op jit(solution)/shard_map/ppermute | solution.py:253
  563.4 5.1 collective-permute-done.30
  569.5 7.1 %collective-permute-done.39 = bf16[96,768]{1,0:T(8,128)(2,1)S(1)} collective-permute-done((bf16[96,768]{1,0:T(8,128)(2,1)S(1)}, bf16[96,768]{1,0:T(8,128)(2,1)S(1)}, u32[]{:S(2)}, u32[]{:S(2)}) %collective-permute-start.39) | collective-permute-done | bytes 147488 | tf_op jit(solution)/shard_map/ppermute | solution.py:253
  579.9 4.4 collective-permute-done.40
  587.1 4.9 collective-permute-done.41
  596.8 9.0 %collective-permute-done.42 = bf16[384,768]{1,0:T(8,128)(2,1)S(1)} collective-permute-done((bf16[384,768]{1,0:T(8,128)(2,1)S(1)}, bf16[384,768]{1,0:T(8,128)(2,1)S(1)}, u32[]{:S(2)}, u32[]{:S(2)}) %collective-permute-start.42) | collective-permute-done | bytes 589856 | tf_op jit(solution)/shard_map/ppermute | solution.py:253
  607.6 4.5 collective-permute-done.34
  (605 shorter events, 317.9 us)
Async XLA Ops:
  7.2 140.8 %all-gather.3.cloned.1.call-start = ((), (), s32[]{:S(2)}) async-start(), calls=%async_computation.1 | async-start | bytes 3538944 | tf_op jit(solution)/shard_map/all_gather | solution.py:346
  8.0 24.7 %collective-permute-start.2 = (bf16[192,768]{1,0:T(8,128)(2,1)}, bf16[192,768]{1,0:T(8,128)(2,1)S(1)}, u32[]{:S(2)}, u32[]{:S(2)}) collective-permute-start(bf16[192,768]{1,0:T(8,128)(2,1)} %param.35), channel_id=1, source_target_pairs={{0,2},{1,3},{2,0},{3,1},{4,6},{5,7},{6,4},{7,5},{8,10},{9,11},{10,... | collective-permute-start | bytes 884744 | tf_op jit(solution)/shard_map/ppermute | solution.py:253
  29.2 24.7 %collective-permute-start = (bf16[640,768]{1,0:T(8,128)(2,1)S(1)}, bf16[640,768]{1,0:T(8,128)(2,1)S(1)}, u32[]{:S(2)}, u32[]{:S(2)}) collective-permute-start(bf16[640,768]{1,0:T(8,128)(2,1)S(1)} %constant_dynamic-update-slice_fusion), channel_id=1, source_target_pairs={{0,2},{1,3},{2,0},{3,1},{4,6},{5,7},{6,4},{7,5},{8,10},{9,11},{10,... | collective-permute-start | bytes 2949128 | tf_op jit(solution)/shard_map/ppermute | solution.py:253
  29.3 50.0 %collective-permute-start.4 = (bf16[192,3072]{1,0:T(8,128)(2,1)}, bf16[192,3072]{1,0:T(8,128)(2,1)}, u32[]{:S(2)}, u32[]{:S(2)}) collective-permute-start(bf16[192,3072]{1,0:T(8,128)(2,1)} %param.39), channel_id=1, source_target_pairs={{0,2},{1,3},{2,0},{3,1},{4,6},{5,7},{6,4},{7,5},{8,10},{9,11},{10,... | collective-permute-start | bytes 3538952 | tf_op jit(solution)/shard_map/ppermute | solution.py:253
  31.3 71.9 %collective-permute-start.6 = (bf16[768,768]{1,0:T(8,128)(2,1)}, bf16[768,768]{1,0:T(8,128)(2,1)}, u32[]{:S(2)}, u32[]{:S(2)}) collective-permute-start(bf16[768,768]{1,0:T(8,128)(2,1)} %param.41), channel_id=1, source_target_pairs={{0,2},{1,3},{2,0},{3,1},{4,6},{5,7},{6,4},{7,5},{8,10},{9,11},{10,... | collective-permute-start | bytes 3538952 | tf_op jit(solution)/shard_map/ppermute | solution.py:253
  33.6 21.4 %collective-permute-start.3 = (bf16[2,192,768]{2,1,0:T(8,128)(2,1)}, bf16[2,192,768]{2,1,0:T(8,128)(2,1)S(1)}, u32[]{:S(2)}, u32[]{:S(2)}) collective-permute-start(bf16[2,192,768]{2,1,0:T(8,128)(2,1)} %maximum_select_fusion.14), channel_id=1, source_target_pairs={{0,1},{1,0},{2,3},{3,2},{4,5},{5,4},{6,7},{7,6},{8,9},{9,8},{10,11... | collective-permute-start | bytes 1769480 | tf_op jit(solution)/shard_map/ppermute | solution.py:253
  54.2 61.7 %collective-permute-start.1 = (bf16[2,640,768]{2,1,0:T(8,128)(2,1)S(1)}, bf16[2,640,768]{2,1,0:T(8,128)(2,1)S(1)}, u32[]{:S(2)}, u32[]{:S(2)}) collective-permute-start(bf16[2,640,768]{2,1,0:T(8,128)(2,1)S(1)} %maximum_select_fusion.8), channel_id=1, source_target_pairs={{0,1},{1,0},{2,3},{3,2},{4,5},{5,4},{6,7},{7,6},{8,9},{9,8},{10,11... | collective-permute-start | bytes 5898248 | tf_op jit(solution)/shard_map/ppermute | solution.py:253
  83.6 52.8 %collective-permute-start.5 = (bf16[2,192,3072]{2,1,0:T(8,128)(2,1)}, bf16[2,192,3072]{2,1,0:T(8,128)(2,1)}, u32[]{:S(2)}, u32[]{:S(2)}) collective-permute-start(bf16[2,192,3072]{2,1,0:T(8,128)(2,1)} %maximum_select_fusion.4), channel_id=1, source_target_pairs={{0,1},{1,0},{2,3},{3,2},{4,5},{5,4},{6,7},{7,6},{8,9},{9,8},{10,11... | collective-permute-start | bytes 7077896 | tf_op jit(solution)/shard_map/ppermute | solution.py:253
  107.4 34.6 %collective-permute-start.7 = (bf16[2,768,768]{2,1,0:T(8,128)(2,1)}, bf16[2,768,768]{2,1,0:T(8,128)(2,1)}, u32[]{:S(2)}, u32[]{:S(2)}) collective-permute-start(bf16[2,768,768]{2,1,0:T(8,128)(2,1)} %maximum_select_fusion.6), channel_id=1, source_target_pairs={{0,1},{1,0},{2,3},{3,2},{4,5},{5,4},{6,7},{7,6},{8,9},{9,8},{10,11... | collective-permute-start | bytes 7077896 | tf_op jit(solution)/shard_map/ppermute | solution.py:253
  197.5 13.0 %all-to-all-start = ((f32[8,4,256]{2,1,0:T(4,128)}), f32[8,4,256]{2,1,0:T(4,128)}, u32[]{:S(2)}, u32[]{:S(2)}) async-start(f32[8,4,256]{2,1,0:T(4,128)} %broadcast_in_dim.192), calls=%async_computation | async-start | bytes 65536 | tf_op jit(solution)/shard_map/all_to_all | solution.py:452
  380.7 18.7 %collective-permute-start.19 = (bf16[2,256,768]{2,1,0:T(8,128)(2,1)S(1)}, bf16[2,256,768]{2,1,0:T(8,128)(2,1)S(1)}, u32[]{:S(2)}, u32[]{:S(2)}) collective-permute-start(bf16[2,256,768]{2,1,0:T(8,128)(2,1)S(1)} %fusion.53), channel_id=1, source_target_pairs={{0,1},{1,0},{2,3},{3,2},{4,5},{5,4},{6,7},{7,6},{8,9},{9,8},{10,11... | collective-permute-start | bytes 2359304 | tf_op jit(solution)/shard_map/ppermute | solution.py:253
  388.4 60.7 %collective-permute-start.8 = (bf16[4,256,768]{2,1,0:T(8,128)(2,1)S(1)}, bf16[4,256,768]{2,1,0:T(8,128)(2,1)S(1)}, u32[]{:S(2)}, u32[]{:S(2)}) collective-permute-start(bf16[4,256,768]{2,1,0:T(8,128)(2,1)S(1)} %dynamic-slice_bitcast_fusion.3), channel_id=1, source_target_pairs={{0,4},{4,0},{8,12},{12,8},{16,20},{20,16},{24,28},{28,24},{1,5},{5... | collective-permute-start | bytes 4718600 | tf_op jit(solution)/shard_map/ppermute | solution.py:253
  409.9 18.1 %collective-permute-start.21 = (bf16[128,768]{1,0:T(8,128)(2,1)S(1)}, bf16[128,768]{1,0:T(8,128)(2,1)S(1)}, u32[]{:S(2)}, u32[]{:S(2)}) collective-permute-start(bf16[128,768]{1,0:T(8,128)(2,1)S(1)} %dynamic-slice_bitcast_fusion.11), channel_id=1, source_target_pairs={{0,4},{4,0},{8,12},{12,8},{16,20},{20,16},{24,28},{28,24},{1,5},{5... | collective-permute-start | bytes 589832 | tf_op jit(solution)/shard_map/ppermute | solution.py:253
  430.0 27.5 %collective-permute-start.11 = (bf16[2,640,768]{2,1,0:T(8,128)(2,1)}, bf16[2,640,768]{2,1,0:T(8,128)(2,1)}, u32[]{:S(2)}, u32[]{:S(2)}) collective-permute-start(bf16[2,640,768]{2,1,0:T(8,128)(2,1)} %dynamic-slice_bitcast_fusion.2), channel_id=1, source_target_pairs={{0,1},{1,0},{2,3},{3,2},{4,5},{5,4},{6,7},{7,6},{8,9},{9,8},{10,11... | collective-permute-start | bytes 5898248 | tf_op jit(solution)/shard_map/ppermute | solution.py:253
  435.3 25.7 %collective-permute-start.35 = (bf16[2,768,768]{2,1,0:T(8,128)(2,1)}, bf16[2,768,768]{2,1,0:T(8,128)(2,1)S(1)}, u32[]{:S(2)}, u32[]{:S(2)}) collective-permute-start(bf16[2,768,768]{2,1,0:T(8,128)(2,1)} %dynamic-slice_bitcast_fusion), channel_id=1, source_target_pairs={{0,1},{1,0},{2,3},{3,2},{4,5},{5,4},{6,7},{7,6},{8,9},{9,8},{10,11... | collective-permute-start | bytes 7077896 | tf_op jit(solution)/shard_map/ppermute | solution.py:253
  445.1 19.2 %collective-permute-start.27 = (bf16[2,768,768]{2,1,0:T(8,128)(2,1)}, bf16[2,768,768]{2,1,0:T(8,128)(2,1)}, u32[]{:S(2)}, u32[]{:S(2)}) collective-permute-start(bf16[2,768,768]{2,1,0:T(8,128)(2,1)} %dynamic-slice_bitcast_fusion.1), channel_id=1, source_target_pairs={{0,1},{1,0},{2,3},{3,2},{4,5},{5,4},{6,7},{7,6},{8,9},{9,8},{10,11... | collective-permute-start | bytes 7077896 | tf_op jit(solution)/shard_map/ppermute | solution.py:253
  450.6 38.7 %collective-permute-start.9 = (bf16[2,256,768]{2,1,0:T(8,128)(2,1)}, bf16[2,256,768]{2,1,0:T(8,128)(2,1)}, u32[]{:S(2)}, u32[]{:S(2)}) collective-permute-start(bf16[2,256,768]{2,1,0:T(8,128)(2,1)} %dynamic-slice_bitcast_fusion.4), channel_id=1, source_target_pairs={{0,8},{4,12},{8,0},{12,4},{16,24},{20,28},{24,16},{28,20},{1,9},{5... | collective-permute-start | bytes 2359304 | tf_op jit(solution)/shard_map/ppermute | solution.py:253
  460.4 24.8 %collective-permute-start.12 = (bf16[1,640,768]{2,1,0:T(8,128)(2,1)S(1)}, bf16[1,640,768]{2,1,0:T(8,128)(2,1)S(1)}, u32[]{:S(2)}, u32[]{:S(2)}) collective-permute-start(bf16[1,640,768]{2,1,0:T(8,128)(2,1)S(1)} %constant_dynamic-slice_fusion.3), channel_id=1, source_target_pairs={{0,2},{1,3},{2,0},{3,1},{4,6},{5,7},{6,4},{7,5},{8,10},{9,11},{10,... | collective-permute-start | bytes 2949128 | tf_op jit(solution)/shard_map/ppermute | solution.py:253
  462.7 47.8 %collective-permute-start.36 = (bf16[1,768,768]{2,1,0:T(8,128)(2,1)}, bf16[1,768,768]{2,1,0:T(8,128)(2,1)}, u32[]{:S(2)}, u32[]{:S(2)}) collective-permute-start(bf16[1,768,768]{2,1,0:T(8,128)(2,1)} %constant_dynamic-slice_fusion), channel_id=1, source_target_pairs={{0,2},{1,3},{2,0},{3,1},{4,6},{5,7},{6,4},{7,5},{8,10},{9,11},{10,... | collective-permute-start | bytes 3538952 | tf_op jit(solution)/shard_map/ppermute | solution.py:253
  467.7 63.4 %collective-permute-start.28 = (bf16[1,768,768]{2,1,0:T(8,128)(2,1)}, bf16[1,768,768]{2,1,0:T(8,128)(2,1)}, u32[]{:S(2)}, u32[]{:S(2)}) collective-permute-start(bf16[1,768,768]{2,1,0:T(8,128)(2,1)} %constant_dynamic-slice_fusion.1), channel_id=1, source_target_pairs={{0,2},{1,3},{2,0},{3,1},{4,6},{5,7},{6,4},{7,5},{8,10},{9,11},{10,... | collective-permute-start | bytes 3538952 | tf_op jit(solution)/shard_map/ppermute | solution.py:253
  491.1 51.9 %collective-permute-start.10 = (bf16[1,256,768]{2,1,0:T(8,128)(2,1)S(1)}, bf16[1,256,768]{2,1,0:T(8,128)(2,1)S(1)}, u32[]{:S(2)}, u32[]{:S(2)}) collective-permute-start(bf16[1,256,768]{2,1,0:T(8,128)(2,1)S(1)} %constant_dynamic-slice_fusion.4), channel_id=1, source_target_pairs={{0,16},{4,20},{8,24},{12,28},{16,0},{20,4},{24,8},{28,12},{1,17},{... | collective-permute-start | bytes 1179656 | tf_op jit(solution)/shard_map/ppermute | solution.py:253
  496.5 36.1 %collective-permute-start.14 = (bf16[160,768]{1,0:T(8,128)(2,1)S(1)}, bf16[160,768]{1,0:T(8,128)(2,1)S(1)}, u32[]{:S(2)}, u32[]{:S(2)}) collective-permute-start(bf16[160,768]{1,0:T(8,128)(2,1)S(1)} %dynamic-slice_bitcast_fusion.10), channel_id=1, source_target_pairs={{0,8},{4,12},{8,0},{12,4},{16,24},{20,28},{24,16},{28,20},{1,9},{5... | collective-permute-start | bytes 737288 | tf_op jit(solution)/shard_map/ppermute | solution.py:253
  512.2 37.1 %collective-permute-start.37 = (bf16[384,768]{1,0:T(8,128)(2,1)S(1)}, bf16[384,768]{1,0:T(8,128)(2,1)S(1)}, u32[]{:S(2)}, u32[]{:S(2)}) collective-permute-start(bf16[384,768]{1,0:T(8,128)(2,1)S(1)} %dynamic-slice_bitcast_fusion.5), channel_id=1, source_target_pairs={{0,4},{4,0},{8,12},{12,8},{16,20},{20,16},{24,28},{28,24},{1,5},{5... | collective-permute-start | bytes 1769480 | tf_op jit(solution)/shard_map/ppermute | solution.py:253
  533.7 17.9 %collective-permute-start.29 = (bf16[384,768]{1,0:T(8,128)(2,1)S(1)}, bf16[384,768]{1,0:T(8,128)(2,1)S(1)}, u32[]{:S(2)}, u32[]{:S(2)}) collective-permute-start(bf16[384,768]{1,0:T(8,128)(2,1)S(1)} %dynamic-slice_bitcast_fusion.6), channel_id=1, source_target_pairs={{0,4},{4,0},{8,12},{12,8},{16,20},{20,16},{24,28},{28,24},{1,5},{5... | collective-permute-start | bytes 1769480 | tf_op jit(solution)/shard_map/ppermute | solution.py:253
  549.2 10.5 %collective-permute-start.17 = (bf16[160,768]{1,0:T(8,128)(2,1)S(1)}, bf16[160,768]{1,0:T(8,128)(2,1)S(1)}, u32[]{:S(2)}, u32[]{:S(2)}) collective-permute-start(bf16[160,768]{1,0:T(8,128)(2,1)S(1)} %bitcast.463), channel_id=1, source_target_pairs={{0,8},{4,12},{8,0},{12,4},{16,24},{20,28},{24,16},{28,20},{1,9},{5... | collective-permute-start | bytes 737288 | tf_op jit(solution)/shard_map/ppermute | solution.py:253
  549.5 13.7 %collective-permute-start.38 = (bf16[192,768]{1,0:T(8,128)(2,1)S(1)}, bf16[192,768]{1,0:T(8,128)(2,1)S(1)}, u32[]{:S(2)}, u32[]{:S(2)}) collective-permute-start(bf16[192,768]{1,0:T(8,128)(2,1)S(1)} %dynamic-slice_bitcast_fusion.8), channel_id=1, source_target_pairs={{0,8},{4,12},{8,0},{12,4},{16,24},{20,28},{24,16},{28,20},{1,9},{5... | collective-permute-start | bytes 884744 | tf_op jit(solution)/shard_map/ppermute | solution.py:253
  551.8 16.7 %collective-permute-start.30 = (bf16[192,768]{1,0:T(8,128)(2,1)S(1)}, bf16[192,768]{1,0:T(8,128)(2,1)S(1)}, u32[]{:S(2)}, u32[]{:S(2)}) collective-permute-start(bf16[192,768]{1,0:T(8,128)(2,1)S(1)} %dynamic-slice_bitcast_fusion.9), channel_id=1, source_target_pairs={{0,8},{4,12},{8,0},{12,4},{16,24},{20,28},{24,16},{28,20},{1,9},{5... | collective-permute-start | bytes 884744 | tf_op jit(solution)/shard_map/ppermute | solution.py:253
  559.8 19.9 %collective-permute-start.18 = (bf16[320,768]{1,0:T(8,128)(2,1)S(1)}, bf16[320,768]{1,0:T(8,128)(2,1)S(1)}, u32[]{:S(2)}, u32[]{:S(2)}) collective-permute-start(bf16[320,768]{1,0:T(8,128)(2,1)S(1)} %bitcast.437), channel_id=1, source_target_pairs={{0,4},{4,0},{8,12},{12,8},{16,20},{20,16},{24,28},{28,24},{1,5},{5... | collective-permute-start | bytes 1474568 | tf_op jit(solution)/shard_map/ppermute | solution.py:253
  563.3 13.3 %collective-permute-start.39 = (bf16[96,768]{1,0:T(8,128)(2,1)S(1)}, bf16[96,768]{1,0:T(8,128)(2,1)S(1)}, u32[]{:S(2)}, u32[]{:S(2)}) collective-permute-start(bf16[96,768]{1,0:T(8,128)(2,1)S(1)} %dynamic-slice_bitcast_fusion.12), channel_id=1, source_target_pairs={{0,16},{4,20},{8,24},{12,28},{16,0},{20,4},{24,8},{28,12},{1,17},{... | collective-permute-start | bytes 442376 | tf_op jit(solution)/shard_map/ppermute | solution.py:253
  568.6 10.8 %collective-permute-start.31 = (bf16[96,768]{1,0:T(8,128)(2,1)S(1)}, bf16[96,768]{1,0:T(8,128)(2,1)S(1)}, u32[]{:S(2)}, u32[]{:S(2)}) collective-permute-start(bf16[96,768]{1,0:T(8,128)(2,1)S(1)} %dynamic-slice_bitcast_fusion.13), channel_id=1, source_target_pairs={{0,16},{4,20},{8,24},{12,28},{16,0},{20,4},{24,8},{28,12},{1,17},{... | collective-permute-start | bytes 442376 | tf_op jit(solution)/shard_map/ppermute | solution.py:253
  592.1 13.6 %collective-permute-start.42 = (bf16[384,768]{1,0:T(8,128)(2,1)S(1)}, bf16[384,768]{1,0:T(8,128)(2,1)S(1)}, u32[]{:S(2)}, u32[]{:S(2)}) collective-permute-start(bf16[384,768]{1,0:T(8,128)(2,1)S(1)} %bitcast.428), channel_id=1, source_target_pairs={{0,4},{4,0},{8,12},{12,8},{16,20},{20,16},{24,28},{28,24},{1,5},{5... | collective-permute-start | bytes 1769480 | tf_op jit(solution)/shard_map/ppermute | solution.py:253
  595.3 16.8 %collective-permute-start.34 = (bf16[384,768]{1,0:T(8,128)(2,1)S(1)}, bf16[384,768]{1,0:T(8,128)(2,1)S(1)}, u32[]{:S(2)}, u32[]{:S(2)}) collective-permute-start(bf16[384,768]{1,0:T(8,128)(2,1)S(1)} %bitcast.430), channel_id=1, source_target_pairs={{0,4},{4,0},{8,12},{12,8},{16,20},{20,16},{24,28},{28,24},{1,5},{5... | collective-permute-start | bytes 1769480 | tf_op jit(solution)/shard_map/ppermute | solution.py:253
  (86 other events, 1025.2 us)
Sparse Core Ops, SparseCore 0:
  10.3 63.1 all-gather.2

commit v2 on v1

v2 whole, which is shorter than its diff:
```python
import functools
import math

import jax
import jax.numpy as jnp
from jax import lax
from jax.experimental import pallas as pl
from jax.experimental.pallas import tpu as pltpu
from jax.sharding import PartitionSpec as P

HEADS = 12
HEAD_DIM = 64
POOL_HEADS = 2
CLASSES = 14
NDOC = 4

big_negative = -1e30
norm_eps = 1e-05
f32 = jnp.float32
bf16 = jnp.bfloat16
VMEM_LIMIT = 56 * 1024 * 1024
PLAN = [3, 0, 0, 1, 0, 0, 2, 0, 1, 3, 2, 1, 1, 3, 2, 1, 3, 1, 0, 3, 3, 1, 3, 3]


def doc_of(positions, starts_row):
    return jnp.sum((starts_row[None, :] <= positions[:, None]).astype(jnp.int32), axis=1) - 1


def cross_rows(left_mat, right_mat):
    return lax.dot_general(
        left_mat, right_mat, (((0,), (0,)), ((), ())), preferred_element_type=f32
    )


def back_mul(left_mat, right_mat):
    return lax.dot_general(
        left_mat, right_mat, (((1,), (1,)), ((), ())), preferred_element_type=f32
    )


def _half_mask(shape, axis, half):
    return (lax.broadcasted_iota(jnp.int32, shape, axis) // HEAD_DIM) == half


def _split3(row):
    hi = row.astype(bf16)
    rest = row - hi.astype(f32)
    mid = rest.astype(bf16)
    low = (rest - mid.astype(f32)).astype(bf16)
    return hi.astype(f32), mid.astype(f32), low.astype(f32)


def _extra_rows(docrow, row=None):
    at = lax.broadcasted_iota(jnp.int32, (128, docrow.shape[1]), 0)
    out = jnp.where((at < NDOC) & (at != docrow), big_negative, 0.0)
    if row is not None:
        for k, part in enumerate(_split3(row)):
            out = out + jnp.where(at == NDOC + k, part, 0.0)
    return out.astype(bf16)


def project_kernel(
    me_ref, x_ref, all_ref, vec_ref,
    wq0, wq1, wq2, wq3, wk0, wk1, wk2, wk3, wv0, wv1, wv2, wv3,
    q_ref, k_ref, v_ref, all_t_ref, wq_ref, wk_ref, wv_ref, sems,
):
    @pl.when(pl.program_id(0) == 0)
    def _():
        me = me_ref[0]
        copies = fetch_start((wk0, wk1, wk2, wk3), wk_ref, sems, 0, me)
        copies += fetch_start((wv0, wv1, wv2, wv3), wv_ref, sems, 4, me)
        copies += fetch_start((wq0, wq1, wq2, wq3), wq_ref, sems, 8, me)
        fetch_wait(copies)
        query = jnp.dot(x_ref[...], wq_ref[...], preferred_element_type=f32)
        query = (query + vec_ref[pl.ds(VEC_QUERY, 1), :]).astype(bf16).astype(f32)
        q_ref[...] = (query * (1.0 / math.sqrt(HEAD_DIM))).astype(bf16)

    rows = all_ref[...]
    k_ref[...] = jnp.dot(rows, wk_ref[...], preferred_element_type=f32).astype(bf16)
    value = jnp.dot(rows, wv_ref[...], preferred_element_type=f32)
    v_ref[...] = (value + vec_ref[pl.ds(VEC_VALUE, 1), :]).astype(bf16)
    all_t_ref[...] = rows.T


def project(me, x_in, x_all, vecs, wq, wk, wv):
    tok, width = x_in.shape
    seq = x_all.shape[0]
    rows = 256
    whole = lambda v: pl.BlockSpec(v.shape, lambda i: (0, 0), pipeline_mode=pl.Buffered(1))
    block = pl.BlockSpec((rows, width), lambda i: (i, 0))
    shape = jax.ShapeDtypeStruct
    return pl.pallas_call(
        project_kernel,
        grid=(seq // rows,),
        in_specs=[spec(pltpu.SMEM), whole(x_in), block, whole(vecs)] + [spec(pltpu.HBM)] * 12,
        out_specs=[
            pl.BlockSpec((tok, width), lambda i: (0, 0)),
            block,
            block,
            pl.BlockSpec((width, rows), lambda i: (0, i)),
        ],
        out_shape=[
            shape((tok, width), bf16), shape((seq, width), bf16), shape((seq, width), bf16),
            shape((width, seq), bf16),
        ],
        scratch_shapes=[pltpu.VMEM((width, width), bf16)] * 3 + [pltpu.SemaphoreType.DMA((12,))],
        compiler_params=pltpu.CompilerParams(vmem_limit_bytes=VMEM_LIMIT),
        cost_estimate=NO_COST,
        name="project",
    )(me, x_in, x_all, vecs, *wq, *wk, *wv)


def attend_kernel(chunks, q_ref, k_ref, v_ref, extra_ref, doc_ref, attn_ref, low_ref, low_t_ref, lse_ref, s_ref):
    rows = k_ref.shape[0] // chunks
    q_t = q_ref[...].astype(f32).T
    bias = _extra_rows(doc_ref[...])
    outs = []
    for half in range(2):
        q_aug = jnp.concatenate(
            [jnp.where(_half_mask(q_t.shape, 0, half), q_t, 0.0).astype(bf16), bias], axis=0
        )
        top = None
        for c in range(chunks):
            at = pl.ds(c * rows, rows)
            k_aug = jnp.concatenate([k_ref[at, :], extra_ref[at, :]], axis=1)
            s_now = jnp.dot(k_aug, q_aug, preferred_element_type=f32)
            s_ref[half, at, :] = s_now
            top_now = jnp.max(s_now, axis=0, keepdims=True)
            top = top_now if top is None else jnp.maximum(top, top_now)
        total = jnp.zeros_like(top)
        mixed = jnp.zeros((2 * HEAD_DIM, q_t.shape[1]), f32)
        for c in range(chunks):
            at = pl.ds(c * rows, rows)
            p_now = jnp.exp(s_ref[half, at, :] - top)
            total = total + jnp.sum(p_now, axis=0, keepdims=True)
            mixed = mixed + cross_rows(v_ref[at, :], p_now.astype(bf16))
        lse_ref[0, pl.ds(half, 1), :] = top + jnp.log(total)
        outs.append(mixed[half * HEAD_DIM : (half + 1) * HEAD_DIM] / total)
    out_t = jnp.concatenate(outs, axis=0)
    attn_ref[...] = out_t
    low_ref[...] = out_t.T.astype(bf16)
    low_t_ref[...] = out_t.astype(bf16)


def attend(query, keys, values, extra, docs):
    tok, width = query.shape
    seq = keys.shape[0]
    lanes = 2 * HEAD_DIM
    pairs = width // lanes
    shape = jax.ShapeDtypeStruct
    return pl.pallas_call(
        functools.partial(attend_kernel, 4),
        grid=(pairs,),
        in_specs=[
            pl.BlockSpec((tok, lanes), lambda p: (0, p)),
            pl.BlockSpec((seq, lanes), lambda p: (0, p)),
            pl.BlockSpec((seq, lanes), lambda p: (0, p)),
            pl.BlockSpec((seq, lanes), lambda p: (0, 0)),
            pl.BlockSpec((1, tok), lambda p: (0, 0)),
        ],
        out_specs=[
            pl.BlockSpec((lanes, tok), lambda p: (p, 0)),
            pl.BlockSpec((tok, lanes), lambda p: (0, p)),
            pl.BlockSpec((lanes, tok), lambda p: (p, 0)),
            pl.BlockSpec((1, 2, tok), lambda p: (p, 0, 0)),
        ],
        out_shape=[
            shape((width, tok), f32), shape((tok, width), bf16), shape((width, tok), bf16),
            shape((pairs, 2, tok), f32),
        ],
        scratch_shapes=[pltpu.VMEM((2, seq, tok), f32)],
        compiler_params=pltpu.CompilerParams(vmem_limit_bytes=VMEM_LIMIT),
        cost_estimate=NO_COST,
        name="attend",
    )(query, keys, values, extra, docs)


def attend_back_kernel(
    chunks, q_ref, k_ref, v_ref, extra_ref, doc_ref, attn_ref, lse_ref, g_ref, dq_ref, dk_ref, dv_ref
):
    rows = k_ref.shape[0] // chunks
    q_low = q_ref[...]
    g_low = g_ref[...]
    q_t = q_low.astype(f32).T
    g_t = g_low.astype(f32).T
    prod = attn_ref[...] * g_t
    lanes = 2 * HEAD_DIM
    q_side, g_side, q_rows, g_rows = [], [], [], []
    for half in range(2):
        pick = _half_mask(q_t.shape, 0, half)
        delta = jnp.sum(prod[half * HEAD_DIM : (half + 1) * HEAD_DIM], axis=0, keepdims=True)
        q_side.append(
            jnp.concatenate(
                [
                    jnp.where(pick, q_t, 0.0).astype(bf16),
                    _extra_rows(doc_ref[...], -lse_ref[0, pl.ds(half, 1), :]),
                ],
                axis=0,
            )
        )
        g_side.append(
            jnp.concatenate(
                [
                    jnp.where(pick, g_t, 0.0).astype(bf16),
                    _extra_rows(jnp.full_like(doc_ref[...], -1), -delta)
                    * (lax.broadcasted_iota(jnp.int32, (128, q_t.shape[1]), 0) >= NDOC).astype(bf16),
                ],
                axis=0,
            )
        )
        pick_lane = _half_mask(q_low.shape, 1, half)
        q_rows.append(jnp.where(pick_lane, q_low.astype(f32), 0.0).astype(bf16))
        g_rows.append(jnp.where(pick_lane, g_low.astype(f32), 0.0).astype(bf16))
    q_rows = jnp.concatenate(q_rows, axis=0)
    g_rows = jnp.concatenate(g_rows, axis=0)
    dq_t = [jnp.zeros((lanes, q_t.shape[1]), f32) for half in range(2)]
    for c in range(chunks):
        at = pl.ds(c * rows, rows)
        k_now = k_ref[at, :]
        extra = extra_ref[at, :]
        k_aug = jnp.concatenate([k_now, extra], axis=1)
        v_aug = jnp.concatenate([v_ref[at, :], extra], axis=1)
        p_low, s_low = [], []
        for half in range(2):
            prob = jnp.exp(jnp.dot(k_aug, q_side[half], preferred_element_type=f32))
            slope = jnp.dot(v_aug, g_side[half], preferred_element_type=f32)
            p_low.append(prob.astype(bf16))
            s_low.append((prob * slope).astype(bf16))
            dq_t[half] = dq_t[half] + cross_rows(k_now, s_low[half])
        dk_ref[at, :] = jnp.dot(
            jnp.concatenate(s_low, axis=1), q_rows, preferred_element_type=f32
        ).astype(bf16)
        dv_ref[at, :] = jnp.dot(
            jnp.concatenate(p_low, axis=1), g_rows, preferred_element_type=f32
        ).astype(bf16)
    pick = _half_mask(q_t.shape, 0, 0)
    dq_ref[...] = (jnp.where(pick, dq_t[0], dq_t[1]).T * (1.0 / math.sqrt(HEAD_DIM))).astype(bf16)


def attend_back(query, keys, values, extra, docs, attn_t, lse, grad_attn):
    tok, width = query.shape
    seq = keys.shape[0]
    pairs = width // (2 * HEAD_DIM)
    lanes = 2 * HEAD_DIM
    return pl.pallas_call(
        functools.partial(attend_back_kernel, 4),
        grid=(pairs,),
        in_specs=[
            pl.BlockSpec((tok, lanes), lambda p: (0, p)),
            pl.BlockSpec((seq, lanes), lambda p: (0, p)),
            pl.BlockSpec((seq, lanes), lambda p: (0, p)),
            pl.BlockSpec((seq, lanes), lambda p: (0, 0)),
            pl.BlockSpec((1, tok), lambda p: (0, 0)),
            pl.BlockSpec((lanes, tok), lambda p: (p, 0)),
            pl.BlockSpec((1, 2, tok), lambda p: (p, 0, 0)),
            pl.BlockSpec((tok, lanes), lambda p: (0, p)),
        ],
        out_specs=[
            pl.BlockSpec((tok, lanes), lambda p: (0, p)),
            pl.BlockSpec((seq, lanes), lambda p: (0, p)),
            pl.BlockSpec((seq, lanes), lambda p: (0, p)),
        ],
        out_shape=[
            jax.ShapeDtypeStruct((tok, width), bf16),
            jax.ShapeDtypeStruct((seq, width), bf16),
            jax.ShapeDtypeStruct((seq, width), bf16),
        ],
        compiler_params=pltpu.CompilerParams(vmem_limit_bytes=VMEM_LIMIT),
        cost_estimate=NO_COST,
        name="attend_back",
    )(query, keys, values, extra, docs, attn_t, lse, grad_attn)


VEC_QUERY, VEC_VALUE, VEC_OUT, VEC_GAIN1, VEC_BIAS1, VEC_DOWN, VEC_GAIN2, VEC_BIAS2, VEC_UP = range(9)
VEC_POOL, VEC_CLASS = 12, 15
NO_COST = pl.CostEstimate(flops=0, transcendentals=0, bytes_accessed=0)


def spec(space=pltpu.VMEM):
    return pl.BlockSpec(memory_space=space)


def fetch_start(pieces, target, sems, first, me):
    rows = pieces[0].shape[0]
    copies = []
    for r, piece in enumerate(pieces):
        at = pl.multiple_of((me ^ r) * rows, rows)
        copy = pltpu.make_async_copy(piece, target.at[pl.ds(at, rows), :], sems.at[first + r])
        copy.start()
        copies.append(copy)
    return copies


def fetch_wait(copies):
    for copy in copies:
        copy.wait()


def norm_parts(field):
    centre = field - jnp.mean(field, axis=-1, keepdims=True)
    inv_std = lax.rsqrt(jnp.mean(centre * centre, axis=-1, keepdims=True) + norm_eps)
    return centre * inv_std, inv_std


def norm_back(grad_in, normed, inv_std, gain_row):
    scaled = grad_in * gain_row
    return inv_std * (
        scaled
        - jnp.mean(scaled, axis=-1, keepdims=True)
        - normed * jnp.mean(scaled * normed, axis=-1, keepdims=True)
    )


def column_sum(value):
    return jnp.sum(value.astype(f32), axis=0, keepdims=True)


def student_tables(mats):
    width_part = mats.shape[1] - 64
    ws = jnp.concatenate([mats[k, :width_part] for k in range(mats.shape[0])], axis=0)
    wp = jnp.concatenate([mats[k, width_part : width_part + 32] for k in range(mats.shape[0])], axis=0)
    wc = jnp.concatenate([mats[k, width_part + 32 :] for k in range(mats.shape[0])], axis=0)
    return ws, wp, wc


def halves_sum(value):
    lane = lax.broadcasted_iota(jnp.int32, value.shape, 1)
    half = value.shape[1] // POOL_HEADS
    low = jnp.sum(jnp.where(lane < half, value, 0.0), axis=1, keepdims=True)
    high = jnp.sum(jnp.where(lane < half, 0.0, value), axis=1, keepdims=True)
    return jnp.where(lane < half, low, high)


def of_docs(doc, rows):
    out = jnp.where(doc == 0, rows[0], 0.0)
    for k in range(1, NDOC):
        out = jnp.where(doc == k, rows[k], out)
    return out


def forward_kernel(
    me_ref, attn_ref, x_ref, vec_ref, mats_ref, doc_ref,
    wo0, wo1, wo2, wo3, wu0, wu1, wu2, wu3, wd0, wd1, wd2, wd3,
    hid_t_ref, normed1_ref, inv1_ref, act_ref, slope_ref,
    out_ref, normed2_ref, inv2_ref, student_ref, score_ref, part_ref,
    wo_ref, wu_ref, wd_ref, sems,
):
    me = me_ref[0]
    go_o = fetch_start((wo0, wo1, wo2, wo3), wo_ref, sems, 0, me)
    go_u = fetch_start((wu0, wu1, wu2, wu3), wu_ref, sems, 4, me)
    go_d = fetch_start((wd0, wd1, wd2, wd3), wd_ref, sems, 8, me)
    vec = lambda k: vec_ref[pl.ds(k, 1), :]
    fetch_wait(go_o)
    branch = jnp.dot(attn_ref[...], wo_ref[...], preferred_element_type=f32) + vec(VEC_OUT)
    normed, inv_std = norm_parts(x_ref[...].astype(f32) + branch)
    normed1_ref[...] = normed
    inv1_ref[...] = inv_std
    hidden = normed * vec(VEC_GAIN1) + vec(VEC_BIAS1)
    hid_t_ref[...] = hidden.T.astype(bf16)
    hid_low = hidden.astype(bf16)
    width = hidden.shape[1]
    fetch_wait(go_u)
    down = None
    for j in range(wu_ref.shape[1] // width):
        at = pl.ds(j * width, width)
        pre = jnp.dot(hid_low, wu_ref[:, at], preferred_element_type=f32) + vec(VEC_UP + j)
        cdf = 0.5 * (1.0 + lax.erf(pre * (1.0 / math.sqrt(2.0))))
        pdf = jnp.exp(-0.5 * pre * pre) * (1.0 / math.sqrt(2.0 * math.pi))
        slope_ref[:, at] = (cdf + pre * pdf).astype(bf16)
        act = (pre * cdf).astype(bf16)
        act_ref[:, at] = act
        if j == 0:
            fetch_wait(go_d)
        term = jnp.dot(act, wd_ref[at, :], preferred_element_type=f32)
        down = term if down is None else down + term
    normed, inv_std = norm_parts(hidden + (down + vec(VEC_DOWN)))
    normed2_ref[...] = normed
    inv2_ref[...] = inv_std
    out_low = (normed * vec(VEC_GAIN2) + vec(VEC_BIAS2)).astype(bf16)
    out_ref[...] = out_low
    ws, _, _ = student_tables(mats_ref[...])
    pool = ws.shape[1]
    student = jnp.dot(out_low, ws, preferred_element_type=f32) + vec(VEC_POOL)[:, :pool]
    student_ref[...] = student
    scale = 1.0 / math.sqrt(pool // POOL_HEADS)
    score = halves_sum(student * vec(VEC_POOL + 1)[:, :pool]) * scale
    score_ref[...] = score
    doc = doc_ref[...]
    tops = [
        jnp.max(jnp.where(doc == k, score, big_negative), axis=0, keepdims=True) for k in range(NDOC)
    ]
    weight = jnp.exp(score - of_docs(doc, tops))
    mixed = weight * student
    totals = [jnp.sum(jnp.where(doc == k, weight, 0.0), axis=0, keepdims=True) for k in range(NDOC)]
    sums = [jnp.sum(jnp.where(doc == k, mixed, 0.0), axis=0, keepdims=True) for k in range(NDOC)]
    part_ref[...] = jnp.concatenate(tops + totals + sums + [jnp.zeros((4, pool), f32)], axis=0)


def layer_forward_call(me, attn, x_in, vecs, mats, doc, wo, wu, wd):
    tok, width = x_in.shape
    hidden = wu[0].shape[1]
    pool = mats.shape[2]
    shape = jax.ShapeDtypeStruct
    return pl.pallas_call(
        forward_kernel,
        in_specs=[spec(pltpu.SMEM)] + [spec()] * 5 + [spec(pltpu.HBM)] * 12,
        out_specs=[spec()] * 11,
        out_shape=[
            shape((width, tok), bf16), shape((tok, width), f32), shape((tok, 1), f32),
            shape((tok, hidden), bf16), shape((tok, hidden), bf16),
            shape((tok, width), bf16), shape((tok, width), f32), shape((tok, 1), f32),
            shape((tok, pool), f32), shape((tok, pool), f32), shape((16, pool), f32),
        ],
        scratch_shapes=[
            pltpu.VMEM((width, width), bf16), pltpu.VMEM((width, hidden), bf16),
            pltpu.VMEM((hidden, width), bf16), pltpu.SemaphoreType.DMA((12,)),
        ],
        compiler_params=pltpu.CompilerParams(vmem_limit_bytes=VMEM_LIMIT),
        cost_estimate=NO_COST,
        name="layer_forward",
    )(me, attn, x_in, vecs, mats, doc, *wo, *wu, *wd)


def exact_dot(left, right, dims):
    return lax.dot_general(
        left, right, (dims, ((), ())), precision=lax.Precision.HIGHEST, preferred_element_type=f32
    )


def head_kernel(
    label_ref, owner_ref, parts_ref, vec_ref, mats_ref, doc_ref, student_ref, score_ref, out_ref, cot_ref,
    normed2_ref, inv2_ref,
    down_ref, res2_ref, logits_ref, vec_grad_ref, tables_ref,
):
    vec = lambda k: vec_ref[pl.ds(k, 1), :]
    ws, wp, wc = student_tables(mats_ref[...])
    pool = ws.shape[1]
    wp, wc = wp.astype(f32), wc.astype(f32)
    tops = jnp.max(parts_ref[:, 0:NDOC, :], axis=0)
    factor = jnp.exp(parts_ref[:, 0:NDOC, :] - tops[None])
    totals = jnp.sum(parts_ref[:, NDOC : 2 * NDOC, :] * factor, axis=0)
    pooled = jnp.sum(parts_ref[:, 2 * NDOC : 3 * NDOC, :] * factor, axis=0) / totals
    pooled = jnp.concatenate([pooled, jnp.zeros((8 - NDOC, pool), f32)], axis=0)
    act = jnp.tanh(exact_dot(pooled, wp, ((1,), (0,))) + vec(VEC_POOL + 2)[:, :pool])
    logits = exact_dot(act, wc, ((1,), (0,))) + vec(VEC_CLASS)[:, :pool]
    logits_ref[...] = logits
    lane = lax.broadcasted_iota(jnp.int32, logits.shape, 1)
    row = lax.broadcasted_iota(jnp.int32, logits.shape, 0)
    shown = jnp.where(lane < CLASSES, logits, big_negative)
    shown = jnp.exp(shown - jnp.max(shown, axis=1, keepdims=True))
    grad_logits = shown / jnp.sum(shown, axis=1, keepdims=True)
    for k in range(NDOC):
        grad_logits = grad_logits - jnp.where((row == k) & (lane == label_ref[0, k]), 1.0, 0.0)
    grad_logits = jnp.where(row < NDOC, grad_logits, 0.0)
    owner = (owner_ref[0] == 0).astype(f32)
    grad_wc = exact_dot(act, grad_logits, ((0,), (0,))) * owner
    grad_pre = exact_dot(grad_logits, wc, ((1,), (1,))) * (1.0 - act * act)
    grad_wp = exact_dot(pooled, grad_pre, ((0,), (0,))) * owner
    grad_pooled = exact_dot(grad_pre, wp, ((1,), (1,)))
    doc = doc_ref[...]
    student = student_ref[...]
    each = lambda table: [table[k : k + 1] for k in range(NDOC)]
    weight = jnp.exp(score_ref[...] - of_docs(doc, each(tops))) / of_docs(doc, each(totals))
    tok_grad = of_docs(doc, each(grad_pooled))
    grad_score = weight * halves_sum(tok_grad * (student - of_docs(doc, each(pooled))))
    scale = 1.0 / math.sqrt(pool // POOL_HEADS)
    grad_student = weight * tok_grad + grad_score * vec(VEC_POOL + 1)[:, :pool] * scale
    grad_low = grad_student.astype(bf16)
    out_low = out_ref[...]
    grad_ws = cross_rows(out_low, grad_low)
    blocks, rows = mats_ref.shape[0], mats_ref.shape[1]
    high = rows - 64
    for k in range(blocks):
        tables_ref[k, 0:high, :] = grad_ws[k * high : (k + 1) * high]
        tables_ref[k, high : high + 32, :] = grad_wp[32 * k : 32 * k + 32]
        tables_ref[k, high + 32 : high + 64, :] = grad_wc[32 * k : 32 * k + 32]
    grad_layer = cot_ref[...].astype(f32) + back_mul(grad_low, ws)
    normed = normed2_ref[...]
    grad_res = norm_back(grad_layer, normed, inv2_ref[...], vec(VEC_GAIN2))
    res2_ref[...] = grad_res
    low = grad_res.astype(bf16)
    down_ref[...] = low
    width = normed.shape[1]
    wide = lambda v: jnp.concatenate([v, jnp.zeros((1, width - pool), f32)], axis=1)
    rows = [
        column_sum(low),
        column_sum(grad_layer * normed),
        column_sum(grad_layer),
        wide(column_sum(grad_low)),
        wide(column_sum(grad_score * student) * scale),
        wide(column_sum(grad_pre) * owner),
        wide(column_sum(grad_logits) * owner),
        jnp.zeros((1, width), f32),
    ]
    vec_grad_ref[...] = jnp.concatenate(rows, axis=0)


def head_call(labels, owner, parts, vecs, mats, doc, student, score, out_low, cot, normed2, inv2):
    tok, width = out_low.shape
    shape = jax.ShapeDtypeStruct
    return pl.pallas_call(
        head_kernel,
        in_specs=[spec(pltpu.SMEM)] * 2 + [spec()] * 10,
        out_specs=[spec()] * 5,
        out_shape=[
            shape((tok, width), bf16), shape((tok, width), f32), shape((8, mats.shape[2]), f32),
            shape((8, width), f32), shape(mats.shape, f32),
        ],
        compiler_params=pltpu.CompilerParams(vmem_limit_bytes=VMEM_LIMIT),
        cost_estimate=NO_COST,
        name="head",
    )(labels, owner, parts, vecs, mats, doc, student, score, out_low, cot, normed2, inv2)


def backward_kernel(
    me_ref, low_ref, res2_ref, slope_ref, normed1_ref, inv1_ref, vec_ref,
    wo0, wo1, wo2, wo3, wu0, wu1, wu2, wu3, wd0, wd1, wd2, wd3,
    up_ref, res1_ref, branch_ref, attn_ref, vec_grad_ref,
    wo_ref, wu_ref, wd_ref, sems,
):
    me = me_ref[0]
    go_d = fetch_start((wd0, wd1, wd2, wd3), wd_ref, sems, 8, me)
    go_u = fetch_start((wu0, wu1, wu2, wu3), wu_ref, sems, 4, me)
    go_o = fetch_start((wo0, wo1, wo2, wo3), wo_ref, sems, 0, me)
    low = low_ref[...]
    width = low.shape[1]
    fetch_wait(go_d)
    total = res2_ref[...]
    rows = []
    for j in range(wu_ref.shape[1] // width):
        at = pl.ds(j * width, width)
        up = (back_mul(low, wd_ref[at, :]) * slope_ref[:, at].astype(f32)).astype(bf16)
        up_ref[:, at] = up
        rows.append(column_sum(up))
        if j == 0:
            fetch_wait(go_u)
        total = total + back_mul(up, wu_ref[:, at])
    normed = normed1_ref[...]
    rows += [column_sum(total * normed), column_sum(total)]
    grad_res = norm_back(total, normed, inv1_ref[...], vec_ref[pl.ds(VEC_GAIN1, 1), :])
    res1_ref[...] = grad_res
    branch = grad_res.astype(bf16)
    branch_ref[...] = branch
    rows += [column_sum(branch), jnp.zeros((1, width), f32)]
    vec_grad_ref[...] = jnp.concatenate(rows, axis=0)
    fetch_wait(go_o)
    attn_ref[...] = back_mul(branch, wo_ref[...]).astype(bf16)


def layer_backward_call(me, low, res2, slope, normed1, inv1, vecs, wo, wu, wd):
    tok, width = low.shape
    hidden = wu[0].shape[1]
    shape = jax.ShapeDtypeStruct
    return pl.pallas_call(
        backward_kernel,
        in_specs=[spec(pltpu.SMEM)] + [spec()] * 6 + [spec(pltpu.HBM)] * 12,
        out_specs=[spec()] * 5,
        out_shape=[
            shape((tok, hidden), bf16), shape((tok, width), f32), shape((tok, width), bf16),
            shape((tok, width), bf16), shape((8, width), f32),
        ],
        scratch_shapes=[
            pltpu.VMEM((width, width), bf16), pltpu.VMEM((width, hidden), bf16),
            pltpu.VMEM((hidden, width), bf16), pltpu.SemaphoreType.DMA((12,)),
        ],
        compiler_params=pltpu.CompilerParams(vmem_limit_bytes=VMEM_LIMIT),
        cost_estimate=NO_COST,
        name="layer_backward",
    )(me, low, res2, slope, normed1, inv1, vecs, *wo, *wu, *wd)


def down_grad_kernel(order_ref, act_ref, grad_ref, send_ref, keep_ref):
    term = cross_rows(act_ref[...], grad_ref[...]).astype(bf16)
    half = send_ref.shape[0]

    @pl.when(pl.program_id(0) < pl.num_programs(0) // 2)
    def _():
        send_ref[0] = term

    @pl.when(pl.program_id(0) >= pl.num_programs(0) // 2)
    def _():
        keep_ref[0] = term


def send_keep_specs(block):
    nd = len(block)
    zero = (0,) * (nd - 1)
    return [
        pl.BlockSpec(block, lambda i, s: (jnp.minimum(i, 1),) + zero),
        pl.BlockSpec(block, lambda i, s: (jnp.maximum(i - 2, 0),) + zero),
    ]


def down_grad(blocks, act, grad):
    tok, hidden = act.shape
    width = grad.shape[1]
    part = hidden // 4
    shape = jax.ShapeDtypeStruct((2, part, width), bf16)
    return pl.pallas_call(
        down_grad_kernel,
        grid_spec=pltpu.PrefetchScalarGridSpec(
            num_scalar_prefetch=1,
            grid=(4,),
            in_specs=[
                pl.BlockSpec((tok, part), lambda i, s: (0, s[i])),
                pl.BlockSpec((tok, width), lambda i, s: (0, 0)),
            ],
            out_specs=send_keep_specs((1, part, width)),
        ),
        out_shape=[shape, shape],
        compiler_params=pltpu.CompilerParams(vmem_limit_bytes=VMEM_LIMIT),
        cost_estimate=NO_COST,
        name="down_grad",
    )(blocks, act, grad)


def middle_grad_kernel(order_ref, hid_ref, up_ref, attn_ref, branch_ref, tables_ref, vec_a_ref, vec_b_ref, send_ref, keep_ref):
    part = attn_ref.shape[0]
    width = branch_ref.shape[1]
    pool = tables_ref.shape[2]
    half = width // 2

    def put(out):
        base = 0
        for j in range(up_ref.shape[1] // width):
            out[0, base : base + part, :] = jnp.dot(
                hid_ref[...], up_ref[:, j * width : (j + 1) * width], preferred_element_type=f32
            ).astype(bf16)
            base += part
        out[0, base : base + part, :] = jnp.dot(
            attn_ref[...], branch_ref[...], preferred_element_type=f32
        ).astype(bf16)
        base += part
        high = tables_ref.shape[1] - 64
        step = high * pool // width
        out[0, base : base + step, :] = jnp.concatenate(
            [tables_ref[0, k * step : (k + 1) * step, :] for k in range(width // pool)], axis=1
        ).astype(bf16)
        rows = jnp.concatenate([vec_a_ref[...], vec_b_ref[...]], axis=0)
        rows = jnp.concatenate([rows[:, :half], rows[:, half:]], axis=0)
        out[0, base + step : base + step + 32, :] = jnp.concatenate(
            [
                tables_ref[0, high : high + 32, :],
                tables_ref[0, high + 32 : high + 64, :],
                rows,
                jnp.zeros((32, width - 2 * pool - half), f32),
            ],
            axis=1,
        ).astype(bf16)

    pl.when(pl.program_id(0) < 2)(lambda: put(send_ref))
    pl.when(pl.program_id(0) >= 2)(lambda: put(keep_ref))


def middle_grad(blocks, hid_t, up, attn_t, branch, tables, vec_a, vec_b):
    width, tok = attn_t.shape
    part = width // 4
    hidden = up.shape[1]
    rows = hidden // 4 + part + 64
    shape = jax.ShapeDtypeStruct((2, rows, width), bf16)
    return pl.pallas_call(
        middle_grad_kernel,
        grid_spec=pltpu.PrefetchScalarGridSpec(
            num_scalar_prefetch=1,
            grid=(4,),
            in_specs=[
                pl.BlockSpec((part, tok), lambda i, s: (s[i], 0)),
                pl.BlockSpec((tok, hidden), lambda i, s: (0, 0)),
                pl.BlockSpec((part, tok), lambda i, s: (s[i], 0)),
                pl.BlockSpec((tok, width), lambda i, s: (0, 0)),
                pl.BlockSpec((1,) + tables.shape[1:], lambda i, s: (s[i], 0, 0)),
                pl.BlockSpec(vec_a.shape, lambda i, s: (0, 0)),
                pl.BlockSpec(vec_b.shape, lambda i, s: (0, 0)),
            ],
            out_specs=send_keep_specs((1, rows, width)),
        ),
        out_shape=[shape, shape],
        compiler_params=pltpu.CompilerParams(vmem_limit_bytes=VMEM_LIMIT),
        cost_estimate=NO_COST,
        name="middle_grad",
    )(blocks, hid_t, up, attn_t, branch, tables, vec_a, vec_b)


def last_grad_kernel(order_ref, xt_ref, xt_all_ref, dq_ref, dk_ref, dv_ref, send_ref, keep_ref):
    part = xt_ref.shape[0]

    def put(out):
        for k, (left, right) in enumerate(((xt_ref, dq_ref), (xt_all_ref, dk_ref), (xt_all_ref, dv_ref))):
            out[0, k * part : (k + 1) * part, :] = jnp.dot(
                left[...], right[...], preferred_element_type=f32
            ).astype(bf16)
        width = dq_ref.shape[1]
        rows = jnp.concatenate(
            [column_sum(dq_ref[...]), column_sum(dv_ref[...]), jnp.zeros((62, width), f32)], axis=0
        )
        out[0, 3 * part :, :] = rows.astype(bf16)

    pl.when(pl.program_id(0) < 2)(lambda: put(send_ref))
    pl.when(pl.program_id(0) >= 2)(lambda: put(keep_ref))


def last_grad(blocks, position, x_all_t, dq, dk, dv):
    tok = dq.shape[0]
    width, seq = x_all_t.shape
    part = width // 4
    rows = 3 * part + 64
    shape = jax.ShapeDtypeStruct((2, rows, width), bf16)
    whole = lambda r: pl.BlockSpec((r, width), lambda i, s: (0, 0), pipeline_mode=pl.Buffered(1))
    return pl.pallas_call(
        last_grad_kernel,
        grid_spec=pltpu.PrefetchScalarGridSpec(
            num_scalar_prefetch=1,
            grid=(4,),
            in_specs=[
                pl.BlockSpec((part, tok), lambda i, s: (s[i], s[4])),
                pl.BlockSpec((part, seq), lambda i, s: (s[i], 0)),
                whole(tok),
                whole(seq),
                whole(seq),
            ],
            out_specs=send_keep_specs((1, rows, width)),
        ),
        out_shape=[shape, shape],
        compiler_params=pltpu.CompilerParams(vmem_limit_bytes=VMEM_LIMIT),
        cost_estimate=NO_COST,
        name="last_grad",
    )(jnp.concatenate([blocks, position]), x_all_t, x_all_t, dq, dk, dv)


def others_kernel(
    order_ref, me_ref, dk_ref, dv_ref, wk0, wk1, wk2, wk3, wv0, wv1, wv2, wv3,
    send_ref, keep_ref, wk_ref, wv_ref, sems,
):
    @pl.when(pl.program_id(0) == 0)
    def _():
        copies = fetch_start((wk0, wk1, wk2, wk3), wk_ref, sems, 0, me_ref[0])
        copies += fetch_start((wv0, wv1, wv2, wv3), wv_ref, sems, 4, me_ref[0])
        fetch_wait(copies)

    term = (back_mul(dk_ref[...], wk_ref[...]) + back_mul(dv_ref[...], wv_ref[...])).astype(bf16)
    half = pl.num_programs(0) // 2

    @pl.when(pl.program_id(0) < half)
    def _():
        send_ref[0] = term

    @pl.when(pl.program_id(0) >= half)
    def _():
        keep_ref[0] = term


def others_call(mine, me, dk, dv, wk, wv, rows):
    seq, width = dk.shape
    half = seq // rows // 2
    at = jnp.arange(half, dtype=jnp.int32)
    order = jnp.concatenate([2 * at + 1 - mine, 2 * at + mine]).astype(jnp.int32)
    block = pl.BlockSpec((rows, width), lambda i, s: (s[i], 0))
    shape = jax.ShapeDtypeStruct((half, rows, width), bf16)
    return pl.pallas_call(
        others_kernel,
        grid_spec=pltpu.PrefetchScalarGridSpec(
            num_scalar_prefetch=1,
            grid=(2 * half,),
            in_specs=[spec(pltpu.SMEM), block, block] + [spec(pltpu.HBM)] * 8,
            out_specs=[
                pl.BlockSpec((1, rows, width), lambda i, s: (jnp.minimum(i, half - 1), 0, 0)),
                pl.BlockSpec((1, rows, width), lambda i, s: (jnp.maximum(i - half, 0), 0, 0)),
            ],
            scratch_shapes=[
                pltpu.VMEM((width, width), bf16), pltpu.VMEM((width, width), bf16), pltpu.SemaphoreType.DMA((8,)),
            ],
        ),
        out_shape=[shape, shape],
        compiler_params=pltpu.CompilerParams(vmem_limit_bytes=VMEM_LIMIT),
        cost_estimate=NO_COST,
        name="others",
    )(order, me, dk, dv, *wk, *wv)


def pack_kernel(me_ref, *refs):
    vectors, (up_ref, bs_ref, qp_ref, bp_ref, bc_ref), out_ref = refs[:8], refs[8:13], refs[13]
    part = vectors[0].shape[1]
    small = bs_ref.shape[1]
    width = out_ref.shape[1]
    out_ref[...] = jnp.zeros(out_ref.shape, f32)
    for k in range(width // part):

        @pl.when(me_ref[0] == k)
        def _():
            for row, ref in enumerate(vectors):
                out_ref[row : row + 1, k * part : (k + 1) * part] = ref[...].astype(f32)
            out_ref[VEC_UP + k : VEC_UP + k + 1, :] = up_ref[...].astype(f32)
            for row, ref in enumerate((bs_ref, qp_ref, bp_ref)):
                out_ref[VEC_POOL + row : VEC_POOL + row + 1, k * small : (k + 1) * small] = ref[...].astype(f32)
            if k == 0:
                out_ref[VEC_CLASS : VEC_CLASS + 1, 0:CLASSES] = bc_ref[...].astype(f32)


def pack_call(me, vectors, up, pools, classes, width):
    operands = [v.reshape(1, -1) for v in vectors + [up] + pools + [classes]]
    return pl.pallas_call(
        pack_kernel,
        in_specs=[spec(pltpu.SMEM)] + [spec()] * len(operands),
        out_specs=spec(),
        out_shape=jax.ShapeDtypeStruct((16, width), f32),
        cost_estimate=NO_COST,
        name="pack",
    )(me, *operands)


def swap(value, axis, bit):
    count = lax.axis_size(axis)
    return lax.ppermute(value, axis, [(i, i ^ bit) for i in range(count)])


def join_far(shard):
    return double(shard, "fsdp", 2)


def join_core(column):
    core = lax.axis_index("fsdp") % 2
    across = swap(column, "fsdp", 1)
    full = jnp.where(
        core == 0, jnp.stack([column, across], axis=1), jnp.stack([across, column], axis=1)
    )
    return full.reshape(-1, column.shape[-1])


def bits_of(axis):
    return [1 << k for k in range(lax.axis_size(axis).bit_length() - 1)]


def tie(*values):
    return lax.optimization_barrier(values)


class Box:
    def __init__(self, keep):
        self.keep = keep


class Order:
    def __init__(self, holder):
        self.holder = holder

    def after(self, value):
        value, self.holder.keep = tie(value, self.holder.keep)
        return value

    def pin(self, value):
        box = Box(self.after(value))
        self.holder = box
        return box


class Sum:
    def __init__(self, keep, send, steps):
        self.keep, self.send, self.todo = keep, send, steps

    @staticmethod
    def mine(step):
        index = lax.axis_index(step[1])
        out = 0
        for k, bit in enumerate(step[2]):
            out = out + ((index // bit) % 2) * (1 << k)
        return out

    @staticmethod
    def shift(step, r):
        return sum(bit for k, bit in enumerate(step[2]) if (r >> k) & 1)

    def begin(self):
        step = self.todo[0]
        self.got = [swap(v, step[1], self.shift(step, r + 1)) for r, v in enumerate(self.send)]

    def end(self, order):
        step = self.todo.pop(0)
        got = list(self.got)
        got[-1] = order.after(got[-1])
        order.holder = self
        n = self.keep.shape[-1]
        if step[0] == "gather":
            mine = self.mine(step)
            rows = self.keep.shape[0]
            out = jnp.zeros(((len(got) + 1) * rows, n), bf16)
            for r, v in enumerate([self.keep] + got):
                out = lax.dynamic_update_slice_in_dim(out, v, (mine ^ r) * rows, axis=0)
            self.keep = out
        else:
            parts = [self.keep] + got

            def total(pick):
                out = pick(parts[0]).astype(f32)
                for v in parts[1:]:
                    out = out + pick(v).astype(f32)
                return out.astype(bf16)

            following = self.todo[0] if self.todo else None
            if following is not None and following[0] == "scatter":
                mine = self.mine(following)
                ways, rows = 1 << len(following[2]), following[3]

                def piece(r):
                    return lambda v: lax.dynamic_index_in_dim(
                        v.reshape(-1, ways, rows, n), mine ^ r, 1, keepdims=False
                    )

                self.send = [total(piece(r)) for r in range(1, ways)]
                self.keep = total(piece(0))
                return
            self.keep = total(lambda v: v.reshape(-1, n))
        if self.todo:
            self.send = [self.keep] * ((1 << len(self.todo[0][2])) - 1)

    def step(self, order):
        self.end(order)
        if self.todo:
            self.begin()


def bits_of(axis):
    return [1 << k for k in range(lax.axis_size(axis).bit_length() - 1)]


def double(value, axis, bit):
    mine = (lax.axis_index(axis) // bit) % 2
    got = swap(value, axis, bit)
    return jnp.where(mine == 0, jnp.stack([value, got]), jnp.stack([got, value]))


def rounds_of(axis):
    return [(bit,) for bit in bits_of(axis)]


def grad_steps(rows):
    steps = [("scatter", "fsdp", (1,), rows), ("scatter", "fsdp", (2,), rows)]
    for bits in rounds_of("ctx"):
        rows >>= len(bits)
        steps.append(("scatter", "ctx", bits, rows))
    return steps + [("gather", "ctx", bits, 0) for bits in rounds_of("ctx")[::-1]]


def shards(
    tokens,
    starts,
    labels,
    cotangent,
    w_query,
    b_query,
    w_key,
    w_value,
    b_value,
    w_out,
    b_out,
    norm1_gain,
    norm1_bias,
    w_up,
    b_up,
    w_down,
    b_down,
    norm2_gain,
    norm2_bias,
    w_student,
    b_student,
    pool_query,
    w_pool,
    b_pool,
    w_class,
    b_class,
):
    cycle_size = lax.axis_size("ctx")
    cycle_index = lax.axis_index("ctx")
    fsdp_size = lax.axis_size("fsdp")
    me = lax.axis_index("fsdp")
    me_row = me.reshape(1).astype(jnp.int32)
    tok_rows = tokens.shape[1]
    width = tokens.shape[2]
    part = width // fsdp_size
    hidden_part = b_up.shape[0]
    pool_width = w_pool.shape[1]
    seq_total = tok_rows * cycle_size
    score_scale = 1.0 / math.sqrt(HEAD_DIM)
    starts_row = starts[0]
    x_in = tokens[0]
    x_all = lax.all_gather(x_in, "ctx", axis=0, tiled=True)

    def pieces(shard, far):
        return [shard, swap(shard, "fsdp", 1), far, swap(far, "fsdp", 1)]

    far_wk, far_wv, far_wq = swap(w_key, "fsdp", 2), swap(w_value, "fsdp", 2), swap(w_query, "fsdp", 2)
    mats = jnp.concatenate([w_student, w_pool, jnp.pad(w_class, ((0, 0), (0, pool_width - CLASSES)))], axis=0)
    vectors = [b_query, b_value, b_out, norm1_gain, norm1_bias, b_down, norm2_gain, norm2_bias]
    vecs = pack_call(me_row, vectors, b_up, [b_student, pool_query, b_pool], b_class, width)
    far_vecs, mats = swap(vecs, "fsdp", 2), join_far(mats)
    far_wk, far_wv, far_wq, far_vecs, mats, w_out, w_up = tie(
        far_wk, far_wv, far_wq, far_vecs, mats, w_out, w_up
    )
    vecs = vecs + far_vecs
    vecs = vecs + swap(vecs, "fsdp", 1)
    far_wo, far_w1 = swap(w_out, "fsdp", 2), swap(w_up, "fsdp", 2)
    piece_wk, piece_wv, piece_wq = pieces(w_key, far_wk), pieces(w_value, far_wv), pieces(w_query, far_wq)
    mats = join_core(mats).reshape(fsdp_size, -1, pool_width)
    x_all, far_wo, far_w1, mats, w_down = tie(x_all, far_wo, far_w1, mats, w_down)
    far_w2 = swap(w_down, "fsdp", 2)
    piece_wo, piece_w1 = pieces(w_out, far_wo), pieces(w_up, far_w1)

    local_pos = cycle_index * tok_rows + jnp.arange(tok_rows, dtype=jnp.int32)
    local_doc = doc_of(local_pos, starts_row)
    all_doc = doc_of(jnp.arange(seq_total, dtype=jnp.int32), starts_row)
    at = jnp.arange(128, dtype=jnp.int32)[None, :]
    extra = ((at == all_doc[:, None]) | ((at >= NDOC) & (at < NDOC + 3))).astype(bf16)
    docs = local_doc[None, :]
    doc_column = local_doc[:, None]

    query_s, key_b, value_b, x_all_t = project(me_row, x_in, x_all, vecs, piece_wq, piece_wk, piece_wv)
    attn_t, attn_b, attn_low_t, lse = attend(query_s, key_b, value_b, extra, docs)
    attn_b, far_w2 = tie(attn_b, far_w2)
    piece_w2 = pieces(w_down, far_w2)

    hid_t, normed1, inv1, act, slope, out_b, normed2, inv2, student, score, local = layer_forward_call(
        me_row, attn_b, x_in, vecs, mats, doc_column, piece_wo, piece_w1, piece_w2
    )
    parts = lax.all_to_all(
        jnp.broadcast_to(local[None], (cycle_size,) + local.shape), "ctx", 0, 0, tiled=True
    )
    owner = cycle_index.reshape(1).astype(jnp.int32)
    grad_down_b, grad_res2, logits, vec_a, tables = head_call(
        labels, owner, parts, vecs, mats, doc_column, student, score, out_b, cotangent[0], normed2, inv2
    )
    logits = logits[:NDOC, :CLASSES]

    core = me % 2
    blocks = jnp.stack([1 - core, 3 - core, core, 2 + core]).astype(jnp.int32)

    def grad_sum(pair):
        return Sum(pair[1], [pair[0]], grad_steps(pair[0].shape[1]))

    sum_w2 = grad_sum(down_grad(blocks, act, grad_down_b))
    sum_w2.begin()
    grad_up_b, grad_res1, grad_branch_b, grad_attn_b, vec_b = layer_backward_call(
        me_row, grad_down_b, grad_res2, slope, normed1, inv1, vecs, piece_wo, piece_w1, piece_w2
    )
    order = Order(Box(grad_attn_b))
    attn_box = order.holder
    sum_w2.step(order)
    sum_mid = grad_sum(
        middle_grad(blocks, hid_t, grad_up_b, attn_low_t, grad_branch_b, tables, vec_a, vec_b)
    )
    sum_mid.begin()
    grad_attn_b = order.after(attn_box.keep)
    grad_query_b, grad_key_b, grad_value_b = attend_back(
        query_s, key_b, value_b, extra, docs, attn_t, lse, grad_attn_b
    )
    key_box = order.pin(grad_key_b)
    sum_mid.step(order)
    sum_w2.step(order)
    grad_query_b = order.after(grad_query_b)
    send, keep = last_grad(blocks, cycle_index.reshape(1), x_all_t, grad_query_b, key_box.keep, grad_value_b)
    sum_last = Sum(keep, [send], grad_steps(send.shape[1]))
    sum_last.keep = order.after(sum_last.keep)
    order.holder = sum_last
    sum_last.begin()
    grad_value_b = order.after(grad_value_b)
    send, keep = others_call(
        cycle_index % 2, me_row, key_box.keep, grad_value_b, piece_wk, piece_wv, tok_rows
    )
    sum_others = Sum(keep, [send], [("scatter", "ctx", bits, tok_rows) for bits in rounds_of("ctx")])
    sum_others.keep = order.after(sum_others.keep)
    order.holder = sum_others
    sum_others.begin()
    waves = [sum_w2, sum_mid, sum_others, sum_last]
    plan = PLAN if cycle_size == 8 else []
    for k in plan:
        if waves[k].todo:
            waves[k].step(order)
    while any(w.todo for w in waves):
        for w in waves:
            if w.todo:
                w.step(order)

    near = jnp.concatenate([back_mul(grad_query_b, w)[None] for w in piece_wq])
    near = jnp.concatenate([lax.dynamic_index_in_dim(near, me ^ r, 0, keepdims=False) for r in range(fsdp_size)], axis=1)
    grad_tokens = grad_res1 + near
    grad_tokens = grad_tokens + sum_others.keep.reshape(tok_rows, width).astype(f32)
    middle = sum_mid.keep.astype(f32)
    ups_sum, middle = middle[:hidden_part], middle[hidden_part:]
    last = sum_last.keep.astype(f32)
    done_wo = middle[:part]
    high = part * pool_width // width
    tall = middle[part : part + high]
    done_ws = jnp.concatenate(jnp.split(tall, width // pool_width, axis=1), axis=0)
    rest = middle[part + high :]
    done_wp = rest[:, :pool_width]
    done_wc = rest[:, pool_width : pool_width + CLASSES]
    base = 2 * pool_width
    half = width // 2
    rows = jnp.concatenate([rest[:16, base : base + half], rest[16:, base : base + half]], axis=1)
    own = lax.dynamic_slice_in_dim(rows, me * part, part, axis=1)
    pools = lax.dynamic_slice_in_dim(rows[3:6], me * w_pool.shape[0], w_pool.shape[0], axis=1)
    done_bc = rows[6, :CLASSES]
    done_c1 = lax.dynamic_index_in_dim(rows, 8 + me, 0, keepdims=False)
    late = lax.dynamic_slice_in_dim(last[3 * part : 3 * part + 8], me * part, part, axis=1)
    done_w1 = jnp.concatenate(jnp.split(ups_sum, hidden_part // part, axis=0), axis=1)
    return (
        out_b[None],
        logits[None],
        grad_tokens[None],
        last[:part],
        late[0],
        last[part : 2 * part],
        last[2 * part : 3 * part],
        late[1],
        done_wo,
        own[14],
        own[12],
        own[13],
        done_w1,
        done_c1,
        sum_w2.keep.astype(f32),
        own[0],
        own[1],
        own[2],
        done_ws,
        pools[0],
        pools[1],
        done_wp,
        pools[2],
        done_wc,
        done_bc,
    )


def solution(mesh):
    in_specs = (
        P("fsdp", "ctx", None),
        P("fsdp", None),
        P("fsdp", None),
        P("fsdp", "ctx", None),
        P("fsdp", None),
        P("fsdp"),
        P("fsdp", None),
        P("fsdp", None),
        P("fsdp"),
        P("fsdp", None),
        P("fsdp"),
        P("fsdp"),
        P("fsdp"),
        P("fsdp", None),
        P("fsdp"),
        P("fsdp", None),
        P("fsdp"),
        P("fsdp"),
        P("fsdp"),
        P("fsdp", None),
        P("fsdp"),
        P("fsdp"),
        P("fsdp", None),
        P("fsdp"),
        P("fsdp", None),
        P(),
    )
    out_specs = (
        P("fsdp", "ctx", None),
        P("fsdp", None, None),
        P("fsdp", "ctx", None),
        P("fsdp", None),
        P("fsdp"),
        P("fsdp", None),
        P("fsdp", None),
        P("fsdp"),
        P("fsdp", None),
        P("fsdp"),
        P("fsdp"),
        P("fsdp"),
        P("fsdp", None),
        P("fsdp"),
        P("fsdp", None),
        P("fsdp"),
        P("fsdp"),
        P("fsdp"),
        P("fsdp", None),
        P("fsdp"),
        P("fsdp"),
        P("fsdp", None),
        P("fsdp"),
        P("fsdp", None),
        P(),
    )
    return jax.shard_map(shards, mesh=mesh, in_specs=in_specs, out_specs=out_specs, check_vma=False)
```

time: 634 us -> 398 us (0.63); the launches traced: 622 us -> 396 us
  local copies, waits for them, and re-layouts: 168 us -> 28 us
  Pallas kernels: 39.1 us -> 118 us
  matrix products: 65.3 us -> 3.1 us
  waiting for transfers between devices: 214 us -> 158 us
  other arithmetic: 89.4 us -> 35.8 us
  starting transfers between devices: 29.6 us -> 38.2 us
    unnamed x231 -> x55, local copies, waits for them, and re-layouts: 85.9 us -> 5.09 us
    pallas_call x0 -> x9, Pallas kernels: none -> 79.2 us  [the longest x1 13.1 us: last_grad(): pl.pallas_call(last_grad_kernel, grid_spec=pltpu.PrefetchScalarGridSpec(n...]
    ppermute x43 -> x49, waiting for transfers between devices: 208 us -> 147 us  [swap(): return lax.ppermute(value, axis, [(i, i ^ bit) for i in range(count)])]
    dot_general x22 -> x0, matrix products: 48.6 us -> none  [the longest x7 12.9 us: cross_rows(): lax.dot_general(left_mat, right_mat, (((0,), (0,)), ((), ())), preferred_...]
    select_n x12 -> x1, other arithmetic: 31.3 us -> 1.14 us  [join_core(): jnp.where(core == 0, jnp.stack([column, across], axis=1), jnp.stack([acro...]
    pad x49 -> x0, local copies, waits for them, and re-layouts: 26.5 us -> none  [the longest x26 17 us: pack(): cells = [jnp.pad(v, (0, half_room - part)) for v in vectors]]
    reduce_sum x16 -> x0, other arithmetic: 18.6 us -> none  [the longest x3 3.18 us: pick_rows(): jnp.sum(jnp.where(onehot_bool[:, :, None], table[None, :, :], 0.0), axis=1)]
    dot_general x7 -> x4, matrix products: 16.7 us -> 3.1 us  [back_mul(): lax.dot_general(left_mat, right_mat, (((1,), (1,)), ((), ())), preferred_...]
  transfers between devices with their start and end apart: 45 -> 51, of which waited for: 28 -> 25; matrix products, arithmetic and copies ran while one was open for 21% -> 14% of each run, Pallas kernels for 0% -> 21%
where the time goes in v2:
time: 398 us; the launch traced here: 396 us
  waiting for transfers between devices  158 us (40%)
  Pallas kernels  118 us (30%)
  starting transfers between devices  38.2 us (10%)
  other arithmetic  35.8 us (9%)
  local copies, waits for them, and re-layouts  28 us (7%)
  between operations  14.8 us (4%)
    ppermute x49, waiting for transfers between devices, swap(): return lax.ppermute(value, axis, [(i, i ^ bit) for i in range(count)])  147 us
    ppermute x49, starting transfers between devices, swap(): return lax.ppermute(value, axis, [(i, i ^ bit) for i in range(count)])  34.7 us
    pallas_call x1, Pallas kernels, attend_back(): pl.pallas_call(functools.partial(attend_back_kernel, 4), grid=(pairs,), i...  23.9 us
    convert_element_type x18, other arithmetic, total(): return out.astype(bf16)  22.5 us
    pallas_call x1, Pallas kernels, attend(): pl.pallas_call(functools.partial(attend_kernel, 4), grid=(pairs,), in_spe...  15.2 us
    pallas_call x1, Pallas kernels, last_grad(): pl.pallas_call(last_grad_kernel, grid_spec=pltpu.PrefetchScalarGridSpec(n...  13.1 us
    pallas_call x1, Pallas kernels, others_call(): pl.pallas_call(others_kernel, grid_spec=pltpu.PrefetchScalarGridSpec(num_...  12.8 us
    pallas_call x1, Pallas kernels, project(): pl.pallas_call(project_kernel, grid=(seq // rows,), in_specs=[spec(pltpu....  12.5 us
  transfers between devices with their start and end apart: 51, of which 25 were waited for; matrix products, arithmetic and copies ran while one was open for 14% of the time, Pallas kernels for 21%

profile of v2, /device:TPU:0, one launch (start us, length us, event | category | flops | bytes accessed | tf_op | source)
XLA Modules:
  0.0 396.2 jit_solution(16697552686185216938)
XLA Ops:
  29.3 3.5 collective-permute-done.4
  40.7 28.0 %collective-permute-done.5.wo2 = bf16[192,768]{1,0:T(8,128)(2,1)} collective-permute-done((bf16[192,768]{1,0:T(8,128)(2,1)}, bf16[192,768]{1,0:T(8,128)(2,1)}, u32[]{:S(2)}, u32[]{:S(2)}) %collective-permute-start.5) | collective-permute-done | bytes 294944 | tf_op jit(solution)/shard_map/ppermute | solution.py:813
  68.7 4.7 %all-gather.3.cloned.1.call-done = bf16[1,2048,768]{2,1,0:T(8,128)(2,1)} async-done(((bf16[1,256,768]{2,1,0:T(8,128)(2,1)}), bf16[1,2048,768]{2,1,0:T(8,128)(2,1)}) %all-gather.3.cloned.1.call-update) | async-done | bytes 3145744 | tf_op jit(solution)/shard_map/all_gather | solution.py:985
  81.2 12.5 %project.1 = (bf16[256,768]{1,0:T(8,128)(2,1)}, bf16[2048,768]{1,0:T(8,128)(2,1)}, bf16[2048,768]{1,0:T(8,128)(2,1)}, bf16[768,2048]{1,0:T(8,128)(2,1)}) custom-call(s32[1]{0:T(128)} %bitcast.me_ref, bf16[256,768]{1,0:T(8,128)(2,1)} %bitcast.142, bf16[2048,768]{1,0:T(8,128)(2,1)} %bitcast.144, f32[16,768]{1,0:T(8,128)} %add.546.vec_ref, ...), custom_call_target="tpu_custom_call" | custom-call | tf_op jit(solution)/shard_map/project/pallas_call | solution.py:92
  93.8 15.2 %attend.1 = (f32[768,256]{1,0:T(8,128)}, bf16[256,768]{1,0:T(8,128)(2,1)}, bf16[768,256]{1,0:T(8,128)(2,1)}, f32[6,2,256]{2,1,0:T(2,128)}) custom-call(bf16[256,768]{1,0:T(8,128)(2,1)} %get-tuple-element.153.q_ref, bf16[2048,768]{1,0:T(8,128)(2,1)} %get-tuple-element.154.k_ref, bf16[2048,768]{1,0:T(8,128)(2,1)} %get-tuple-element.155.v_ref, ...), custom_call_target="tpu_custom_call" | custom-call | tf_op jit(solution)/shard_map/attend/pallas_call | solution.py:151
  115.0 10.1 %layer_forward.1 = (bf16[768,256]{1,0:T(8,128)(2,1)}, f32[256,768]{1,0:T(8,128)}, f32[256,1]{1,0:T(8,128)}, bf16[256,3072]{1,0:T(8,128)(2,1)}, bf16[256,3072]{1,...) custom-call(s32[1]{0:T(128)} %bitcast.me_ref, ...), custom_call_target="tpu_custom_call" | custom-call | tf_op jit(solution)/shard_map/layer_forward/pallas_call | solution.py:404
  126.4 3.5 all-to-all-start
  130.5 6.1 %all-to-all-done.parts_ref = f32[8,16,128]{2,1,0:T(8,128)S(1)} async-done(((f32[8,16,128]{2,1,0:T(8,128)}), f32[8,16,128]{2,1,0:T(8,128)S(1)}, u32[]{:S(2)}, u32[]{:S(2)}) %all-to-all-start) | async-done | bytes 65568 | tf_op jit(solution)/shard_map/all_to_all | solution.py:1023
  137.2 5.0 %head.1 = (bf16[256,768]{1,0:T(8,128)(2,1)}, f32[256,768]{1,0:T(8,128)}, f32[8,128]{1,0:T(8,128)}, f32[8,768]{1,0:T(8,128)}, f32[4,256,128]{2,1,0:T(8,128)}) custom-call(s32[1,4]{1,0:T(1,128)} %label_ref.1, s32[1]{0:T(128)} %bitcast.16.owner_ref, f32[8,16,128]{2,1,0:T(8,128)} %copy-done.18, f32[16,768]{1,0:T(8,128)} %add.546.vec_ref, ...), custom_call_target="tpu_custom_call" | custom-call | tf_op jit(solution)/shard_map/head/pallas_call | solution.py:501
  142.2 6.5 %down_grad.1 = (bf16[2,768,768]{2,1,0:T(8,128)(2,1)}, bf16[2,768,768]{2,1,0:T(8,128)(2,1)}) custom-call(s32[4]{0:T(128)} %pad_add_fusion.order_ref, bf16[256,3072]{1,0:T(8,128)(2,1)} %get-tuple-element.178.act_ref, bf16[256,768]{1,0:T(8,128)(2,1)} %get-tuple-element.170.low_ref.grad_ref), custom_call_target="tpu_custom_call" | custom-call | tf_op jit(solution)/shard_map/down_grad/pallas_call | solution.py:599
  148.8 10.2 %layer_backward.1 = (bf16[256,3072]{1,0:T(8,128)(2,1)}, f32[256,768]{1,0:T(8,128)}, bf16[256,768]{1,0:T(8,128)(2,1)}, bf16[256,768]{1,0:T(8,128)(2,1)}, f32[8,768]{1,0:T(8,128)}) custom-call(s32[1]{0:T(128)} %bitcast.me_ref, bf16[256,768]{1,0:T(8,128)(2,1)} %get-tuple-element.170.low_ref.grad_ref, f32[256,768]{1,0:T(8,128)} %get-tuple-element.171.res2_ref, ...), custom_call_target="tpu_custom_call" | custom-call | tf_op jit(solution)/shard_map/layer_backward/pallas_call | solution.py:554
  159.0 7.5 %middle_grad.1 = (bf16[2,1024,768]{2,1,0:T(8,128)(2,1)}, bf16[2,1024,768]{2,1,0:T(8,128)(2,1)}) custom-call(s32[4]{0:T(128)} %pad_add_fusion.order_ref, bf16[768,256]{1,0:T(8,128)(2,1)} %get-tuple-element.189.hid_ref, bf16[256,3072]{1,0:T(8,128)(2,1)} %get-tuple-element.190.up_ref, bf16[768,256]{1,0:T(8,128)(2,1)} %get-tuple-element.191.attn_ref, ...), custom_call_target="tpu_custom_call" | custom-call | tf_op jit(solution)/shard_map/middle_grad/pallas_call | solution.py:661
  167.0 3.9 add_convert_fusion.2
  172.1 23.9 %attend_back.1 = (bf16[256,768]{1,0:T(8,128)(2,1)}, bf16[2048,768]{1,0:T(8,128)(2,1)}, bf16[2048,768]{1,0:T(8,128)(2,1)}) custom-call(bf16[256,768]{1,0:T(8,128)(2,1)} %get-tuple-element.153.q_ref, bf16[2048,768]{1,0:T(8,128)(2,1)} %get-tuple-element.154.k_ref, bf16[2048,768]{1,0:T(8,128)(2,1)} %get-tuple-element.155.v_ref, ...), custom_call_target="tpu_custom_call" | custom-call | tf_op jit(solution)/shard_map/attend_back/pallas_call | solution.py:245
  196.0 3.8 add_convert_fusion
  202.2 13.1 %last_grad.1 = (bf16[2,640,768]{2,1,0:T(8,128)(2,1)}, bf16[2,640,768]{2,1,0:T(8,128)(2,1)}) custom-call(s32[5]{0:T(128)} %concatenate.29.order_ref, bf16[768,2048]{1,0:T(8,128)(2,1)} %get-tuple-element.204.xt_ref.xt_all_ref, bf16[768,2048]{1,0:T(8,128)(2,1)} %get-tuple-element.204.xt_ref.xt_all_ref, bf16[256,768]{1,0:T(8,128)(2,1)} %get-tuple-element.201.dq_ref, ...), custom_call_target="tpu_custom_call" | custom-call | tf_op jit(solution)/shard_map/last_grad/pallas_call | solution.py:709
  217.8 12.8 %others.1 = (bf16[4,256,768]{2,1,0:T(8,128)(2,1)}, bf16[4,256,768]{2,1,0:T(8,128)(2,1)}) custom-call(s32[8]{0:T(128)} %pad_add_fusion.1.order_ref, s32[1]{0:T(128)} %bitcast.me_ref, bf16[2048,768]{1,0:T(8,128)(2,1)} %get-tuple-element.202.dk_ref, bf16[2048,768]{1,0:T(8,128)(2,1)} %get-tuple-element.208.dv_ref, bf16[192,768]{1,0:T(8,128)(2,1)} %wk0.3, ...), custom_call_target="tpu_custom_call" | custom-call | tf_op jit(solution)/shard_map/others/pallas_call | solution.py:759
  237.4 8.5 %collective-permute-done.28 = bf16[1,192,768]{2,1,0:T(8,128)(2,1)S(1)} collective-permute-done((bf16[1,192,768]{2,1,0:T(8,128)(2,1)}, bf16[1,192,768]{2,1,0:T(8,128)(2,1)S(1)}, u32[]{:S(2)}, u32[]{:S(2)}) %collective-permute-start.28) | collective-permute-done | bytes 294944 | tf_op jit(solution)/shard_map/ppermute | solution.py:813
  247.0 5.4 %collective-permute-done.30 = bf16[1,1024,768]{2,1,0:T(8,128)(2,1)} collective-permute-done((bf16[1,1024,768]{2,1,0:T(8,128)(2,1)}, bf16[1,1024,768]{2,1,0:T(8,128)(2,1)}, u32[]{:S(2)}, u32[]{:S(2)}) %collective-permute-start.30) | collective-permute-done | bytes 1572896 | tf_op jit(solution)/shard_map/ppermute | solution.py:813
  254.7 6.8 %collective-permute-done.29 = bf16[1,96,768]{2,1,0:T(8,128)(2,1)S(1)} collective-permute-done((bf16[1,96,768]{2,1,0:T(8,128)(2,1)S(1)}, bf16[1,96,768]{2,1,0:T(8,128)(2,1)S(1)}, u32[]{:S(2)}, u32[]{:S(2)}) %collective-permute-start.29) | collective-permute-done | bytes 147488 | tf_op jit(solution)/shard_map/ppermute | solution.py:813
  273.3 5.6 %collective-permute-done.34 = bf16[192,768]{1,0:T(8,128)(2,1)S(1)} collective-permute-done((bf16[192,768]{1,0:T(8,128)(2,1)S(1)}, bf16[192,768]{1,0:T(8,128)(2,1)S(1)}, u32[]{:S(2)}, u32[]{:S(2)}) %collective-permute-start.34) | collective-permute-done | bytes 294944 | tf_op jit(solution)/shard_map/ppermute | solution.py:813
  278.9 4.9 %collective-permute-done.31 = bf16[1,512,768]{2,1,0:T(8,128)(2,1)S(1)} collective-permute-done((bf16[1,512,768]{2,1,0:T(8,128)(2,1)S(1)}, bf16[1,512,768]{2,1,0:T(8,128)(2,1)S(1)}, u32[]{:S(2)}, u32[]{:S(2)}) %collective-permute-start.31) | collective-permute-done | bytes 786464 | tf_op jit(solution)/shard_map/ppermute | solution.py:813
  289.3 6.5 %collective-permute-done.36 = bf16[2,256,768]{2,1,0:T(8,128)(2,1)S(1)} collective-permute-done((bf16[2,256,768]{2,1,0:T(8,128)(2,1)S(1)}, bf16[2,256,768]{2,1,0:T(8,128)(2,1)S(1)}, u32[]{:S(2)}, u32[]{:S(2)}) %collective-permute-start.36) | collective-permute-done | bytes 786464 | tf_op jit(solution)/shard_map/ppermute | solution.py:813
  296.0 7.0 %collective-permute-done.35 = bf16[1,256,768]{2,1,0:T(8,128)(2,1)S(1)} collective-permute-done((bf16[1,256,768]{2,1,0:T(8,128)(2,1)S(1)}, bf16[1,256,768]{2,1,0:T(8,128)(2,1)S(1)}, u32[]{:S(2)}, u32[]{:S(2)}) %collective-permute-start.35) | collective-permute-done | bytes 393248 | tf_op jit(solution)/shard_map/ppermute | solution.py:813
  308.9 13.5 %collective-permute-done.37 = bf16[1,128,768]{2,1,0:T(8,128)(2,1)S(1)} collective-permute-done((bf16[1,128,768]{2,1,0:T(8,128)(2,1)S(1)}, bf16[1,128,768]{2,1,0:T(8,128)(2,1)S(1)}, u32[]{:S(2)}, u32[]{:S(2)}) %collective-permute-start.37) | collective-permute-done | bytes 196640 | tf_op jit(solution)/shard_map/ppermute | solution.py:813
  325.4 9.8 %collective-permute-done.39 = bf16[1,256,768]{2,1,0:T(8,128)(2,1)S(1)} collective-permute-done((bf16[1,256,768]{2,1,0:T(8,128)(2,1)S(1)}, bf16[1,256,768]{2,1,0:T(8,128)(2,1)S(1)}, u32[]{:S(2)}, u32[]{:S(2)}) %collective-permute-start.39) | collective-permute-done | bytes 393248 | tf_op jit(solution)/shard_map/ppermute | solution.py:813
  335.3 4.0 %collective-permute-done.38 = bf16[128,768]{1,0:T(8,128)(2,1)S(1)} collective-permute-done((bf16[128,768]{1,0:T(8,128)(2,1)S(1)}, bf16[128,768]{1,0:T(8,128)(2,1)S(1)}, u32[]{:S(2)}, u32[]{:S(2)}) %collective-permute-start.38) | collective-permute-done | bytes 196640 | tf_op jit(solution)/shard_map/ppermute | solution.py:813
  340.1 3.6 collective-permute-done.41
  345.0 9.0 %collective-permute-done.42 = bf16[256,768]{1,0:T(8,128)(2,1)} collective-permute-done((bf16[256,768]{1,0:T(8,128)(2,1)S(1)}, bf16[256,768]{1,0:T(8,128)(2,1)}, u32[]{:S(2)}, u32[]{:S(2)}) %collective-permute-start.42) | collective-permute-done | bytes 393248 | tf_op jit(solution)/shard_map/ppermute | solution.py:813
  358.8 3.8 collective-permute-done.46
  363.0 10.8 %collective-permute-done.43 = bf16[512,768]{1,0:T(8,128)(2,1)S(1)} collective-permute-done((bf16[512,768]{1,0:T(8,128)(2,1)S(1)}, bf16[512,768]{1,0:T(8,128)(2,1)S(1)}, u32[]{:S(2)}, u32[]{:S(2)}) %collective-permute-start.43) | collective-permute-done | bytes 786464 | tf_op jit(solution)/shard_map/ppermute | solution.py:813
  381.4 5.8 %collective-permute-done.48 = bf16[320,768]{1,0:T(8,128)(2,1)S(1)} collective-permute-done((bf16[320,768]{1,0:T(8,128)(2,1)S(1)}, bf16[320,768]{1,0:T(8,128)(2,1)S(1)}, u32[]{:S(2)}, u32[]{:S(2)}) %collective-permute-start.48) | collective-permute-done | bytes 491552 | tf_op jit(solution)/shard_map/ppermute | solution.py:813
  (239 shorter events, 106.1 us)
Async XLA Ops:
  7.2 66.2 %all-gather.3.cloned.1.call-start = ((), (), s32[]{:S(2)}) async-start(), calls=%async_computation.1 | async-start | bytes 3538944 | tf_op jit(solution)/shard_map/all_gather | solution.py:985
  8.0 25.5 %collective-permute-start = (bf16[192,768]{1,0:T(8,128)(2,1)}, bf16[192,768]{1,0:T(8,128)(2,1)S(1)}, u32[]{:S(2)}, u32[]{:S(2)}) collective-permute-start(bf16[192,768]{1,0:T(8,128)(2,1)} %wk0.3), channel_id=1, source_target_pairs={{0,2},{1,3},{2,0},{3,1},{4,6},{5,7},{6,4},{7,5},{8,10},{9,11},{10,... | collective-permute-start | bytes 884744 | tf_op jit(solution)/shard_map/ppermute | solution.py:813
  11.0 22.5 %collective-permute-start.1 = (bf16[192,768]{1,0:T(8,128)(2,1)}, bf16[192,768]{1,0:T(8,128)(2,1)S(1)}, u32[]{:S(2)}, u32[]{:S(2)}) collective-permute-start(bf16[192,768]{1,0:T(8,128)(2,1)} %wv0.3), channel_id=1, source_target_pairs={{0,2},{1,3},{2,0},{3,1},{4,6},{5,7},{6,4},{7,5},{8,10},{9,11},{10,... | collective-permute-start | bytes 884744 | tf_op jit(solution)/shard_map/ppermute | solution.py:813
  11.1 23.9 %collective-permute-start.2 = (bf16[192,768]{1,0:T(8,128)(2,1)}, bf16[192,768]{1,0:T(8,128)(2,1)}, u32[]{:S(2)}, u32[]{:S(2)}) collective-permute-start(bf16[192,768]{1,0:T(8,128)(2,1)} %wq0.1), channel_id=1, source_target_pairs={{0,2},{1,3},{2,0},{3,1},{4,6},{5,7},{6,4},{7,5},{8,10},{9,11},{10,... | collective-permute-start | bytes 884744 | tf_op jit(solution)/shard_map/ppermute | solution.py:813
  14.6 18.1 %collective-permute-start.4 = (bf16[256,128]{1,0:T(8,128)(2,1)S(1)}, bf16[256,128]{1,0:T(8,128)(2,1)S(1)}, u32[]{:S(2)}, u32[]{:S(2)}) collective-permute-start(bf16[256,128]{1,0:T(8,128)(2,1)S(1)} %get-tuple-element.408), channel_id=1, source_target_pairs={{0,2},{1,3},{2,0},{3,1},{4,6},{5,7},{6,4},{7,5},{8,10},{9,11},{10,... | collective-permute-start | bytes 196616 | tf_op jit(solution)/shard_map/ppermute | solution.py:813
  34.9 33.8 %collective-permute-start.6 = (bf16[192,3072]{1,0:T(8,128)(2,1)}, bf16[192,3072]{1,0:T(8,128)(2,1)S(1)}, u32[]{:S(2)}, u32[]{:S(2)}) collective-permute-start(bf16[192,3072]{1,0:T(8,128)(2,1)} %wu0.1), channel_id=1, source_target_pairs={{0,2},{1,3},{2,0},{3,1},{4,6},{5,7},{6,4},{7,5},{8,10},{9,11},{10,... | collective-permute-start | bytes 3538952 | tf_op jit(solution)/shard_map/ppermute | solution.py:813
  36.7 32.0 %collective-permute-start.5 = (bf16[192,768]{1,0:T(8,128)(2,1)}, bf16[192,768]{1,0:T(8,128)(2,1)}, u32[]{:S(2)}, u32[]{:S(2)}) collective-permute-start(bf16[192,768]{1,0:T(8,128)(2,1)} %wo0.1), channel_id=1, source_target_pairs={{0,2},{1,3},{2,0},{3,1},{4,6},{5,7},{6,4},{7,5},{8,10},{9,11},{10,... | collective-permute-start | bytes 884744 | tf_op jit(solution)/shard_map/ppermute | solution.py:813
  37.0 39.9 %collective-permute-start.9 = (bf16[192,768]{1,0:T(8,128)(2,1)}, bf16[192,768]{1,0:T(8,128)(2,1)}, u32[]{:S(2)}, u32[]{:S(2)}) collective-permute-start(bf16[192,768]{1,0:T(8,128)(2,1)} %wq0.1), channel_id=1, source_target_pairs={{0,1},{1,0},{2,3},{3,2},{4,5},{5,4},{6,7},{7,6},{8,9},{9,8},{10,11... | collective-permute-start | bytes 884744 | tf_op jit(solution)/shard_map/ppermute | solution.py:813
  37.5 39.9 %collective-permute-start.11 = (bf16[192,768]{1,0:T(8,128)(2,1)}, bf16[192,768]{1,0:T(8,128)(2,1)}, u32[]{:S(2)}, u32[]{:S(2)}) collective-permute-start(bf16[192,768]{1,0:T(8,128)(2,1)} %wk0.3), channel_id=1, source_target_pairs={{0,1},{1,0},{2,3},{3,2},{4,5},{5,4},{6,7},{7,6},{8,9},{9,8},{10,11... | collective-permute-start | bytes 884744 | tf_op jit(solution)/shard_map/ppermute | solution.py:813
  38.7 40.9 %collective-permute-start.13 = (bf16[192,768]{1,0:T(8,128)(2,1)}, bf16[192,768]{1,0:T(8,128)(2,1)}, u32[]{:S(2)}, u32[]{:S(2)}) collective-permute-start(bf16[192,768]{1,0:T(8,128)(2,1)} %wv0.3), channel_id=1, source_target_pairs={{0,1},{1,0},{2,3},{3,2},{4,5},{5,4},{6,7},{7,6},{8,9},{9,8},{10,11... | collective-permute-start | bytes 884744 | tf_op jit(solution)/shard_map/ppermute | solution.py:813
  73.4 35.6 %collective-permute-start.15 = (bf16[768,768]{1,0:T(8,128)(2,1)}, bf16[768,768]{1,0:T(8,128)(2,1)}, u32[]{:S(2)}, u32[]{:S(2)}) collective-permute-start(bf16[768,768]{1,0:T(8,128)(2,1)} %wd0.1), channel_id=1, source_target_pairs={{0,2},{1,3},{2,0},{3,1},{4,6},{5,7},{6,4},{7,5},{8,10},{9,11},{10,... | collective-permute-start | bytes 3538952 | tf_op jit(solution)/shard_map/ppermute | solution.py:813
  79.6 34.5 %collective-permute-start.18 = (bf16[192,3072]{1,0:T(8,128)(2,1)S(1)}, bf16[192,3072]{1,0:T(8,128)(2,1)}, u32[]{:S(2)}, u32[]{:S(2)}) collective-permute-start(bf16[192,3072]{1,0:T(8,128)(2,1)S(1)} %copy-done.1), channel_id=1, source_target_pairs={{0,1},{1,0},{2,3},{3,2},{4,5},{5,4},{6,7},{7,6},{8,9},{9,8},{10,11... | collective-permute-start | bytes 3538952 | tf_op jit(solution)/shard_map/ppermute | solution.py:813
  79.9 35.1 %collective-permute-start.20 = (bf16[768,768]{1,0:T(8,128)(2,1)S(1)}, bf16[768,768]{1,0:T(8,128)(2,1)}, u32[]{:S(2)}, u32[]{:S(2)}) collective-permute-start(bf16[768,768]{1,0:T(8,128)(2,1)S(1)} %copy-done.2), channel_id=1, source_target_pairs={{0,1},{1,0},{2,3},{3,2},{4,5},{5,4},{6,7},{7,6},{8,9},{9,8},{10,11... | collective-permute-start | bytes 3538952 | tf_op jit(solution)/shard_map/ppermute | solution.py:813
  80.1 34.8 %collective-permute-start.19 = (bf16[192,3072]{1,0:T(8,128)(2,1)S(1)}, bf16[192,3072]{1,0:T(8,128)(2,1)}, u32[]{:S(2)}, u32[]{:S(2)}) collective-permute-start(bf16[192,3072]{1,0:T(8,128)(2,1)S(1)} %collective-permute-done.6.wu2), channel_id=1, source_target_pairs={{0,1},{1,0},{2,3},{3,2},{4,5},{5,4},{6,7},{7,6},{8,9},{9,8},{10,11... | collective-permute-start | bytes 3538952 | tf_op jit(solution)/shard_map/ppermute | solution.py:813
  148.8 18.3 %collective-permute-start.22 = (bf16[2,768,768]{2,1,0:T(8,128)(2,1)}, bf16[2,768,768]{2,1,0:T(8,128)(2,1)}, u32[]{:S(2)}, u32[]{:S(2)}) collective-permute-start(bf16[2,768,768]{2,1,0:T(8,128)(2,1)} %get-tuple-element.179), channel_id=1, source_target_pairs={{0,1},{1,0},{2,3},{3,2},{4,5},{5,4},{6,7},{7,6},{8,9},{9,8},{10,11... | collective-permute-start | bytes 7077896 | tf_op jit(solution)/shard_map/ppermute | solution.py:813
  166.5 29.5 %collective-permute-start.24 = (bf16[2,1024,768]{2,1,0:T(8,128)(2,1)}, bf16[2,1024,768]{2,1,0:T(8,128)(2,1)}, u32[]{:S(2)}, u32[]{:S(2)}) collective-permute-start(bf16[2,1024,768]{2,1,0:T(8,128)(2,1)} %get-tuple-element.197), channel_id=1, source_target_pairs={{0,1},{1,0},{2,3},{3,2},{4,5},{5,4},{6,7},{7,6},{8,9},{9,8},{10,11... | collective-permute-start | bytes 9437192 | tf_op jit(solution)/shard_map/ppermute | solution.py:813
  170.9 28.9 %collective-permute-start.23 = (bf16[1,768,768]{2,1,0:T(8,128)(2,1)}, bf16[1,768,768]{2,1,0:T(8,128)(2,1)}, u32[]{:S(2)}, u32[]{:S(2)}) collective-permute-start(bf16[1,768,768]{2,1,0:T(8,128)(2,1)} %get-tuple-element.367), channel_id=1, source_target_pairs={{0,2},{1,3},{2,0},{3,1},{4,6},{5,7},{6,4},{7,5},{8,10},{9,11},{10,... | collective-permute-start | bytes 3538952 | tf_op jit(solution)/shard_map/ppermute | solution.py:813
  215.3 17.0 %collective-permute-start.25 = (bf16[2,640,768]{2,1,0:T(8,128)(2,1)}, bf16[2,640,768]{2,1,0:T(8,128)(2,1)}, u32[]{:S(2)}, u32[]{:S(2)}) collective-permute-start(bf16[2,640,768]{2,1,0:T(8,128)(2,1)} %get-tuple-element.212), channel_id=1, source_target_pairs={{0,1},{1,0},{2,3},{3,2},{4,5},{5,4},{6,7},{7,6},{8,9},{9,8},{10,11... | collective-permute-start | bytes 5898248 | tf_op jit(solution)/shard_map/ppermute | solution.py:813
  215.3 37.1 %collective-permute-start.30 = (bf16[1,1024,768]{2,1,0:T(8,128)(2,1)}, bf16[1,1024,768]{2,1,0:T(8,128)(2,1)}, u32[]{:S(2)}, u32[]{:S(2)}) collective-permute-start(bf16[1,1024,768]{2,1,0:T(8,128)(2,1)} %get-tuple-element.365), channel_id=1, source_target_pairs={{0,2},{1,3},{2,0},{3,1},{4,6},{5,7},{6,4},{7,5},{8,10},{9,11},{10,... | collective-permute-start | bytes 4718600 | tf_op jit(solution)/shard_map/ppermute | solution.py:813
  216.8 18.4 %collective-permute-start.27 = (bf16[1,384,768]{2,1,0:T(8,128)(2,1)}, bf16[1,384,768]{2,1,0:T(8,128)(2,1)}, u32[]{:S(2)}, u32[]{:S(2)}) collective-permute-start(bf16[1,384,768]{2,1,0:T(8,128)(2,1)} %get-tuple-element.375), channel_id=1, source_target_pairs={{0,4},{4,0},{8,12},{12,8},{16,20},{20,16},{24,28},{28,24},{1,5},{5... | collective-permute-start | bytes 1769480 | tf_op jit(solution)/shard_map/ppermute | solution.py:813
  230.6 38.5 %collective-permute-start.32 = (bf16[4,256,768]{2,1,0:T(8,128)(2,1)}, bf16[4,256,768]{2,1,0:T(8,128)(2,1)}, u32[]{:S(2)}, u32[]{:S(2)}) collective-permute-start(bf16[4,256,768]{2,1,0:T(8,128)(2,1)} %get-tuple-element.222), channel_id=1, source_target_pairs={{0,4},{4,0},{8,12},{12,8},{16,20},{20,16},{24,28},{28,24},{1,5},{5... | collective-permute-start | bytes 4718600 | tf_op jit(solution)/shard_map/ppermute | solution.py:813
  262.2 21.7 %collective-permute-start.31 = (bf16[1,512,768]{2,1,0:T(8,128)(2,1)S(1)}, bf16[1,512,768]{2,1,0:T(8,128)(2,1)S(1)}, u32[]{:S(2)}, u32[]{:S(2)}) collective-permute-start(bf16[1,512,768]{2,1,0:T(8,128)(2,1)S(1)} %get-tuple-element.374), channel_id=1, source_target_pairs={{0,4},{4,0},{8,12},{12,8},{16,20},{20,16},{24,28},{28,24},{1,5},{5... | collective-permute-start | bytes 2359304 | tf_op jit(solution)/shard_map/ppermute | solution.py:813
  264.2 23.2 %collective-permute-start.26 = (bf16[1,640,768]{2,1,0:T(8,128)(2,1)S(1)}, bf16[1,640,768]{2,1,0:T(8,128)(2,1)S(1)}, u32[]{:S(2)}, u32[]{:S(2)}) collective-permute-start(bf16[1,640,768]{2,1,0:T(8,128)(2,1)S(1)} %copy-done.16), channel_id=1, source_target_pairs={{0,2},{1,3},{2,0},{3,1},{4,6},{5,7},{6,4},{7,5},{8,10},{9,11},{10,... | collective-permute-start | bytes 2949128 | tf_op jit(solution)/shard_map/ppermute | solution.py:813
  270.9 24.9 %collective-permute-start.36 = (bf16[2,256,768]{2,1,0:T(8,128)(2,1)S(1)}, bf16[2,256,768]{2,1,0:T(8,128)(2,1)S(1)}, u32[]{:S(2)}, u32[]{:S(2)}) collective-permute-start(bf16[2,256,768]{2,1,0:T(8,128)(2,1)S(1)} %get-tuple-element.371), channel_id=1, source_target_pairs={{0,8},{4,12},{8,0},{12,4},{16,24},{20,28},{24,16},{28,20},{1,9},{5... | collective-permute-start | bytes 2359304 | tf_op jit(solution)/shard_map/ppermute | solution.py:813
  284.1 18.9 %collective-permute-start.35 = (bf16[1,256,768]{2,1,0:T(8,128)(2,1)S(1)}, bf16[1,256,768]{2,1,0:T(8,128)(2,1)S(1)}, u32[]{:S(2)}, u32[]{:S(2)}) collective-permute-start(bf16[1,256,768]{2,1,0:T(8,128)(2,1)S(1)} %get-tuple-element.389), channel_id=1, source_target_pairs={{0,8},{4,12},{8,0},{12,4},{16,24},{20,28},{24,16},{28,20},{1,9},{5... | collective-permute-start | bytes 1179656 | tf_op jit(solution)/shard_map/ppermute | solution.py:813
  287.7 34.9 %collective-permute-start.40 = (bf16[1,320,768]{2,1,0:T(8,128)(2,1)S(1)}, bf16[1,320,768]{2,1,0:T(8,128)(2,1)S(1)}, u32[]{:S(2)}, u32[]{:S(2)}) collective-permute-start(bf16[1,320,768]{2,1,0:T(8,128)(2,1)S(1)} %get-tuple-element.377), channel_id=1, source_target_pairs={{0,4},{4,0},{8,12},{12,8},{16,20},{20,16},{24,28},{28,24},{1,5},{5... | collective-permute-start | bytes 1474568 | tf_op jit(solution)/shard_map/ppermute | solution.py:813
  303.0 19.4 %collective-permute-start.37 = (bf16[1,128,768]{2,1,0:T(8,128)(2,1)S(1)}, bf16[1,128,768]{2,1,0:T(8,128)(2,1)S(1)}, u32[]{:S(2)}, u32[]{:S(2)}) collective-permute-start(bf16[1,128,768]{2,1,0:T(8,128)(2,1)S(1)} %get-tuple-element.398), channel_id=1, source_target_pairs={{0,16},{4,20},{8,24},{12,28},{16,0},{20,4},{24,8},{28,12},{1,17},{... | collective-permute-start | bytes 589832 | tf_op jit(solution)/shard_map/ppermute | solution.py:813
  305.0 50.9 %collective-permute-start.45 = (bf16[384,768]{1,0:T(8,128)(2,1)S(1)}, bf16[384,768]{1,0:T(8,128)(2,1)S(1)}, u32[]{:S(2)}, u32[]{:S(2)}) collective-permute-start(bf16[384,768]{1,0:T(8,128)(2,1)S(1)} %constant_dynamic-update-slice_fusion.11), channel_id=1, source_target_pairs={{0,4},{4,0},{8,12},{12,8},{16,20},{20,16},{24,28},{28,24},{1,5},{5... | collective-permute-start | bytes 1769480 | tf_op jit(solution)/shard_map/ppermute | solution.py:813
  307.0 28.2 %collective-permute-start.39 = (bf16[1,256,768]{2,1,0:T(8,128)(2,1)S(1)}, bf16[1,256,768]{2,1,0:T(8,128)(2,1)S(1)}, u32[]{:S(2)}, u32[]{:S(2)}) collective-permute-start(bf16[1,256,768]{2,1,0:T(8,128)(2,1)S(1)} %get-tuple-element.386), channel_id=1, source_target_pairs={{0,16},{4,20},{8,24},{12,28},{16,0},{20,4},{24,8},{28,12},{1,17},{... | collective-permute-start | bytes 1179656 | tf_op jit(solution)/shard_map/ppermute | solution.py:813
  322.5 16.8 %collective-permute-start.38 = (bf16[128,768]{1,0:T(8,128)(2,1)S(1)}, bf16[128,768]{1,0:T(8,128)(2,1)S(1)}, u32[]{:S(2)}, u32[]{:S(2)}) collective-permute-start(bf16[128,768]{1,0:T(8,128)(2,1)S(1)} %fusion.21), channel_id=1, source_target_pairs={{0,16},{4,20},{8,24},{12,28},{16,0},{20,4},{24,8},{28,12},{1,17},{... | collective-permute-start | bytes 589832 | tf_op jit(solution)/shard_map/ppermute | solution.py:813
  323.4 20.3 %collective-permute-start.41 = (bf16[1,160,768]{2,1,0:T(8,128)(2,1)}, bf16[1,160,768]{2,1,0:T(8,128)(2,1)}, u32[]{:S(2)}, u32[]{:S(2)}) collective-permute-start(bf16[1,160,768]{2,1,0:T(8,128)(2,1)} %get-tuple-element.395), channel_id=1, source_target_pairs={{0,8},{4,12},{8,0},{12,4},{16,24},{20,28},{24,16},{28,20},{1,9},{5... | collective-permute-start | bytes 737288 | tf_op jit(solution)/shard_map/ppermute | solution.py:813
  355.0 18.8 %collective-permute-start.43 = (bf16[512,768]{1,0:T(8,128)(2,1)S(1)}, bf16[512,768]{1,0:T(8,128)(2,1)S(1)}, u32[]{:S(2)}, u32[]{:S(2)}) collective-permute-start(bf16[512,768]{1,0:T(8,128)(2,1)S(1)} %constant_dynamic-update-slice_fusion.4), channel_id=1, source_target_pairs={{0,4},{4,0},{8,12},{12,8},{16,20},{20,16},{24,28},{28,24},{1,5},{5... | collective-permute-start | bytes 2359304 | tf_op jit(solution)/shard_map/ppermute | solution.py:813
  (43 other events, 524.2 us)
Sparse Core Ops, SparseCore 0:
  10.3 63.1 all-gather.2
